TPU v7x, 32 devices: a whole 2x2x4 slice. The times are simulated.
32 devices in a mesh: dp: 4 (over z), seq: 8 (over y, x, core).
Axes of the slice: x: 2, y: 2, z: 4, core: 2. Of those that a mesh axis runs over, the one named last changes fastest.
Arguments:
- inputs: bfloat16 [2, 4, 512, 2048], P(None, 'dp', 'seq'), may hold values from -6 to 6
- norm_attn: bfloat16 [2048], P(('dp', 'seq')), may hold values from 0.5 to 1.5
- w_query: bfloat16 [2048, 2048], P(('dp', 'seq')), may hold values from -0.125 to 0.125
- w_key: bfloat16 [2048, 2048], P(('dp', 'seq')), may hold values from -0.125 to 0.125
- w_value: bfloat16 [2048, 2048], P(('dp', 'seq')), may hold values from -0.125 to 0.125
- conv_weight: bfloat16 [4, 6144], P(None, ('dp', 'seq')), may hold values from -3 to 3
- w_alpha: bfloat16 [2048, 16], P(('dp', 'seq')), may hold values from -0.125 to 0.125
- w_beta: bfloat16 [2048, 16], P(('dp', 'seq')), may hold values from -0.125 to 0.125
- decay_rate: float32 [16], replicated, may hold values from 0.00048828125 to 0.05
- decay_bias: float32 [16], replicated, may hold values from -3 to 3
- w_outgate: bfloat16 [2048, 2048], P(('dp', 'seq')), may hold values from -0.125 to 0.125
- head_gain: float32 [128], replicated, may hold values from 0.5 to 1.5
- w_output: bfloat16 [2048, 2048], P(('dp', 'seq')), may hold values from -0.25 to 0.25
- norm_mlp: bfloat16 [2048], P(('dp', 'seq')), may hold values from 0.5 to 1.5
- w_gate: bfloat16 [2048, 5632], P(('dp', 'seq')), may hold values from -0.125 to 0.125
- w_up: bfloat16 [2048, 5632], P(('dp', 'seq')), may hold values from -0.125 to 0.125
- w_down: bfloat16 [5632, 2048], P(('dp', 'seq')), may hold values from -0.15625 to 0.15625
- cotangent: bfloat16 [2, 4, 512, 2048], P(None, 'dp', 'seq'), may hold values from -6 to 6
Outputs:
- output: bfloat16 [2, 4, 512, 2048], P(None, 'dp', 'seq')
- input_grad: float32 [2, 4, 512, 2048], P(None, 'dp', 'seq')
- grad_norm_attn: float32 [2048], P(('dp', 'seq'))
- grad_w_query: float32 [2048, 2048], P(('dp', 'seq'))
- grad_w_key: float32 [2048, 2048], P(('dp', 'seq'))
- grad_w_value: float32 [2048, 2048], P(('dp', 'seq'))
- grad_conv_weight: float32 [4, 6144], P(None, ('dp', 'seq'))
- grad_w_alpha: float32 [2048, 16], P(('dp', 'seq'))
- grad_w_beta: float32 [2048, 16], P(('dp', 'seq'))
- grad_decay_rate: float32 [16], replicated
- grad_decay_bias: float32 [16], replicated
- grad_w_outgate: float32 [2048, 2048], P(('dp', 'seq'))
- grad_head_gain: float32 [128], replicated
- grad_w_output: float32 [2048, 2048], P(('dp', 'seq'))
- grad_norm_mlp: float32 [2048], P(('dp', 'seq'))
- grad_w_gate: float32 [2048, 5632], P(('dp', 'seq'))
- grad_w_up: float32 [2048, 5632], P(('dp', 'seq'))
- grad_w_down: float32 [5632, 2048], P(('dp', 'seq'))
All inputs are finite; a program needn't handle non-finite values.
Results may differ from a plain program's by a relative error of at most 0.03.
Values may be sent and summed in bfloat16 or wider, within the bound.
No kernel may reach another device: no remote copies, remote signals or barrier semaphores. Data moves between devices by JAX's collectives and lax.ppermute only.
A program may use at most 368 MiB of HBM per device.

v0:
```python
import jax
import jax.numpy as jnp
from jax import lax
from jax.sharding import PartitionSpec as P

BLOCK = 64
CONV = 4
MB = 2


eps_norm = 1e-06
highest = lax.Precision.HIGHEST


def from_behind(value, axis, steps):
    count = lax.axis_size(axis)
    leading, last = (max(0, -steps), min(count, count - steps))
    return lax.ppermute(value, axis, [(source, source + steps) for source in range(leading, last)])


def rms_scale(values, gain_vec):
    return (
        values * lax.rsqrt(jnp.mean(values * values, axis=-1, keepdims=True) + eps_norm) * gain_vec
    )


def unit_rows(values):
    return values * lax.rsqrt(jnp.sum(values * values, axis=-1, keepdims=True) + eps_norm)


def product(left_side, right_side):
    return jnp.dot(left_side, right_side, preferred_element_type=jnp.float32)


def contract_rows(left_side, right_side):
    return lax.dot_general(
        left_side, right_side, (((0,), (0,)), ((), ())), preferred_element_type=jnp.float32
    )


def times_transposed(left_side, right_side):
    return lax.dot_general(
        left_side, right_side, (((1,), (1,)), ((), ())), preferred_element_type=jnp.float32
    )


def delta_rule(query_in, key_in, value_in, beta_in, decay_in):
    head_count, length, head_width = query_in.shape
    blocks = length // BLOCK
    query_blocks = query_in.reshape(head_count, blocks, BLOCK, head_width)
    key_blocks = key_in.reshape(head_count, blocks, BLOCK, head_width)
    value_blocks = value_in.reshape(head_count, blocks, BLOCK, head_width)
    beta_blocks = beta_in.reshape(head_count, blocks, BLOCK)
    cumulative = jnp.cumsum(decay_in.reshape(head_count, blocks, BLOCK), axis=-1)
    places = jnp.arange(BLOCK)
    strict = places[:, None] > places[None, :]
    within = places[:, None] >= places[None, :]
    spread = cumulative[..., :, None] - cumulative[..., None, :]
    fall_strict = jnp.where(strict, jnp.exp(jnp.where(strict, spread, 0.0)), 0.0)
    fall_within = jnp.where(within, jnp.exp(jnp.where(within, spread, 0.0)), 0.0)
    key_key = jnp.einsum("hnid,hnjd->hnij", key_blocks, key_blocks, precision=highest)
    query_key = jnp.einsum("hnid,hnjd->hnij", query_blocks, key_blocks, precision=highest)
    lower_part = -(beta_blocks[..., :, None] * fall_strict * key_key)
    inverse = jnp.eye(BLOCK, dtype=jnp.float32) + lower_part
    powered = lower_part
    for doubling in range(int(BLOCK).bit_length() - 2):
        powered = jnp.einsum("hnij,hnjk->hnik", powered, powered, precision=highest)
        inverse = inverse + jnp.einsum("hnij,hnjk->hnik", inverse, powered, precision=highest)
    growth = jnp.exp(cumulative)
    fresh_part = jnp.einsum(
        "hnij,hnjd->hnid", inverse, beta_blocks[..., None] * value_blocks, precision=highest
    )
    carried = jnp.einsum(
        "hnij,hnjd->hnid",
        inverse,
        (beta_blocks * growth)[..., None] * key_blocks,
        precision=highest,
    )
    scores = query_key * fall_within
    query_grown = growth[..., None] * query_blocks
    key_fallen = jnp.exp(cumulative[..., -1:] - cumulative)[..., None] * key_blocks
    totals = jnp.exp(cumulative[..., -1])

    def advance(memory, block_data):
        fresh_now, carried_now, scores_now, query_now, key_now, total_now = block_data
        written = fresh_now - jnp.einsum("hid,hde->hie", carried_now, memory, precision=highest)
        results = jnp.einsum("hid,hde->hie", query_now, memory, precision=highest)
        results = results + jnp.einsum("hij,hje->hie", scores_now, written, precision=highest)
        memory = total_now[:, None, None] * memory + jnp.einsum(
            "hid,hie->hde", key_now, written, precision=highest
        )
        return (memory, results)

    by_block = (
        jnp.moveaxis(fresh_part, 1, 0),
        jnp.moveaxis(carried, 1, 0),
        jnp.moveaxis(scores, 1, 0),
        jnp.moveaxis(query_grown, 1, 0),
        jnp.moveaxis(key_fallen, 1, 0),
        jnp.moveaxis(totals, 1, 0),
    )
    initial = jnp.zeros((head_count, head_width, head_width), jnp.float32)
    final_memory, results = lax.scan(jax.checkpoint(advance), initial, by_block)
    return jnp.moveaxis(results, 0, 1).reshape(head_count, length, head_width)


def gated_inputs(padded, conv_full, alpha_pre, beta_pre, decay_rate, decay_bias):
    rows_out = padded.shape[0] - CONV + 1
    convolved = conv_full[0] * padded[0:rows_out]
    for conv_tap in range(1, CONV):
        convolved = convolved + conv_full[conv_tap] * padded[conv_tap : conv_tap + rows_out]
    active = jax.nn.silu(convolved)
    head_count = decay_rate.shape[0]
    model_width = active.shape[1] // 3
    head_width = model_width // head_count
    pieces = active.reshape(rows_out, 3, head_count, head_width)
    query_out = unit_rows(pieces[:, 0]) * head_width ** (-0.5)
    key_out = unit_rows(pieces[:, 1])
    value_out = pieces[:, 2]
    beta_out = jax.nn.sigmoid(beta_pre)
    decay_out = -decay_rate * jax.nn.softplus(alpha_pre + decay_bias)
    return (
        query_out.reshape(rows_out, model_width),
        key_out.reshape(rows_out, model_width),
        value_out.reshape(rows_out, model_width),
        beta_out,
        decay_out,
    )


def head_rule(query_in, key_in, value_in, beta_in, decay_in):
    length, model_width = query_in.shape
    head_count = beta_in.shape[1]
    head_width = model_width // head_count
    query_heads = jnp.transpose(query_in.reshape(length, head_count, head_width), (1, 0, 2))
    key_heads = jnp.transpose(key_in.reshape(length, head_count, head_width), (1, 0, 2))
    value_heads = jnp.transpose(value_in.reshape(length, head_count, head_width), (1, 0, 2))
    outcome = delta_rule(query_heads, key_heads, value_heads, beta_in.T, decay_in.T)
    return jnp.transpose(outcome, (1, 0, 2)).reshape(length, model_width)


def gated_output(core_in, out_gate, head_gain):
    rows_out, model_width = core_in.shape
    head_width = head_gain.shape[0]
    pieces = core_in.reshape(rows_out, model_width // head_width, head_width)
    normed = (
        pieces * lax.rsqrt(jnp.mean(pieces * pieces, axis=-1, keepdims=True) + eps_norm) * head_gain
    )
    return normed.reshape(rows_out, model_width) * jax.nn.silu(out_gate)


def on_device(
    inputs,
    norm_attn,
    w_query,
    w_key,
    w_value,
    conv_weight,
    w_alpha,
    w_beta,
    decay_rate,
    decay_bias,
    w_outgate,
    head_gain,
    w_output,
    norm_mlp,
    w_gate,
    w_up,
    w_down,
    cotangent,
):
    f32 = jnp.float32
    bf16 = jnp.bfloat16
    model_width = w_query.shape[1]
    rim_rows = CONV - 1
    gain_attn_total = jnp.zeros((norm_attn.shape[0] * lax.axis_size(("dp", "seq")),), f32)
    gain_mlp_total = jnp.zeros((norm_mlp.shape[0] * lax.axis_size(("dp", "seq")),), f32)
    conv_total = jnp.zeros(
        (conv_weight.shape[0], conv_weight.shape[1] * lax.axis_size(("dp", "seq"))), f32
    )
    rate_total = jnp.zeros(decay_rate.shape, f32)
    bias_total = jnp.zeros(decay_bias.shape, f32)
    gain_total = jnp.zeros(head_gain.shape, f32)
    kept_hidden_in = []
    kept_hidden_mid = []
    kept_activ = []
    kept_seed = []
    kept_grad_gate = []
    kept_grad_up = []
    kept_mixed = []
    kept_grad_mixer = []
    kept_grad_proj = []
    kept_alpha = []
    kept_beta = []
    kept_outgate = []
    outputs = []
    input_grads = []
    for micro_batch in range(MB):
        mixer = (
            lax.all_gather(norm_attn, ("dp", "seq"), axis=0, tiled=True),
            lax.all_gather(w_query, ("dp", "seq"), axis=0, tiled=True),
            lax.all_gather(w_key, ("dp", "seq"), axis=0, tiled=True),
            lax.all_gather(w_value, ("dp", "seq"), axis=0, tiled=True),
            lax.all_gather(conv_weight, ("dp", "seq"), axis=1, tiled=True),
            lax.all_gather(w_alpha, ("dp", "seq"), axis=0, tiled=True),
            lax.all_gather(w_beta, ("dp", "seq"), axis=0, tiled=True),
            lax.all_gather(w_outgate, ("dp", "seq"), axis=0, tiled=True),
            lax.all_gather(w_output, ("dp", "seq"), axis=0, tiled=True),
        )
        (
            gain_attn,
            query_full,
            key_full,
            value_full,
            conv_full,
            alpha_full,
            beta_full,
            outgate_full,
            output_full,
        ) = mixer
        tokens = inputs[micro_batch, 0].astype(f32)
        normed_in, pull_in = jax.vjp(rms_scale, tokens, gain_attn.astype(f32))
        hidden_in = normed_in.astype(bf16)
        projected = jnp.concatenate(
            [
                product(hidden_in, query_full),
                product(hidden_in, key_full),
                product(hidden_in, value_full),
            ],
            axis=1,
        ).astype(bf16)
        before = from_behind(projected[-rim_rows:], "seq", 1)
        padded = jnp.concatenate([before, projected], axis=0).astype(f32)
        alpha_pre = product(hidden_in, alpha_full)
        beta_pre = product(hidden_in, beta_full)
        gated, pull_gated = jax.vjp(
            gated_inputs, padded, conv_full.astype(f32), alpha_pre, beta_pre, decay_rate, decay_bias
        )
        query_low = gated[0].astype(bf16)
        key_low = gated[1].astype(bf16)
        value_low = gated[2].astype(bf16)
        beta_low = gated[3].astype(bf16)
        decay_low = gated[4].astype(bf16)
        arrived = (
            lax.all_to_all(query_low, "seq", split_axis=1, concat_axis=0, tiled=True),
            lax.all_to_all(key_low, "seq", split_axis=1, concat_axis=0, tiled=True),
            lax.all_to_all(value_low, "seq", split_axis=1, concat_axis=0, tiled=True),
            lax.all_to_all(beta_low, "seq", split_axis=1, concat_axis=0, tiled=True),
            lax.all_to_all(decay_low, "seq", split_axis=1, concat_axis=0, tiled=True),
        )
        core_heads, pull_core = jax.vjp(
            head_rule,
            arrived[0].astype(f32),
            arrived[1].astype(f32),
            arrived[2].astype(f32),
            arrived[3].astype(f32),
            arrived[4].astype(f32),
        )
        core_seq = lax.all_to_all(
            core_heads.astype(bf16), "seq", split_axis=0, concat_axis=1, tiled=True
        )
        out_gate = product(hidden_in, outgate_full)
        mixed_out, pull_out = jax.vjp(gated_output, core_seq.astype(f32), out_gate, head_gain)
        mixed_low = mixed_out.astype(bf16)
        residual = tokens + product(mixed_low, output_full)
        feed = (
            lax.all_gather(norm_mlp, ("dp", "seq"), axis=0, tiled=True),
            lax.all_gather(w_gate, ("dp", "seq"), axis=0, tiled=True),
            lax.all_gather(w_up, ("dp", "seq"), axis=0, tiled=True),
            lax.all_gather(w_down, ("dp", "seq"), axis=0, tiled=True),
        )
        gain_mlp, gate_full, up_full, down_full = feed
        normed_mid, pull_mid = jax.vjp(rms_scale, residual, gain_mlp.astype(f32))
        hidden_mid = normed_mid.astype(bf16)
        gate_pre = product(hidden_mid, gate_full)
        up_proj = product(hidden_mid, up_full)
        activ = (jax.nn.silu(gate_pre) * up_proj).astype(bf16)
        outputs.append((residual + product(activ, down_full)).astype(bf16))
        seed_grad = cotangent[micro_batch, 0]
        from_down = times_transposed(seed_grad, down_full)
        sigmoid_gate = jax.nn.sigmoid(gate_pre)
        grad_gate = (
            from_down * up_proj * sigmoid_gate * (1.0 + gate_pre * (1.0 - sigmoid_gate))
        ).astype(bf16)
        grad_up = (from_down * jax.nn.silu(gate_pre)).astype(bf16)
        back_mid = times_transposed(grad_gate, gate_full) + times_transposed(grad_up, up_full)
        grad_res_norm, grad_gain_mlp = pull_mid(back_mid)
        grad_res = seed_grad.astype(f32) + grad_res_norm
        gain_mlp_total = gain_mlp_total + grad_gain_mlp
        grad_mixer_out = grad_res.astype(bf16)
        grad_mixed = times_transposed(grad_mixer_out, output_full)
        grad_core_seq, grad_out_gate, grad_head_gain = pull_out(grad_mixed)
        gate_out_low = grad_out_gate.astype(bf16)
        core_back = lax.all_to_all(
            grad_core_seq.astype(bf16), "seq", split_axis=1, concat_axis=0, tiled=True
        )
        head_grads = pull_core(core_back.astype(f32))
        returned = (
            lax.all_to_all(
                head_grads[0].astype(bf16), "seq", split_axis=0, concat_axis=1, tiled=True
            ),
            lax.all_to_all(
                head_grads[1].astype(bf16), "seq", split_axis=0, concat_axis=1, tiled=True
            ),
            lax.all_to_all(
                head_grads[2].astype(bf16), "seq", split_axis=0, concat_axis=1, tiled=True
            ),
            lax.all_to_all(
                head_grads[3].astype(bf16), "seq", split_axis=0, concat_axis=1, tiled=True
            ),
            lax.all_to_all(
                head_grads[4].astype(bf16), "seq", split_axis=0, concat_axis=1, tiled=True
            ),
        )
        grad_padded, grad_conv, grad_alpha, grad_beta, grad_rate, grad_bias = pull_gated(
            (
                returned[0].astype(f32),
                returned[1].astype(f32),
                returned[2].astype(f32),
                returned[3].astype(f32),
                returned[4].astype(f32),
            )
        )
        spill = from_behind(grad_padded[:rim_rows].astype(jnp.bfloat16), "seq", -1).astype(
            jnp.float32
        )
        grad_proj = grad_padded[rim_rows:].at[-rim_rows:].add(spill).astype(bf16)
        alpha_low = grad_alpha.astype(bf16)
        beta_grad_low = grad_beta.astype(bf16)
        back_in = (
            times_transposed(grad_proj[:, :model_width], query_full)
            + times_transposed(grad_proj[:, model_width : 2 * model_width], key_full)
            + times_transposed(grad_proj[:, 2 * model_width :], value_full)
            + times_transposed(alpha_low, alpha_full)
            + times_transposed(beta_grad_low, beta_full)
            + times_transposed(gate_out_low, outgate_full)
        )
        grad_tok_norm, grad_gain_attn = pull_in(back_in)
        input_grads.append(grad_res + grad_tok_norm)
        gain_attn_total = gain_attn_total + grad_gain_attn
        conv_total = conv_total + grad_conv
        rate_total = rate_total + grad_rate
        bias_total = bias_total + grad_bias
        gain_total = gain_total + grad_head_gain
        kept_hidden_in.append(hidden_in)
        kept_hidden_mid.append(hidden_mid)
        kept_activ.append(activ)
        kept_seed.append(seed_grad)
        kept_grad_gate.append(grad_gate)
        kept_grad_up.append(grad_up)
        kept_mixed.append(mixed_low)
        kept_grad_mixer.append(grad_mixer_out)
        kept_grad_proj.append(grad_proj)
        kept_alpha.append(alpha_low)
        kept_beta.append(beta_grad_low)
        kept_outgate.append(gate_out_low)
    all_hidden_mid = jnp.concatenate(kept_hidden_mid, axis=0)
    mlp_sums = (
        lax.psum_scatter(gain_mlp_total, ("dp", "seq"), scatter_dimension=0, tiled=True),
        lax.psum_scatter(
            contract_rows(all_hidden_mid, jnp.concatenate(kept_grad_gate, axis=0)),
            ("dp", "seq"),
            scatter_dimension=0,
            tiled=True,
        ),
        lax.psum_scatter(
            contract_rows(all_hidden_mid, jnp.concatenate(kept_grad_up, axis=0)),
            ("dp", "seq"),
            scatter_dimension=0,
            tiled=True,
        ),
        lax.psum_scatter(
            contract_rows(jnp.concatenate(kept_activ, axis=0), jnp.concatenate(kept_seed, axis=0)),
            ("dp", "seq"),
            scatter_dimension=0,
            tiled=True,
        ),
    )
    all_hidden_in = jnp.concatenate(kept_hidden_in, axis=0)
    all_grad_proj = jnp.concatenate(kept_grad_proj, axis=0)
    mixer_sums = (
        lax.psum_scatter(gain_attn_total, ("dp", "seq"), scatter_dimension=0, tiled=True),
        lax.psum_scatter(
            contract_rows(all_hidden_in, all_grad_proj[:, :model_width]),
            ("dp", "seq"),
            scatter_dimension=0,
            tiled=True,
        ),
        lax.psum_scatter(
            contract_rows(all_hidden_in, all_grad_proj[:, model_width : 2 * model_width]),
            ("dp", "seq"),
            scatter_dimension=0,
            tiled=True,
        ),
        lax.psum_scatter(
            contract_rows(all_hidden_in, all_grad_proj[:, 2 * model_width :]),
            ("dp", "seq"),
            scatter_dimension=0,
            tiled=True,
        ),
        lax.psum_scatter(conv_total, ("dp", "seq"), scatter_dimension=1, tiled=True),
        lax.psum_scatter(
            contract_rows(all_hidden_in, jnp.concatenate(kept_alpha, axis=0)),
            ("dp", "seq"),
            scatter_dimension=0,
            tiled=True,
        ),
        lax.psum_scatter(
            contract_rows(all_hidden_in, jnp.concatenate(kept_beta, axis=0)),
            ("dp", "seq"),
            scatter_dimension=0,
            tiled=True,
        ),
        lax.psum_scatter(
            contract_rows(all_hidden_in, jnp.concatenate(kept_outgate, axis=0)),
            ("dp", "seq"),
            scatter_dimension=0,
            tiled=True,
        ),
        lax.psum_scatter(
            contract_rows(
                jnp.concatenate(kept_mixed, axis=0), jnp.concatenate(kept_grad_mixer, axis=0)
            ),
            ("dp", "seq"),
            scatter_dimension=0,
            tiled=True,
        ),
    )
    small_sums = lax.psum((rate_total, bias_total, gain_total), ("dp", "seq"))
    output_all = jnp.stack(outputs, axis=0)[:, None]
    input_grad_all = jnp.stack(input_grads, axis=0)[:, None]
    return (
        output_all,
        input_grad_all,
        mixer_sums[0],
        mixer_sums[1],
        mixer_sums[2],
        mixer_sums[3],
        mixer_sums[4],
        mixer_sums[5],
        mixer_sums[6],
        small_sums[0],
        small_sums[1],
        mixer_sums[7],
        small_sums[2],
        mixer_sums[8],
        mlp_sums[0],
        mlp_sums[1],
        mlp_sums[2],
        mlp_sums[3],
    )


def solution(mesh):
    in_specs = (
        P(None, "dp", "seq", None),
        P(("dp", "seq")),
        P(("dp", "seq"), None),
        P(("dp", "seq"), None),
        P(("dp", "seq"), None),
        P(None, ("dp", "seq")),
        P(("dp", "seq"), None),
        P(("dp", "seq"), None),
        P(),
        P(),
        P(("dp", "seq"), None),
        P(),
        P(("dp", "seq"), None),
        P(("dp", "seq")),
        P(("dp", "seq"), None),
        P(("dp", "seq"), None),
        P(("dp", "seq"), None),
        P(None, "dp", "seq", None),
    )
    out_specs = (
        P(None, "dp", "seq", None),
        P(None, "dp", "seq", None),
        P(("dp", "seq")),
        P(("dp", "seq"), None),
        P(("dp", "seq"), None),
        P(("dp", "seq"), None),
        P(None, ("dp", "seq")),
        P(("dp", "seq"), None),
        P(("dp", "seq"), None),
        P(),
        P(),
        P(("dp", "seq"), None),
        P(),
        P(("dp", "seq"), None),
        P(("dp", "seq")),
        P(("dp", "seq"), None),
        P(("dp", "seq"), None),
        P(("dp", "seq"), None),
    )
    return jax.shard_map(
        on_device, mesh=mesh, in_specs=in_specs, out_specs=out_specs, check_vma=False
    )
```

profile of v0, /device:TPU:0, one launch (start us, length us, event | category | flops | bytes accessed | tf_op | source)
XLA Modules:
  0.0 4024.7 jit_solution(4301263699450317740)
XLA Ops:
  12.5 42.6 %all-reduce.31 = (bf16[2048]{0:T(1024)(128)(2,1)S(1)}, bf16[2048]{0:T(1024)(128)(2,1)S(1)}) all-reduce(bf16[2048]{0:T(1024)(128)(2,1)S(1)} %dynamic-update-slice.6, bf16[2048]{0:T(1024)(128)(2,1)S(1)} %dynamic-update-slice.7), channel_id=1, replica_groups=mesh['dp'=4,'seq'=8] {'dp','seq'}, use_global_device_ids=true, to_apply=%add.26 | all-reduce | flops 4096 | bytes 16384
  55.1 41.8 %all-gather = bf16[32,64,16]{1,2,0:T(8,128)(2,1)S(1)} all-gather(bf16[1,64,16]{1,2,0:T(8,128)(2,1)S(1)} %bitcast.1130), channel_id=1, replica_groups=mesh['dp'=4,'seq'=8] {'dp','seq'}, dimensions={0}, use_global_device_ids=true | all-gather | bytes 67584 | tf_op jit(solution)/shard_map/all_gather | solution.py:205
  103.8 39.0 all-gather.2
  145.2 37.5 all-gather.1
  219.9 31.1 all-gather.12.cloned.1.call-done
  272.8 57.0 %all-gather.18.cloned.1.call-done = bf16[2048,2048]{1,0:T(8,128)(2,1)} async-done(((bf16[64,2048]{1,0:T(8,128)(2,1)}), bf16[2048,2048]{1,0:T(8,128)(2,1)}) %all-gather.18.cloned.1.call-update) | async-done | bytes 8388624 | tf_op jit(solution)/shard_map/all_gather | solution.py:207
  437.7 51.9 %while.86 = (s32[]{:T(128)}, f32[2,128,128]{2,1,0:T(8,128)S(1)}, bf16[8,2,64,128]{3,2,0,1:T(8,128)(2,1)}, f32[8,2,128,128]{3,2,1,0:T(8,128)}, f32[8,2]{1,0:T(8,1...) while((s32[]{:T(128)}, f32[2,128,128]{2,1,0:T(8,128)S(1)}, ...), condition=%wide.region_5.7_spmd.clone, body=%wide.region_4.6_spmd.clone.sunk | while | flops 88309760 | bytes 1510065 | solution.py:103
  516.6 47.1 %while.87 = (s32[]{:T(128)}, f32[2,128,128]{2,1,0:T(8,128)S(1)}, bf16[8,2,64,128]{3,2,0,1:T(8,128)(2,1)S(1)}, f32[8,2,128,128]{3,2,1,0:T(8,128)}, f32[8,2]{1,0:T...) while((s32[]{:T(128)}, f32[2,128,128]{2,1,0:T(8,128)S(1)}, ...), condition=%wide.region_13.15_spmd.clone, body=%wide.region_12.14_spmd.clone.sunk | while | flops 88309760 | bytes 1510065 | solution.py:103
  613.2 92.7 %all-gather.24.cloned.1.call-done = bf16[2048,5632]{1,0:T(8,128)(2,1)} async-done(((bf16[64,5632]{1,0:T(8,128)(2,1)}), bf16[2048,5632]{1,0:T(8,128)(2,1)}) %all-gather.24.cloned.1.call-update) | async-done | bytes 23068688 | tf_op jit(solution)/shard_map/all_gather | solution.py:269
  734.9 116.7 %all-gather.26.cloned.1.call-done = bf16[5632,2048]{1,0:T(8,128)(2,1)} async-done(((bf16[176,2048]{1,0:T(8,128)(2,1)}), bf16[5632,2048]{1,0:T(8,128)(2,1)}) %all-gather.26.cloned.1.call-update) | async-done | bytes 23068688 | tf_op jit(solution)/shard_map/all_gather | solution.py:270
  966.5 80.6 %while.89 = (s32[]{:T(128)}, f32[2,128,128]{2,1,0:T(8,128)S(1)}, f32[8,2,64,128]{3,2,1,0:T(8,128)}, f32[8,2,64,128]{3,2,1,0:T(8,128)}, f32[8,2,64,64]{2,3,0,1:T(...) while((s32[]{:T(128)}, f32[2,128,128]{2,1,0:T(8,128)S(1)}, ...), condition=%wide.region_37.39_spmd.clone, body=%wide.region_35.38_spmd.clone.sunk | while | flops 201588736 | bytes 4227371 | solution.py:103
  1075.4 80.7 %while.88 = (s32[]{:T(128)}, f32[2,128,128]{2,1,0:T(8,128)S(1)}, f32[8,2,64,128]{3,2,1,0:T(8,128)}, f32[8,2,64,128]{3,2,1,0:T(8,128)}, f32[8,2,64,64]{2,3,0,1:T(...) while((s32[]{:T(128)}, f32[2,128,128]{2,1,0:T(8,128)S(1)}, ...), condition=%wide.region_20.22_spmd.clone, body=%wide.region_18.21_spmd.clone.sunk | while | flops 201588736 | bytes 4227371 | solution.py:103
  1378.2 18.0 fusion.74
  1416.5 19.2 fusion.82
  1465.7 34.2 reduce-scatter.38.cloned.1.call-done
  1543.0 38.0 all-reduce.30
  1604.6 182.9 %reduce-scatter.24.cloned.1.call-done = f32[64,2048]{1,0:T(8,128)} async-done(((f32[2048,2048]{1,0:T(8,128)}), f32[64,2048]{1,0:T(8,128)}) %reduce-scatter.24.cloned.1.call-update) | async-done | bytes 524304 | tf_op jit(solution)/shard_map/reduce_scatter | solution.py:414
  1787.5 187.4 %reduce-scatter.26.cloned.1.call-done = f32[64,2048]{1,0:T(8,128)} async-done(((f32[2048,2048]{1,0:T(8,128)}), f32[64,2048]{1,0:T(8,128)}) %reduce-scatter.26.cloned.1.call-update) | async-done | bytes 524304 | tf_op jit(solution)/shard_map/reduce_scatter | solution.py:420
  1974.9 187.3 %reduce-scatter.18.cloned.1.call-done = f32[64,2048]{1,0:T(8,128)} async-done(((f32[2048,2048]{1,0:T(8,128)}), f32[64,2048]{1,0:T(8,128)}) %reduce-scatter.18.cloned.1.call-update) | async-done | bytes 524304 | tf_op jit(solution)/shard_map/reduce_scatter | solution.py:383
  2162.3 187.3 %reduce-scatter.20.cloned.1.call-done = f32[64,2048]{1,0:T(8,128)} async-done(((f32[2048,2048]{1,0:T(8,128)}), f32[64,2048]{1,0:T(8,128)}) %reduce-scatter.20.cloned.1.call-update) | async-done | bytes 524304 | tf_op jit(solution)/shard_map/reduce_scatter | solution.py:389
  2349.6 187.2 %reduce-scatter.22.cloned.1.call-done = f32[64,2048]{1,0:T(8,128)} async-done(((f32[2048,2048]{1,0:T(8,128)}), f32[64,2048]{1,0:T(8,128)}) %reduce-scatter.22.cloned.1.call-update) | async-done | bytes 524304 | tf_op jit(solution)/shard_map/reduce_scatter | solution.py:395
  2536.8 489.4 %reduce-scatter.28.cloned.1.call-done = f32[64,5632]{1,0:T(8,128)} async-done(((f32[2048,5632]{1,0:T(8,128)}), f32[64,5632]{1,0:T(8,128)}) %reduce-scatter.28.cloned.1.call-update) | async-done | bytes 1441808 | tf_op jit(solution)/shard_map/reduce_scatter | solution.py:360
  3026.2 495.8 %reduce-scatter.30.cloned.1.call-done = f32[64,5632]{1,0:T(8,128)} async-done(((f32[2048,5632]{1,0:T(8,128)}), f32[64,5632]{1,0:T(8,128)}) %reduce-scatter.30.cloned.1.call-update) | async-done | bytes 1441808 | tf_op jit(solution)/shard_map/reduce_scatter | solution.py:366
  3522.0 496.0 %reduce-scatter.32.cloned.1.call-done = f32[176,2048]{1,0:T(8,128)} async-done(((f32[5632,2048]{1,0:T(8,128)}), f32[176,2048]{1,0:T(8,128)}) %reduce-scatter.32.cloned.1.call-update) | async-done | bytes 1441808 | tf_op jit(solution)/shard_map/reduce_scatter | solution.py:372
  (1550 shorter events, 1022.3 us)
Async XLA Ops:
  7.2 202.6 %all-gather.16.cloned.1.call-start = ((), (), s32[]{:S(2)}) async-start(), calls=%async_computation.37 | async-start | bytes 8650752 | tf_op jit(solution)/shard_map/all_gather | solution.py:203
  8.0 206.9 %all-gather.14.cloned.1.call-start = ((), (), s32[]{:S(2)}) async-start(), calls=%async_computation.36 | async-start | bytes 8650752 | tf_op jit(solution)/shard_map/all_gather | solution.py:202
  8.7 242.2 %all-gather.12.cloned.1.call-start = ((), (), s32[]{:S(2)}) async-start(), calls=%async_computation.35 | async-start | bytes 8650752 | tf_op jit(solution)/shard_map/all_gather | solution.py:201
  9.5 320.3 %all-gather.18.cloned.1.call-start = ((), (), s32[]{:S(2)}) async-start(), calls=%async_computation.38 | async-start | bytes 8650752 | tf_op jit(solution)/shard_map/all_gather | solution.py:207
  10.0 582.9 %all-gather.20.cloned.1.call-start = ((), (), s32[]{:S(2)}) async-start(), calls=%async_computation.39 | async-start | bytes 8650752 | tf_op jit(solution)/shard_map/all_gather | solution.py:208
  10.6 591.6 %all-gather.22.cloned.1.call-start = ((), (), s32[]{:S(2)}) async-start(), calls=%async_computation.40 | async-start | bytes 23789568 | tf_op jit(solution)/shard_map/all_gather | solution.py:268
  11.2 694.7 %all-gather.24.cloned.1.call-start = ((), (), s32[]{:S(2)}) async-start(), calls=%async_computation.41 | async-start | bytes 23789568 | tf_op jit(solution)/shard_map/all_gather | solution.py:269
  99.5 86.0 %all-to-all-start = ((bf16[64,8,2]{0,2,1:T(2,128)(2,1)}), bf16[64,8,2]{0,2,1:T(2,128)(2,1)S(1)}, u32[]{:S(2)}, u32[]{:S(2)}) async-start(bf16[64,8,2]{0,2,1:T(2,128)(2,1)} %bitcast.3), calls=%async_computation | async-start | bytes 8192 | tf_op jit(solution)/shard_map/all_to_all | solution.py:249
  102.9 748.7 %all-gather.26.cloned.1.call-start = ((), (), s32[]{:S(2)}) async-start(), calls=%async_computation.42 | async-start | bytes 23789568 | tf_op jit(solution)/shard_map/all_gather | solution.py:270
  256.6 78.1 %collective-permute-start = (bf16[3,6144]{1,0:T(4,128)(2,1)}, bf16[3,6144]{1,0:T(4,128)(2,1)}, u32[]{:S(2)}, u32[]{:S(2)}) collective-permute-start(bf16[3,6144]{1,0:T(4,128)(2,1)} %pad_maximum_fusion.8), channel_id=1, source_target_pairs={{0,1},{1,2},{2,3},{3,4},{4,5},{5,6},{6,7},{8,9},{9,10},{10,11},{11... | collective-permute-start | bytes 110600 | tf_op jit(solution)/shard_map/ppermute | solution.py:18
  269.7 66.1 %collective-permute-start.1 = (bf16[3,6144]{1,0:T(4,128)(2,1)}, bf16[3,6144]{1,0:T(4,128)(2,1)}, u32[]{:S(2)}, u32[]{:S(2)}) collective-permute-start(bf16[3,6144]{1,0:T(4,128)(2,1)} %pad_maximum_fusion.6), channel_id=1, source_target_pairs={{0,1},{1,2},{2,3},{3,4},{4,5},{5,6},{6,7},{8,9},{9,10},{10,11},{11... | collective-permute-start | bytes 110600 | tf_op jit(solution)/shard_map/ppermute | solution.py:18
  492.7 72.1 %all-to-all-start.5 = ((bf16[8,64,256]{2,1,0:T(8,128)(2,1)}), bf16[8,64,256]{2,1,0:T(8,128)(2,1)S(1)}, u32[]{:S(2)}, u32[]{:S(2)}) async-start(bf16[8,64,256]{2,1,0:T(8,128)(2,1)} %convert_element_type.588), calls=%async_computation.5 | async-start | bytes 524288 | tf_op jit(solution)/shard_map/all_to_all | solution.py:259
  958.6 112.0 %all-to-all-start.12 = ((bf16[64,8,256]{2,0,1:T(8,128)(2,1)}), bf16[64,8,256]{2,0,1:T(8,128)(2,1)}, u32[]{:S(2)}, u32[]{:S(2)}) async-start(bf16[64,8,256]{2,0,1:T(8,128)(2,1)} %bitcast.841), calls=%async_computation.12 | async-start | bytes 524288 | tf_op jit(solution)/shard_map/all_to_all | solution.py:294
  1228.1 236.2 %reduce-scatter.36.cloned.1.call-start = ((), (), s32[]{:S(2)}) async-start(), calls=%async_computation.52 | async-start | bytes 1081344
  1243.9 255.9 %reduce-scatter.38.cloned.1.call-start = ((), (), s32[]{:S(2)}) async-start(), calls=%async_computation.53 | async-start | bytes 1081344
  1299.1 304.0 %reduce-scatter.34.cloned.1.call-start = ((), (), s32[]{:S(2)}) async-start(), calls=%async_computation.51 | async-start | bytes 3244032
  1320.8 466.8 %reduce-scatter.24.cloned.1.call-start = ((), (), s32[]{:S(2)}) async-start(), calls=%async_computation.46 | async-start | bytes 17301504 | tf_op jit(solution)/shard_map/reduce_scatter | solution.py:414
  1330.0 644.9 %reduce-scatter.26.cloned.1.call-start = ((), (), s32[]{:S(2)}) async-start(), calls=%async_computation.47 | async-start | bytes 17301504 | tf_op jit(solution)/shard_map/reduce_scatter | solution.py:420
  1339.4 822.9 %reduce-scatter.18.cloned.1.call-start = ((), (), s32[]{:S(2)}) async-start(), calls=%async_computation.43 | async-start | bytes 17301504 | tf_op jit(solution)/shard_map/reduce_scatter | solution.py:383
  1360.2 989.4 %reduce-scatter.20.cloned.1.call-start = ((), (), s32[]{:S(2)}) async-start(), calls=%async_computation.44 | async-start | bytes 17301504 | tf_op jit(solution)/shard_map/reduce_scatter | solution.py:389
  1368.5 1168.3 %reduce-scatter.22.cloned.1.call-start = ((), (), s32[]{:S(2)}) async-start(), calls=%async_computation.45 | async-start | bytes 17301504 | tf_op jit(solution)/shard_map/reduce_scatter | solution.py:395
  1376.8 1649.5 %reduce-scatter.28.cloned.1.call-start = ((), (), s32[]{:S(2)}) async-start(), calls=%async_computation.48 | async-start | bytes 47579136 | tf_op jit(solution)/shard_map/reduce_scatter | solution.py:360
  1396.2 2125.7 %reduce-scatter.30.cloned.1.call-start = ((), (), s32[]{:S(2)}) async-start(), calls=%async_computation.49 | async-start | bytes 47579136 | tf_op jit(solution)/shard_map/reduce_scatter | solution.py:366
  1415.5 2602.5 %reduce-scatter.32.cloned.1.call-start = ((), (), s32[]{:S(2)}) async-start(), calls=%async_computation.50 | async-start | bytes 47579136 | tf_op jit(solution)/shard_map/reduce_scatter | solution.py:372
  (326 other events, 7415.8 us)
Sparse Core Ops, SparseCore 0:
  10.9 81.6 all-gather.15
  95.5 76.3 all-gather.13
  174.8 76.1 all-gather.11
  253.7 76.0 all-gather.17
  332.5 75.9 all-gather.19
  411.2 148.9 all-gather.21
  563.0 142.8 all-gather.23
  708.7 142.7 all-gather.25
  1231.7 134.7 reduce-scatter.35
  1368.7 131.1 reduce-scatter.37
  1505.3 97.7 reduce-scatter.33
  1605.8 181.7 reduce-scatter.23
  1790.4 184.4 reduce-scatter.25
  1977.6 184.5 reduce-scatter.17
  2165.0 184.5 reduce-scatter.19
  2352.3 184.4 reduce-scatter.21
  2539.5 486.6 reduce-scatter.27
  3028.9 493.0 reduce-scatter.29
  3524.9 493.0 reduce-scatter.31
where the time goes:
time: 4050 us; the launch traced here: 4020 us
  waiting for transfers between devices  2830 us (70%)
  matrix products  582 us (14%)
  local copies, waits for them, and re-layouts  211 us (5%)
  blocking collectives  199 us (5%)
  starting transfers between devices  112 us (3%)
  other arithmetic  64.1 us (2%)
    reduce_scatter x2, waiting for transfers between devices, on_device(): lax.psum_scatter(contract_rows(all_hidden_mid, jnp.concatenate(kept_grad_...  985 us
    reduce_scatter x1, waiting for transfers between devices, on_device(): lax.psum_scatter(contract_rows(jnp.concatenate(kept_activ, axis=0), jnp.c...  496 us
    reduce_scatter x1, waiting for transfers between devices, on_device(): lax.psum_scatter(contract_rows(jnp.concatenate(kept_mixed, axis=0), jnp.c...  187 us
    reduce_scatter x1, waiting for transfers between devices, on_device(): lax.psum_scatter(contract_rows(all_hidden_in, all_grad_proj[:, :model_wid...  187 us
    reduce_scatter x1, waiting for transfers between devices, on_device(): lax.psum_scatter(contract_rows(all_hidden_in, all_grad_proj[:, model_widt...  187 us
    reduce_scatter x1, waiting for transfers between devices, on_device(): lax.psum_scatter(contract_rows(all_hidden_in, all_grad_proj[:, 2 * model_...  187 us
    reduce_scatter x1, waiting for transfers between devices, on_device(): lax.psum_scatter(contract_rows(all_hidden_in, jnp.concatenate(kept_outgat...  183 us
    dot_general x20, matrix products, times_transposed(): lax.dot_general(left_side, right_side, (((1,), (1,)), ((), ())), preferre...  135 us
  transfers between devices with their start and end apart: 47, of which 30 were waited for; matrix products, arithmetic and copies ran while one was open for 15% of the time, Pallas kernels for 0%

commit v1 on v0

v1 whole, which is shorter than its diff:
```python
import functools

import jax
import jax.numpy as jnp
from jax import lax
from jax.experimental import pallas as pl
from jax.experimental.pallas import tpu as pltpu
from jax.sharding import PartitionSpec as P

BLOCK = 64
CONV = 4
MB = 2


eps_norm = 1e-06
highest = lax.Precision.HIGHEST


def rms_scale(values, gain_vec):
    return (
        values * lax.rsqrt(jnp.mean(values * values, axis=-1, keepdims=True) + eps_norm) * gain_vec
    )


def product(left_side, right_side):
    return jnp.dot(left_side, right_side, preferred_element_type=jnp.float32)


def contract_rows(left_side, right_side):
    return lax.dot_general(
        left_side, right_side, (((0,), (0,)), ((), ())), preferred_element_type=jnp.float32
    )


def times_transposed(left_side, right_side):
    return lax.dot_general(
        left_side, right_side, (((1,), (1,)), ((), ())), preferred_element_type=jnp.float32
    )


ALL = ("dp", "seq")


def swap(value, bit):
    count = lax.axis_size("seq")
    return lax.ppermute(value, "seq", [(place, place ^ bit) for place in range(count)])


def seq_offsets():
    count = lax.axis_size("seq")
    half = count // 2
    return [2 * place for place in range(half)] + [2 * place + 1 for place in range(half)]


def gather_seq(value):
    count = lax.axis_size("seq")
    held = {0: value}
    if count == 8:
        half = value.shape[0] // 2
        held[2] = swap(value, 2)
        held[4] = swap(value, 4)
        held[6] = jnp.concatenate(
            [swap(held[2][:half], 4), swap(held[4][half:], 2)], axis=0
        )
    else:
        bit = 2
        while bit < count:
            for offset in list(held):
                held[offset | bit] = swap(held[offset], bit)
            bit *= 2
    for offset in list(held):
        held[offset | 1] = swap(held[offset], 1)
    return jnp.stack([held[offset] for offset in seq_offsets()], axis=0)


def add_low(left_side, right_side):
    return (left_side.astype(jnp.float32) + right_side.astype(jnp.float32)).astype(jnp.bfloat16)


def scatter_seq(parts):
    f32 = jnp.float32
    count = lax.axis_size("seq")
    half = count // 2
    own = add_low(parts[:half], swap(parts[half:], 1))
    if count == 8:
        rows = own.shape[1] // 2
        first, second = own[:, :rows], own[:, rows:]
        first = add_low(first[:2], swap(first[2:], 4))
        second_y = second[0::2]
        second = add_low(second_y, swap(second[1::2], 2))
        first = first[0].astype(f32) + swap(first[1], 2).astype(f32)
        second = second[0].astype(f32) + swap(second[1], 4).astype(f32)
        return jnp.concatenate([first, second], axis=0)
    while half > 1:
        half //= 2
        own = add_low(own[:half], swap(own[half:], 2 * half))
    return own[0].astype(f32)


NN = ((1,), (0,))
NT = ((1,), (1,))
TN = ((0,), (0,))
PAIR = 2


def low_dot(left_side, right_side, dims):
    bf16 = jnp.bfloat16
    return lax.dot_general(
        left_side.astype(bf16),
        right_side.astype(bf16),
        (dims, ((), ())),
        preferred_element_type=jnp.float32,
    )


def rounded(value):
    return value.astype(jnp.bfloat16).astype(jnp.float32)


def softplus(value):
    return jnp.maximum(value, 0.0) + jnp.log1p(jnp.exp(-jnp.abs(value)))


def rows_sum(value):
    return jnp.sum(value, axis=1, keepdims=True)


def stack(pieces):
    return jnp.concatenate(pieces, axis=0)


def half(value, which):
    return value[which * BLOCK : (which + 1) * BLOCK]


def fill_masks(mask_ref, level_ref):
    size = PAIR * BLOCK
    down = lax.broadcasted_iota(jnp.int32, (size, size), 0)
    across = lax.broadcasted_iota(jnp.int32, (size, size), 1)
    apart = down ^ across
    mask_ref[0] = jnp.where((apart < BLOCK) & (down >= across), 1.0, 0.0)
    mask_ref[1] = jnp.where(apart == 0, 1.0, 0.0)
    for level in range(level_ref.shape[0]):
        inside = (apart >= 1 << level) & (apart < 2 << level) & (down > across)
        level_ref[level] = jnp.where(inside, 1.0, 0.0).astype(jnp.bfloat16)


def head_pieces(convolved, extras, gate_ref, mine, width):
    chains = []
    for conv_out, extra in zip(convolved, extras):
        active = conv_out * jax.nn.sigmoid(conv_out)
        beta = rounded(jax.nn.sigmoid(extra))
        decay = rounded(-gate_ref[0:1] * softplus(extra + gate_ref[1:2]))
        for head in range(mine):
            part = [
                active[:, (kind * mine + head) * width : (kind * mine + head + 1) * width]
                for kind in range(3)
            ]
            chains.append(
                part + [beta[:, mine + head : mine + head + 1], decay[:, head : head + 1]]
            )
    return chains


def block_values(chains, mask_ref, width):
    raw_query, raw_key, value, beta, decay = [stack(list(pieces)) for pieces in zip(*chains)]
    scale_query = lax.rsqrt(rows_sum(raw_query * raw_query) + eps_norm)
    scale_key = lax.rsqrt(rows_sum(raw_key * raw_key) + eps_norm)
    unit_query, unit_key = raw_query * scale_query, raw_key * scale_key
    query = rounded(unit_query * width ** (-0.5))
    key = rounded(unit_key)
    value = rounded(value)
    within = mask_ref[0]
    cumulative = low_dot(within, jnp.broadcast_to(decay, query.shape), NN)
    along = jnp.transpose(cumulative)[0:1, :]
    fall = within * jnp.exp(within * (cumulative[:, 0:1] - along))
    key_key = low_dot(key, key, NT)
    query_key = low_dot(query, key, NT)
    last = stack(
        [
            jnp.broadcast_to(half(cumulative, which)[BLOCK - 1 :], (BLOCK, width))
            for which in range(PAIR)
        ]
    )
    growth = jnp.exp(cumulative)
    key_fall = jnp.exp(last - cumulative)
    return dict(
        scale_query=scale_query,
        scale_key=scale_key,
        unit_query=unit_query,
        unit_key=unit_key,
        query=query,
        key=key,
        value=value,
        beta=beta,
        fall=fall,
        key_key=key_key,
        query_key=query_key,
        scores=query_key * fall,
        growth=growth,
        key_fall=key_fall,
        key_grown=growth * key,
        query_grown=growth * query,
        key_fallen=key_fall * key,
        totals=jnp.exp(last),
    )


def mixer_forward_body(
    me_ref,
    proj_ref,
    extra_ref,
    conv_ref,
    gate_ref,
    gain_ref,
    mixed_ref,
    conv_out_ref,
    core_ref,
    inverse_ref,
    made_ref,
    written_ref,
    memory_ref,
    rows_ref,
    state_ref,
    mask_ref,
    level_ref,
):
    bf16 = jnp.bfloat16
    sequences = proj_ref.shape[2]
    width = gain_ref.shape[1]
    cols = mixed_ref.shape[4]
    mine = cols // width
    pairs = sequences * mine // PAIR
    taps = conv_ref.shape[0]
    core_bit = jnp.bitwise_and(me_ref[0], 1)

    @pl.when(pl.program_id(0) == 0)
    def _():
        rows_ref[...] = jnp.zeros_like(rows_ref)
        state_ref[...] = jnp.zeros_like(state_ref)
        fill_masks(mask_ref, level_ref)

    blocks = []
    for block in range(2):
        spot = jnp.bitwise_xor(core_bit, block)
        convolved, extras = [], []
        for seq in range(sequences):
            rows_ref[seq, 8:] = rounded(proj_ref[spot, 0, seq, :, : 3 * cols])
            conv_out = conv_ref[0:1] * rows_ref[seq, 9 - taps : 9 - taps + BLOCK]
            for tap in range(1, taps):
                first = 9 - taps + tap
                conv_out = conv_out + conv_ref[tap : tap + 1] * rows_ref[seq, first : first + BLOCK]
            rows_ref[seq, 0:8] = rows_ref[seq, BLOCK : BLOCK + 8]
            conv_out_ref[0, block, seq] = conv_out
            convolved.append(conv_out)
            extras.append(extra_ref[spot, 0, seq])
        chains = head_pieces(convolved, extras, gate_ref, mine, width)
        for pair in range(pairs):
            made = block_values(chains[PAIR * pair : PAIR * (pair + 1)], mask_ref, width)
            lower = (made["beta"] * made["key_key"] * made["fall"]).astype(bf16)
            made["lower"] = lower
            made["inverse"] = mask_ref[1] - (level_ref[0] * lower).astype(jnp.float32)
            blocks.append((block, pair, made))
    for level in range(1, level_ref.shape[0]):
        inner = [
            low_dot(level_ref[level] * made["lower"], made["inverse"], NN) for _, _, made in blocks
        ]
        for (_, _, made), right_side in zip(blocks, inner):
            made["inverse"] = made["inverse"] - low_dot(made["inverse"], right_side, NN)
    for block, pair, made in blocks:
        inverse = made["inverse"].astype(bf16)
        inverse_ref[0, block, pair] = inverse
        weighted = jnp.concatenate(
            [made["beta"] * made["value"], made["beta"] * made["key_grown"]], axis=1
        )
        made["fresh_carried"] = low_dot(inverse, weighted, NN)
        made_ref[0, block, pair] = made["fresh_carried"].astype(bf16)
    for block, pair, made in blocks:
        fresh, carried = made["fresh_carried"][:, :width], made["fresh_carried"][:, width:]
        written, results = [], []
        for which in range(PAIR):
            chain = PAIR * pair + which
            state = state_ref[chain]
            low_state = state.astype(bf16)
            memory_ref[0, block, chain] = low_state
            seen = low_dot(
                stack([half(carried, which), half(made["query_grown"], which)]), low_state, NN
            )
            new = half(fresh, which) - seen[:BLOCK]
            written.append(new)
            results.append(seen[BLOCK:])
            state_ref[chain] = half(made["totals"], which)[0:1] * state + low_dot(
                half(made["key_fallen"], which), new, TN
            )
        written = stack(written).astype(bf16)
        written_ref[0, block, pair] = written
        core = (stack(results) + low_dot(made["scores"], written, NN)).astype(bf16)
        core_ref[0, block, pair] = core
        core = core.astype(jnp.float32)
        normed = core * lax.rsqrt(rows_sum(core * core) / width + eps_norm) * gain_ref[0:1]
        spot = jnp.bitwise_xor(core_bit, block)
        for which in range(PAIR):
            seq, head = divmod(PAIR * pair + which, mine)
            span = slice(head * width, (head + 1) * width)
            out_gate = proj_ref[
                spot, 0, seq, :, 3 * cols + head * width : 3 * cols + (head + 1) * width
            ]
            mixed = half(normed, which) * out_gate * jax.nn.sigmoid(out_gate)
            mixed_ref[spot, 0, seq, :, span] = mixed.astype(bf16)


def mixer_backward_body(
    me_ref,
    proj_ref,
    extra_ref,
    grad_mixed_ref,
    conv_out_ref,
    core_ref,
    inverse_ref,
    made_ref,
    written_ref,
    memory_ref,
    conv_ref,
    gate_ref,
    gain_ref,
    grad_proj_ref,
    grad_extra_ref,
    grad_conv_ref,
    grad_small_ref,
    rows_ref,
    state_ref,
    mask_ref,
    level_ref,
):
    f32 = jnp.float32
    bf16 = jnp.bfloat16
    sequences = proj_ref.shape[2]
    width = gain_ref.shape[1]
    cols = grad_mixed_ref.shape[4]
    mine = cols // width
    pairs = sequences * mine // PAIR
    taps = conv_ref.shape[0]
    core_bit = jnp.bitwise_and(me_ref[0], 1)

    @pl.when(pl.program_id(0) == 0)
    def _():
        rows_ref[...] = jnp.zeros_like(rows_ref)
        state_ref[...] = jnp.zeros_like(state_ref)
        grad_conv_ref[...] = jnp.zeros_like(grad_conv_ref)
        grad_small_ref[...] = jnp.zeros_like(grad_small_ref)
        fill_masks(mask_ref, level_ref)

    within = mask_ref[0]
    gain = gain_ref[0:1]
    grad_gain = jnp.zeros((1, width), f32)
    blocks = []
    for block in (1, 0):
        spot = jnp.bitwise_xor(core_bit, block)
        convolved = [conv_out_ref[0, block, seq] for seq in range(sequences)]
        extras = [extra_ref[spot, 0, seq] for seq in range(sequences)]
        chains = head_pieces(convolved, extras, gate_ref, mine, width)
        for pair in range(pairs):
            made = block_values(chains[PAIR * pair : PAIR * (pair + 1)], mask_ref, width)
            core = core_ref[0, block, pair].astype(f32)
            core_scale = lax.rsqrt(rows_sum(core * core) / width + eps_norm)
            normed = core * core_scale
            grad_unit = []
            for which in range(PAIR):
                seq, head = divmod(PAIR * pair + which, mine)
                span = slice(3 * cols + head * width, 3 * cols + (head + 1) * width)
                out_gate = proj_ref[spot, 0, seq, :, span]
                grad_mixed = grad_mixed_ref[
                    spot, 0, seq, :, head * width : (head + 1) * width
                ].astype(f32)
                sigmoid = jax.nn.sigmoid(out_gate)
                silu = out_gate * sigmoid
                scaled = grad_mixed * half(normed, which)
                grad_gate = scaled * gain * (sigmoid + silu * (1.0 - sigmoid))
                grad_proj_ref[spot, 0, seq, :, span] = grad_gate.astype(bf16)
                grad_gain = grad_gain + jnp.sum(scaled * silu, axis=0, keepdims=True)
                grad_unit.append(grad_mixed * gain * silu)
            grad_unit = stack(grad_unit)
            inner = rows_sum(grad_unit * normed) / width
            made["grad_core"] = (core_scale * (grad_unit - normed * inner)).astype(bf16)
            made["from_scores"] = low_dot(made["scores"], made["grad_core"], TN)
            made["grad_scores"] = (
                low_dot(made["grad_core"], written_ref[0, block, pair], NT) * made["fall"]
            )
            blocks.append((block, pair, made))
    grad_small_ref[0:1] += grad_gain

    for block, pair, made in blocks:
        carried = made_ref[0, block, pair, :, width:]
        parts = []
        for which in range(PAIR):
            chain = PAIR * pair + which
            state, grad_state = memory_ref[0, block, chain], state_ref[chain]
            low_grad_state = grad_state.astype(bf16)
            grad_out = half(made["grad_core"], which)
            grad_new = half(made["from_scores"], which) + low_dot(
                half(made["key_fallen"], which), low_grad_state, NN
            )
            low_new = grad_new.astype(bf16)
            totals = half(made["totals"], which)[0:1]
            state_ref[chain] = (
                totals * grad_state
                + low_dot(half(made["query_grown"], which), grad_out, TN)
                - low_dot(half(carried, which), low_new, TN)
            )
            back = low_dot(stack([grad_out, low_new]), state, NT)
            parts.append(
                (
                    low_new,
                    back[:BLOCK],
                    -back[BLOCK:],
                    low_dot(half(written_ref[0, block, pair], which), low_grad_state, NT),
                    rows_sum(
                        jnp.sum(state.astype(f32) * grad_state, axis=0, keepdims=True) * totals
                    ),
                )
            )
        made["grad_new"], made["grad_query_grown"], made["grad_carried"] = [
            stack([part[index] for part in parts]) for index in range(3)
        ]
        made["grad_key_fallen"] = stack([part[3] for part in parts])
        made["grad_totals"] = [part[4] for part in parts]

    lane = lax.broadcasted_iota(jnp.int32, (BLOCK, extra_ref.shape[4]), 1)
    at_end = lax.broadcasted_iota(jnp.int32, (BLOCK, 1), 0) == BLOCK - 1
    ones = jnp.ones((PAIR * BLOCK, width), bf16)
    results = {}
    for block, pair, made in blocks:
        beta, growth, fall = made["beta"], made["growth"], made["fall"]
        query, key, value = made["query"], made["key"], made["value"]
        fall_strict = fall - mask_ref[1]
        grad_weighted = low_dot(
            inverse_ref[0, block, pair],
            jnp.concatenate([made["grad_new"].astype(f32), made["grad_carried"]], axis=1),
            TN,
        )
        grad_lower = -low_dot(grad_weighted, made_ref[0, block, pair], NT) * fall_strict
        grad_key_key = grad_lower * beta
        from_lower = grad_lower * made["key_key"]
        grad_value_part, grad_key_part = grad_weighted[:, :width], grad_weighted[:, width:]
        grad_scores = made["grad_scores"]
        carried_part = grad_key_part * made["key_grown"]
        grad_beta = rows_sum(from_lower) + rows_sum(carried_part + grad_value_part * value)
        shifts = beta * from_lower + grad_scores * made["query_key"]
        fallen_part = made["grad_key_fallen"] * made["key_fallen"]
        fallen = rows_sum(fallen_part)
        grad_cumulative = rows_sum(shifts) + rows_sum(
            made["grad_query_grown"] * made["query_grown"] + beta * carried_part - fallen_part
        )
        ends = stack(
            [
                jnp.where(
                    at_end,
                    jnp.sum(half(fallen, which), axis=0, keepdims=True) + made["grad_totals"][which],
                    0.0,
                )
                for which in range(PAIR)
            ]
        )
        grad_cumulative = grad_cumulative + ends - low_dot(shifts, ones, TN)
        grad_decay = rounded(low_dot(within, grad_cumulative, TN))
        both = stack([grad_scores, grad_key_key]).astype(bf16)
        down = low_dot(both, key, NN)
        grad_query = growth * made["grad_query_grown"] + down[: PAIR * BLOCK]
        grad_key = (
            made["key_fall"] * made["grad_key_fallen"]
            + beta * growth * grad_key_part
            + down[PAIR * BLOCK :]
            + low_dot(both, stack([query, key]), TN)
        )
        grad_query = rounded(grad_query) * width ** (-0.5)
        grad_key = rounded(grad_key)
        grad_value = rounded(beta * grad_value_part)
        grad_beta = rounded(grad_beta)
        unit_query, unit_key = made["unit_query"], made["unit_key"]
        grad_query = made["scale_query"] * (
            grad_query - unit_query * rows_sum(grad_query * unit_query)
        )
        grad_key = made["scale_key"] * (grad_key - unit_key * rows_sum(grad_key * unit_key))
        for which in range(PAIR):
            results[block, PAIR * pair + which] = [
                half(part, which)
                for part in (grad_query, grad_key, grad_value, grad_decay, grad_beta)
            ]

    for block in (1, 0):
        spot = jnp.bitwise_xor(core_bit, block)
        for seq in range(sequences):
            conv_out = conv_out_ref[0, block, seq]
            sigmoid = jax.nn.sigmoid(conv_out)
            chains = [results[block, seq * mine + head] for head in range(mine)]
            grad_active = jnp.concatenate(
                [chain[kind] for kind in range(3) for chain in chains], axis=1
            )
            rows_ref[seq, :BLOCK] = grad_active * sigmoid * (1.0 + conv_out * (1.0 - sigmoid))
            pre = rounded(proj_ref[spot, 0, seq, :, : 3 * cols])
            grad_pre = jnp.zeros_like(conv_out)
            for tap in range(taps):
                shifted = rows_ref[seq, taps - 1 - tap : taps - 1 - tap + BLOCK]
                grad_pre = grad_pre + conv_ref[tap : tap + 1] * shifted
                grad_conv_ref[tap : tap + 1] += jnp.sum(pre * shifted, axis=0, keepdims=True)
            grad_proj_ref[spot, 0, seq, :, : 3 * cols] = grad_pre.astype(bf16)
            rows_ref[seq, BLOCK:] = rows_ref[seq, 0:8]
            extra = extra_ref[spot, 0, seq]
            moved = extra + gate_ref[1:2]
            spread_decay = jnp.zeros_like(extra)
            spread_beta = jnp.zeros_like(extra)
            for head, chain in enumerate(chains):
                spread_decay = jnp.where(lane == head, chain[3][:, 0:1], spread_decay)
                spread_beta = jnp.where(lane == mine + head, chain[4], spread_beta)
            grad_alpha = -gate_ref[0:1] * spread_decay * jax.nn.sigmoid(moved)
            squash = jax.nn.sigmoid(extra)
            grad_extra = grad_alpha + spread_beta * squash * (1.0 - squash)
            grad_extra_ref[spot, 0, seq] = grad_extra.astype(bf16)
            grad_small_ref[1:2] -= jnp.sum(spread_decay * softplus(moved), axis=0, keepdims=True)
            grad_small_ref[2:3] += jnp.sum(grad_alpha, axis=0, keepdims=True)


def ff_pack_body(width, gate_ref, up_ref, out_ref):
    count = out_ref.shape[0]
    blocks = gate_ref.shape[1] // (count * width)
    for spot in range(count):
        pieces = [
            ref[:, (block * count + spot) * width : (block * count + spot + 1) * width]
            for ref in (gate_ref, up_ref)
            for block in range(blocks)
        ]
        out_ref[spot] = jnp.concatenate(pieces, axis=1)


def ff_pack(gate, up, count, width):
    rows, hidden = gate.shape
    return pl.pallas_call(
        functools.partial(ff_pack_body, width),
        out_shape=jax.ShapeDtypeStruct((count, rows, 2 * hidden // count), gate.dtype),
    )(gate, up)


def ff_unpack_body(width, in_ref, gate_ref, up_ref):
    count = in_ref.shape[0]
    blocks = gate_ref.shape[1] // (count * width)
    for which, ref in enumerate((gate_ref, up_ref)):
        pieces = []
        for block in range(blocks):
            first = (which * blocks + block) * width
            pieces += [in_ref[spot, :, first : first + width] for spot in range(count)]
        ref[...] = jnp.concatenate([piece.astype(jnp.float32) for piece in pieces], axis=1)


def ff_unpack(packed, width):
    count, rows, columns = packed.shape
    shape = jax.ShapeDtypeStruct((rows, count * columns // 2), jnp.float32)
    return pl.pallas_call(functools.partial(ff_unpack_body, width), out_shape=[shape, shape])(packed)


def whole_spec(shape):
    return pl.BlockSpec(shape, lambda step, me: (0,) * len(shape))


def mixer_specs(projected, head_width, mine, forward):
    _, steps, sequences, span, _ = projected.shape
    chains = sequences * mine
    pairs = chains // PAIR
    cols = mine * head_width

    def step_of(step):
        return step if forward else steps - 1 - step

    def gathered(channels):
        return pl.BlockSpec(
            (2, 1, sequences, span, channels),
            lambda step, me: (
                0,
                jnp.bitwise_xor(jnp.right_shift(me[0], 1), step_of(step)),
                0,
                0,
                0,
            ),
        )

    def ordered(*shape):
        return pl.BlockSpec((1,) + shape, lambda step, me: (step_of(step),) + (0,) * len(shape))

    size = PAIR * span
    kept = [
        (jax.ShapeDtypeStruct((steps,) + shape, kind), ordered(*shape))
        for shape, kind in [
            ((2, sequences, span, 3 * cols), jnp.float32),
            ((2, pairs, size, head_width), jnp.bfloat16),
            ((2, pairs, size, size), jnp.bfloat16),
            ((2, pairs, size, 2 * head_width), jnp.bfloat16),
            ((2, pairs, size, head_width), jnp.bfloat16),
            ((2, chains, head_width, head_width), jnp.bfloat16),
        ]
    ]
    scratch = [
        pltpu.VMEM((sequences, span + 8, 3 * cols), jnp.float32),
        pltpu.VMEM((chains, head_width, head_width), jnp.float32),
        pltpu.VMEM((2, size, size), jnp.float32),
        pltpu.VMEM((int(BLOCK).bit_length() - 1, size, size), jnp.bfloat16),
    ]
    cost = pl.CostEstimate(
        flops=4 * steps * pairs * size**3 * 18,
        bytes_accessed=12 << 20,
        transcendentals=2 * steps << 18,
    )
    return gathered, kept, scratch, cost


def mixer_forward(me, projected, extra, conv_mine, gate_rows, gain_row, mine):
    channels = projected.shape[-1]
    head_width = gain_row.shape[1]
    gathered, kept, scratch, cost = mixer_specs(projected, head_width, mine, True)
    cols = mine * head_width
    return pl.pallas_call(
        mixer_forward_body,
        grid_spec=pltpu.PrefetchScalarGridSpec(
            num_scalar_prefetch=1,
            grid=(projected.shape[1],),
            in_specs=[
                gathered(channels),
                gathered(extra.shape[-1]),
                whole_spec(conv_mine.shape),
                whole_spec(gate_rows.shape),
                whole_spec(gain_row.shape),
            ],
            out_specs=[gathered(cols)] + [spec for _, spec in kept],
            scratch_shapes=scratch,
        ),
        out_shape=[jax.ShapeDtypeStruct(projected.shape[:-1] + (cols,), jnp.bfloat16)]
        + [shape for shape, _ in kept],
        compiler_params=pltpu.CompilerParams(vmem_limit_bytes=40 << 20),
        cost_estimate=cost,
    )(me, projected, extra, conv_mine, gate_rows, gain_row)


def mixer_backward(
    me, projected, extra, grad_mixed, kept_values, conv_mine, gate_rows, gain_row, mine
):
    channels = projected.shape[-1]
    head_width = gain_row.shape[1]
    gathered, kept, scratch, cost = mixer_specs(projected, head_width, mine, False)
    cols = mine * head_width
    return pl.pallas_call(
        mixer_backward_body,
        grid_spec=pltpu.PrefetchScalarGridSpec(
            num_scalar_prefetch=1,
            grid=(projected.shape[1],),
            in_specs=[gathered(channels), gathered(extra.shape[-1]), gathered(cols)]
            + [spec for _, spec in kept]
            + [
                whole_spec(conv_mine.shape),
                whole_spec(gate_rows.shape),
                whole_spec(gain_row.shape),
            ],
            out_specs=[
                gathered(channels),
                gathered(extra.shape[-1]),
                whole_spec(conv_mine.shape),
                whole_spec((8, head_width)),
            ],
            scratch_shapes=scratch,
        ),
        out_shape=[
            jax.ShapeDtypeStruct(projected.shape, jnp.bfloat16),
            jax.ShapeDtypeStruct(extra.shape, jnp.bfloat16),
            jax.ShapeDtypeStruct(conv_mine.shape, jnp.float32),
            jax.ShapeDtypeStruct((8, head_width), jnp.float32),
        ],
        compiler_params=pltpu.CompilerParams(vmem_limit_bytes=40 << 20),
        cost_estimate=cost,
    )(me, projected, extra, grad_mixed, *kept_values, conv_mine, gate_rows, gain_row)


def after(value, *others):
    return lax.optimization_barrier((value,) + others)[0]


def on_device(
    inputs,
    norm_attn,
    w_query,
    w_key,
    w_value,
    conv_weight,
    w_alpha,
    w_beta,
    decay_rate,
    decay_bias,
    w_outgate,
    head_gain,
    w_output,
    norm_mlp,
    w_gate,
    w_up,
    w_down,
    cotangent,
):
    f32 = jnp.float32
    bf16 = jnp.bfloat16
    n_dp = lax.axis_size("dp")
    n_seq = lax.axis_size("seq")
    devices = n_dp * n_seq
    me = lax.axis_index("seq")
    rows, width = w_query.shape
    heads = w_alpha.shape[1]
    head_width = head_gain.shape[0]
    mine = heads // n_seq
    cols = mine * head_width
    group = head_width // rows
    bands = n_seq // group
    band, place = me // group, me % group
    hidden = w_gate.shape[1]
    ff_rows = w_down.shape[0]
    ff = n_dp * ff_rows
    taps = conv_weight.shape[0]
    tokens_shape = inputs.shape
    span = inputs.shape[2]
    count = inputs.shape[0] * inputs.shape[1]
    total = n_seq * count * span

    def by_device(weight):
        split = weight.reshape(weight.shape[0], group, mine, bands, -1)
        return jnp.transpose(split, (3, 1, 0, 2, 4)).reshape(n_seq, weight.shape[0], -1)

    def by_columns(blocks):
        pieces = []
        for head in range(heads):
            spot, from_band = divmod(head, bands)
            from_place, which = divmod(spot, mine)
            block = blocks[from_band * group + from_place]
            pieces.append(block[:, which * head_width : (which + 1) * head_width])
        return jnp.concatenate(pieces, axis=1).astype(f32)

    def swap_all(blocks):
        return lax.all_to_all(blocks, ALL, split_axis=0, concat_axis=0, tiled=True)

    packed = jnp.concatenate([by_device(w) for w in (w_query, w_key, w_value, w_outgate)], axis=2)

    def exchange(blocks):
        return lax.all_to_all(blocks, "seq", split_axis=0, concat_axis=0, tiled=True)

    def gather_dp(block):
        return lax.all_gather(block, "dp", axis=0, tiled=True)

    sent = exchange(packed)
    mixer_full = gather_dp(sent.reshape(n_seq * rows, -1))
    shared = jnp.concatenate(
        [
            w_alpha.T.reshape(-1),
            w_beta.T.reshape(-1),
            norm_attn,
            norm_mlp,
            conv_weight.reshape(-1),
        ]
    )
    shared, w_gate, w_up, sent = lax.optimization_barrier((shared, w_gate, w_up, sent))
    shared = swap_all(jnp.broadcast_to(shared[None], (devices, shared.shape[0])))

    groups = [list(range(first, first + group)) for first in range(0, n_seq, group)]

    def exchange_group(blocks):
        if group == 2:
            away = swap(lax.dynamic_index_in_dim(blocks, 1 - place, 0, keepdims=False), 1)
            stay = lax.dynamic_index_in_dim(blocks, place, 0, keepdims=False)
            low = place == 0
            return jnp.stack([jnp.where(low, stay, away), jnp.where(low, away, stay)], axis=0)
        return lax.all_to_all(
            blocks, "seq", split_axis=0, concat_axis=0, tiled=True, axis_index_groups=groups
        )

    def to_heads(pieces):
        split = exchange_group(pieces.reshape(group, mine * rows, width))
        split = split.reshape(group, mine, rows, width)
        return jnp.transpose(split, (1, 0, 2, 3)).reshape(cols, width)

    def from_heads(full):
        split = jnp.transpose(full.reshape(mine, group, rows, width), (1, 0, 2, 3))
        return exchange_group(split.reshape(group, mine * rows, width))

    output_full = to_heads(gather_dp(w_output))

    gate_up_sent = exchange(ff_pack(w_gate, w_up, n_seq, ff_rows)).reshape(n_seq * rows, -1)
    gate_up_full = gather_dp(gate_up_sent)
    down_full = gather_dp(w_down).reshape(ff, width)
    mixer_full, shared, output_full = lax.optimization_barrier((mixer_full, shared, output_full))

    x_own = inputs.reshape(count * span, width)
    x_all = gather_seq(x_own).reshape(total, width)
    seed_own = cotangent.reshape(count * span, width)
    seed_all = gather_seq(seed_own).reshape(total, width)

    gates = shared[:, : 2 * heads * rows].reshape(devices, 2 * heads, rows)
    gates = jnp.transpose(gates, (1, 0, 2)).reshape(2, group, mine, bands, width)
    gates = lax.dynamic_index_in_dim(gates, band, 3, keepdims=False)
    gates = lax.dynamic_index_in_dim(gates, place, 1, keepdims=False).reshape(2 * mine, width)
    gates = jnp.pad(gates, ((0, 128 - 2 * mine), (0, 0)))
    first = 2 * heads * rows
    gain_attn = shared[:, first : first + rows].reshape(-1).astype(f32)
    gain_mlp = shared[:, first + rows : first + 2 * rows].reshape(-1).astype(f32)
    conv_all = shared[:, first + 2 * rows :].reshape(devices, taps, -1)
    conv_all = jnp.transpose(conv_all, (1, 0, 2)).reshape(taps, 3, group, mine, bands, head_width)
    conv_mine = lax.dynamic_index_in_dim(conv_all, band, 4, keepdims=False)
    conv_mine = lax.dynamic_index_in_dim(conv_mine, place, 2, keepdims=False)
    conv_mine = conv_mine.reshape(taps, 3 * cols).astype(f32)

    def my_heads(vector):
        split = lax.dynamic_index_in_dim(vector.reshape(group, mine, bands), band, 2, False)
        return lax.dynamic_index_in_dim(split, place, 0, keepdims=False)

    rate_mine = my_heads(decay_rate)
    bias_mine = my_heads(decay_bias)

    hidden_in = rms_scale(x_all.astype(f32), gain_attn).astype(bf16)
    projected = product(hidden_in, mixer_full)
    extra = times_transposed(hidden_in, gates).reshape(2, n_seq // 2, count, span, -1)

    projected = projected.reshape(2, n_seq // 2, count, span, -1)
    me_row = me.astype(jnp.int32).reshape(1)
    gate_rows = jnp.zeros((2, gates.shape[0]), f32)
    gate_rows = gate_rows.at[0, :mine].set(rate_mine).at[1, :mine].set(bias_mine)
    gain_row = head_gain.reshape(1, head_width)
    mixed, *kept_values = mixer_forward(
        me_row, projected, extra, conv_mine, gate_rows, gain_row, mine
    )
    mixed = mixed.reshape(total, cols)

    def shares(value):
        return value.astype(bf16).reshape(n_seq, count * span, -1)

    residual = x_own.astype(f32) + scatter_seq(shares(product(mixed, output_full)))
    normed_mid, pull_mid = jax.vjp(rms_scale, residual, gain_mlp)
    hidden_mid = gather_seq(normed_mid.astype(bf16)).reshape(total, width)
    gate_up = product(hidden_mid, gate_up_full)
    gate_pre, up_proj = gate_up[:, :ff], gate_up[:, ff:]
    sigmoid_gate = jax.nn.sigmoid(gate_pre)
    silu_gate = gate_pre * sigmoid_gate
    activ = (silu_gate * up_proj).astype(bf16)
    down_grads = contract_rows(activ, seed_all).astype(bf16)
    down_full, down_grads = lax.optimization_barrier((down_full, down_grads))
    from_down = times_transposed(seed_all, down_full)
    grad_gate = from_down * up_proj * sigmoid_gate * (1.0 + gate_pre * (1.0 - sigmoid_gate))
    grad_gate_up = jnp.concatenate([grad_gate, from_down * silu_gate], axis=1).astype(bf16)
    back_mid = scatter_seq(shares(times_transposed(grad_gate_up, gate_up_full)))
    grad_res_norm, grad_gain_mlp = pull_mid(back_mid)
    grad_res = seed_own.astype(f32) + grad_res_norm

    def scatter_dp(value):
        return lax.psum_scatter(value.astype(bf16), "dp", scatter_dimension=0, tiled=True)

    grad_down = scatter_dp(down_grads)
    grad_gate_up_own = scatter_dp(contract_rows(hidden_mid, grad_gate_up))

    grad_mixer_out = gather_seq(grad_res.astype(bf16)).reshape(total, width)
    grad_mixed = times_transposed(grad_mixer_out, output_full).astype(bf16)
    grad_projected, grad_extra, grad_conv, grad_small = mixer_backward(
        me_row,
        projected,
        extra,
        grad_mixed.reshape(2, n_seq // 2, count, span, cols),
        kept_values,
        conv_mine,
        gate_rows,
        gain_row,
        mine,
    )
    grad_projected = grad_projected.reshape(total, -1)
    grad_extra = grad_extra.reshape(total, -1)
    grad_head_gain = grad_small[0]
    grad_rate, grad_bias = grad_small[1, :mine], grad_small[2, :mine]
    grad_output = from_heads(contract_rows(mixed, grad_mixer_out).astype(bf16))
    weight_grads = contract_rows(hidden_in, grad_projected).astype(bf16)
    weight_grads = jnp.concatenate([weight_grads, grad_output.reshape(width, -1)], axis=1)
    weight_grads, grad_projected, grad_extra, activ = lax.optimization_barrier(
        (weight_grads, grad_projected, grad_extra, activ)
    )
    mixer_own = scatter_dp(weight_grads)
    back_in = times_transposed(grad_projected, mixer_full) + product(grad_extra, gates)
    back_in = scatter_seq(shares(back_in))
    grad_gate_up_own = exchange(grad_gate_up_own.reshape(n_seq, rows, -1))
    output_own = residual + scatter_seq(shares(product(activ, down_full)))
    grad_w_gate, grad_w_up = ff_unpack(grad_gate_up_own, ff_rows)
    back_in, grad_w_gate, grad_w_up = lax.optimization_barrier((back_in, grad_w_gate, grad_w_up))
    tokens = x_own.astype(f32)
    _, pull_in = jax.vjp(rms_scale, tokens, gain_attn)
    grad_tok_norm, grad_gain_attn = pull_in(back_in)
    input_grad = grad_res + grad_tok_norm

    conv_grad = jnp.zeros((taps, 3, group, mine, bands, head_width), f32)
    conv_grad = lax.dynamic_update_slice(
        conv_grad,
        grad_conv.reshape(taps, 3, 1, mine, 1, head_width),
        (0, 0, place, 0, band, 0),
    )
    conv_grad = jnp.transpose(conv_grad.reshape(taps, devices, -1), (1, 0, 2))
    gate_grad = contract_rows(grad_extra, hidden_in)[: 2 * mine]
    def place_heads(vector):
        slots = jnp.zeros((group, mine, bands), f32)
        return lax.dynamic_update_slice(
            slots, vector.reshape(1, mine, 1), (place, 0, band)
        ).reshape(heads)

    def by_owner(values):
        split = values.reshape(-1, devices, rows)
        return jnp.transpose(split, (1, 0, 2)).reshape(devices, -1)

    common = jnp.concatenate([grad_head_gain, place_heads(grad_rate), place_heads(grad_bias)])
    parts = [
        by_owner(gate_grad),
        by_owner(jnp.stack([grad_gain_attn, grad_gain_mlp])),
        conv_grad.reshape(devices, -1),
        jnp.broadcast_to(common[None], (devices, common.shape[0])),
    ]
    edges = [0]
    for part in parts:
        edges.append(edges[-1] + part.shape[1])
    parts.append(jnp.zeros((devices, -edges[-1] % 128), f32))
    swapped = swap_all(jnp.concatenate(parts, axis=1))
    done = lax.optimization_barrier(
        (swapped, grad_w_gate, grad_w_up, grad_down.astype(f32), output_own, input_grad)
    )
    mixer_own, *done = lax.optimization_barrier((mixer_own, *done))
    swapped, grad_w_gate, grad_w_up, grad_down, output_own, input_grad = done
    grad_output = mixer_own[:, 4 * cols :].reshape(rows, width).astype(f32)
    mixer_own = exchange(mixer_own[:, : 4 * cols].reshape(n_seq, rows, -1))
    sums = jnp.sum(swapped, axis=0)
    gate_sums = jnp.sum(swapped[:, : edges[1]].reshape(n_dp, n_seq, -1), axis=0)
    gate_sums = gate_sums.reshape(bands, group, 2, mine, rows)
    gate_sums = jnp.transpose(gate_sums, (2, 4, 1, 3, 0)).reshape(2, rows, heads)
    gain_sums = sums[edges[1] : edges[2]].reshape(2, rows)
    common = sums[edges[3] : edges[4]]
    return (
        output_own.astype(bf16).reshape(tokens_shape),
        input_grad.reshape(tokens_shape),
        gain_sums[0],
        by_columns(mixer_own[:, :, :cols]),
        by_columns(mixer_own[:, :, cols : 2 * cols]),
        by_columns(mixer_own[:, :, 2 * cols : 3 * cols]),
        sums[edges[2] : edges[3]].reshape(conv_weight.shape),
        gate_sums[0],
        gate_sums[1],
        common[head_width : head_width + heads],
        common[head_width + heads :],
        by_columns(mixer_own[:, :, 3 * cols :]),
        common[:head_width],
        grad_output,
        gain_sums[1],
        grad_w_gate,
        grad_w_up,
        grad_down,
    )


def solution(mesh):
    in_specs = (
        P(None, "dp", "seq", None),
        P(("dp", "seq")),
        P(("dp", "seq"), None),
        P(("dp", "seq"), None),
        P(("dp", "seq"), None),
        P(None, ("dp", "seq")),
        P(("dp", "seq"), None),
        P(("dp", "seq"), None),
        P(),
        P(),
        P(("dp", "seq"), None),
        P(),
        P(("dp", "seq"), None),
        P(("dp", "seq")),
        P(("dp", "seq"), None),
        P(("dp", "seq"), None),
        P(("dp", "seq"), None),
        P(None, "dp", "seq", None),
    )
    out_specs = (
        P(None, "dp", "seq", None),
        P(None, "dp", "seq", None),
        P(("dp", "seq")),
        P(("dp", "seq"), None),
        P(("dp", "seq"), None),
        P(("dp", "seq"), None),
        P(None, ("dp", "seq")),
        P(("dp", "seq"), None),
        P(("dp", "seq"), None),
        P(),
        P(),
        P(("dp", "seq"), None),
        P(),
        P(("dp", "seq"), None),
        P(("dp", "seq")),
        P(("dp", "seq"), None),
        P(("dp", "seq"), None),
        P(("dp", "seq"), None),
    )
    return jax.shard_map(
        on_device, mesh=mesh, in_specs=in_specs, out_specs=out_specs, check_vma=False
    )
```

time: 4050 us -> 605 us (0.15)
  waiting for transfers between devices: 2830 us -> 207 us
  matrix products: 582 us -> 88.4 us
  blocking collectives: 199 us -> 44.3 us
  local copies, waits for them, and re-layouts: 211 us -> 82.8 us
  starting transfers between devices: 112 us -> 50 us
  Pallas kernels: 0 us -> 44.6 us
    reduce_scatter x8 -> x3, waiting for transfers between devices: 2410 us -> 20.4 us  [scatter_dp(): lax.psum_scatter(value.astype(bf16), 'dp', scatter_dimension=0, tiled=True)]
    all_gather x8 -> x4, waiting for transfers between devices: 298 us -> 41.4 us  [gather_dp(): return lax.all_gather(block, 'dp', axis=0, tiled=True)]
    dot_general x292 -> x0, matrix products: 242 us -> none  [the longest x64 43.8 us: advance(): jnp.einsum('hid,hde->hie', carried_now, memory, precision=highest)]
    all_gather x3 -> x0, blocking collectives: 118 us -> none  [the longest x1 41.8 us: on_device(): lax.all_gather(w_alpha, ('dp', 'seq'), axis=0, tiled=True)]
    dot_general x20 -> x5, matrix products: 135 us -> 32.9 us  [times_transposed(): lax.dot_general(left_side, right_side, (((1,), (1,)), ((), ())), preferre...]
    ppermute x4 -> x54, waiting for transfers between devices: 1.92 us -> 101 us  [swap(): lax.ppermute(value, 'seq', [(place, place ^ bit) for place in range(count)])]
    all_to_all x24 -> x4, starting transfers between devices: 101 us -> 14.5 us  [the longest x2 7.94 us: exchange(): lax.all_to_all(blocks, 'seq', split_axis=0, concat_axis=0, tiled=True)]
    unnamed x2 -> x0, blocking collectives: 80.6 us -> none
  transfers between devices with their start and end apart: 47 -> 65, of which waited for: 30 -> 33; matrix products, arithmetic and copies ran while one was open for 15% -> 34% of each run, Pallas kernels for 0% -> 7%
where the time goes in v1:
time: 605 us; the launch traced here: 595 us
  waiting for transfers between devices  207 us (34%)
  matrix products  88.4 us (15%)
  local copies, waits for them, and re-layouts  82.8 us (14%)
  other arithmetic  61.5 us (10%)
  starting transfers between devices  50 us (8%)
  Pallas kernels  44.6 us (7%)
  blocking collectives  44.3 us (7%)
  between operations  16.3 us (3%)
    ppermute x54, waiting for transfers between devices, swap(): lax.ppermute(value, 'seq', [(place, place ^ bit) for place in range(count)])  101 us
    all_to_all x2, blocking collectives, exchange(): lax.all_to_all(blocks, 'seq', split_axis=0, concat_axis=0, tiled=True)  44.3 us
    unnamed x224, local copies, waits for them, and re-layouts  41.8 us
    all_gather x4, waiting for transfers between devices, gather_dp(): return lax.all_gather(block, 'dp', axis=0, tiled=True)  41.4 us
    ppermute x54, starting transfers between devices, swap(): lax.ppermute(value, 'seq', [(place, place ^ bit) for place in range(count)])  35 us
    dot_general x5, matrix products, times_transposed(): lax.dot_general(left_side, right_side, (((1,), (1,)), ((), ())), preferre...  32.9 us
    dot_general x5, matrix products, product(): return jnp.dot(left_side, right_side, preferred_element_type=jnp.float32)  28.2 us
    dot_general x5, matrix products, contract_rows(): lax.dot_general(left_side, right_side, (((0,), (0,)), ((), ())), preferre...  27.3 us
  transfers between devices with their start and end apart: 65, of which 33 were waited for; matrix products, arithmetic and copies ran while one was open for 34% of the time, Pallas kernels for 7%

profile of v1, /device:TPU:0, one launch (start us, length us, event | category | flops | bytes accessed | tf_op | source)
XLA Modules:
  0.0 595.3 jit_solution(6186752547631725781)
XLA Ops:
  13.3 20.4 %all_to_all.41 = bf16[8,64,1024]{2,1,0:T(8,128)(2,1)} all-to-all(bf16[8,64,1024]{2,1,0:T(8,128)(2,1)S(1)} %pad_maximum_fusion.4), channel_id=1, replica_groups=mesh['dp'=4,'seq'=8] {'seq'}, dimensions={0} | all-to-all | bytes 2097152 | tf_op jit(solution)/shard_map/all_to_all | solution.py:745
  37.2 23.8 %all_to_all.42 = bf16[8,64,1408]{2,1,0:T(8,128)(2,1)} all-to-all(bf16[8,64,1408]{2,1,0:T(8,128)(2,1)} %shard_map.314), channel_id=1, replica_groups=mesh['dp'=4,'seq'=8] {'seq'}, dimensions={0} | all-to-all | bytes 2883584 | tf_op jit(solution)/shard_map/all_to_all | solution.py:745
  68.6 7.4 %collective-permute-done = bf16[128,2048]{1,0:T(8,128)(2,1)S(1)} collective-permute-done((bf16[128,2048]{1,0:T(8,128)(2,1)S(1)}, bf16[128,2048]{1,0:T(8,128)(2,1)S(1)}, u32[]{:S(2)}, u32[]{:S(2)}) %collective-permute-start) | collective-permute-done | bytes 524320 | tf_op jit(solution)/shard_map/ppermute | solution.py:46
  79.9 7.5 %collective-permute-done.9 = bf16[128,2048]{1,0:T(8,128)(2,1)} collective-permute-done((bf16[128,2048]{1,0:T(8,128)(2,1)}, bf16[128,2048]{1,0:T(8,128)(2,1)}, u32[]{:S(2)}, u32[]{:S(2)}) %collective-permute-start.9) | collective-permute-done | bytes 524320 | tf_op jit(solution)/shard_map/ppermute | solution.py:46
  107.9 9.2 %all-to-all-done.1 = bf16[32,2,1472]{2,1,0:T(2,128)(2,1)S(1)} async-done(((bf16[32,2,1472]{2,1,0:T(2,128)(2,1)}), bf16[32,2,1472]{2,1,0:T(2,128)(2,1)S(1)}, u32[]{:S(2)}, u32[]{:S(2)}) %all-to-all-start.1) | async-done | bytes 188448 | tf_op jit(solution)/shard_map/all_to_all | solution.py:740
  131.6 9.3 %fusion.6.proj_ref = f32[2,4,2,64,1024]{4,3,2,1,0:T(8,128)} fusion(bf16[2048,1024]{1,0:T(8,128)(2,1)S(1)} %copy-done.59, f32[2048]{0:T(1024)S(1)} %reshape.804, f32[2,4,2,64]{3,2,1,0:T(2,128)S(1)} %rsqrt.40, bf16[2,4,2,64,2048]{4,3,2,1,0:T(8,128)(2,1)} %bitcast.320), kind=kOutput, calls=%fused_computation.17 | convolution fusion | flops 4303355904 | bytes 12595200 | tf_op jit(solution)/shard_map/dot_general | solution.py:26
  144.5 14.0 %shard_map.313 = (bf16[2,4,2,64,256]{4,3,2,1,0:T(8,128)(2,1)S(1)}, f32[4,2,2,64,768]{4,3,2,1,0:T(8,128)S(1)}, bf16[4,2,2,128,128]{4,3,2,1,0:T(8,128)(2,1)S(1)}, ...) custom-call(s32[1]{0:T(128)} %bitcast.24.me_ref, ...), custom_call_target="tpu_custom_call" | custom-call | flops 1207959552 | bytes 12582912 | tf_op jit(solution)/shard_map/pallas_call | solution.py:619
  182.3 7.4 %collective-permute-done.18 = bf16[2,64,2048]{2,1,0:T(8,128)(2,1)} collective-permute-done((bf16[2,64,2048]{2,1,0:T(8,128)(2,1)}, bf16[2,64,2048]{2,1,0:T(8,128)(2,1)}, u32[]{:S(2)}, u32[]{:S(2)}) %collective-permute-start.18) | collective-permute-done | bytes 524320 | tf_op jit(solution)/shard_map/ppermute | solution.py:46
  212.8 5.7 collective-permute-done.22
  233.0 10.6 %fusion.49 = f32[1024,1408]{1,0:T(8,128)S(1)} fusion(bf16[1024,2048]{1,0:T(8,128)(2,1)} %bitcast.60, bf16[2048,1408]{1,0:T(8,128)(2,1)} %all-gather.11.cloned.1.call-done), kind=kOutput, calls=%fused_computation.294 | convolution fusion | flops 5905580032 | bytes 15728640 | tf_op jit(solution)/shard_map/dot_general | solution.py:26
  253.4 38.5 %all-gather.9.cloned.1.call-done = bf16[704,2048]{1,0:T(8,128)(2,1)} async-done(((bf16[176,2048]{1,0:T(8,128)(2,1)}), bf16[704,2048]{1,0:T(8,128)(2,1)}) %all-gather.9.cloned.1.call-update) | async-done | bytes 2883600 | tf_op jit(solution)/shard_map/all_gather | solution.py:748
  291.9 10.9 %multiply_convert_fusion.3 = (bf16[1024,704]{1,0:T(8,128)(2,1)}, bf16[1024,704]{1,0:T(8,128)(2,1)}) fusion(f32[1024,1408]{1,0:T(8,128)} %copy-done.36, bf16[1024,2048]{1,0:T(8,128)(2,1)} %bitcast.407, bf16[704,2048]{1,0:T(8,128)(2,1)} %all-gather.9.cloned.1.call-done), kind=kOutput, calls=%fused_computation.25 | convolution fusion | flops 2962161664 | bytes 15728640 | tf_op jit(solution)/shard_map/dot_general | solution.py:36
  302.9 9.9 %convolution_convert_fusion.2 = bf16[1024,2048]{1,0:T(8,128)(2,1)S(1)} fusion(bf16[2048,1408]{1,0:T(8,128)(2,1)} %all-gather.11.cloned.1.call-done, bf16[1024,704]{1,0:T(8,128)(2,1)} %get-tuple-element.132, bf16[1024,704]{1,0:T(8,128)(2,1)} %get-tuple-element.131), kind=kOutput, calls=%fused_computation.20 | convolution fusion | flops 5913444352 | bytes 12845056 | tf_op jit(solution)/shard_map/dot_general | solution.py:36
  321.8 12.1 %convolution_convert_fusion = bf16[2048,1408]{1,0:T(8,128)(2,1)} fusion(bf16[1024,2048]{1,0:T(8,128)(2,1)} %bitcast.60, bf16[1024,704]{1,0:T(8,128)(2,1)S(1)} %copy-done.64, bf16[1024,704]{1,0:T(8,128)(2,1)S(1)} %copy-done.63), kind=kOutput, calls=%fused_computation.7 | convolution fusion | flops 5914230784 | bytes 12845056 | tf_op jit(solution)/shard_map/dot_general | solution.py:30
  339.2 11.3 %collective-permute-done.33 = bf16[2,64,2048]{2,1,0:T(8,128)(2,1)S(1)} collective-permute-done((bf16[2,64,2048]{2,1,0:T(8,128)(2,1)S(1)}, bf16[2,64,2048]{2,1,0:T(8,128)(2,1)S(1)}, u32[]{:S(2)}, u32[]{:S(2)}) %collective-permute-start.33) | collective-permute-done | bytes 524320 | tf_op jit(solution)/shard_map/ppermute | solution.py:46
  389.8 24.3 %shard_map.315 = (bf16[2,4,2,64,1024]{4,3,2,1,0:T(8,128)(2,1)S(1)}, bf16[2,4,2,64,128]{4,3,2,1,0:T(8,128)(2,1)S(1)}, f32[4,768]{1,0:T(4,128)S(1)}, f32[8,128]{1,0:T(8,128)S(1)}) custom-call(s32[1]{0:T(128)} %bitcast.24.me_ref, f32[2,4,2,64,1024]{4,3,2,1,0:T(8,128)S(1)} %copy-done.1, f32[2,4,2,64,128]{4,3,2,1,0:T(8,128)S(1)} %copy-done.3, ...), custom_call_target="tpu_custom_call" | custom-call | flops 1207959552 | bytes 12582912 | tf_op jit(solution)/shard_map/pallas_call | solution.py:648
  414.1 6.4 %convolution_convert_fusion.4 = bf16[2048,1024]{0,1:T(8,128)(2,1)} fusion(bf16[1024,2048]{1,0:T(8,128)(2,1)S(1)} %bitcast.377, bf16[1024,1024]{1,0:T(8,128)(2,1)S(1)} %bitcast.361), kind=kOutput, calls=%fused_computation.22 | convolution fusion | flops 4297064448 | bytes 10485760 | tf_op jit(solution)/shard_map/dot_general | solution.py:30
  427.4 6.4 %fusion.50 = f32[1024,2048]{1,0:T(8,128)S(1)} fusion(bf16[1024,1024]{1,0:T(8,128)(2,1)S(1)} %bitcast.362, bf16[2048,1024]{1,0:T(8,128)(2,1)} %all-gather.5.cloned.1.call-done), kind=kOutput, calls=%fused_computation.295 | convolution fusion | flops 4294967296 | bytes 14680064 | tf_op jit(solution)/shard_map/dot_general | solution.py:36
  468.2 7.9 %collective-permute-done.45 = bf16[2,64,2048]{2,1,0:T(8,128)(2,1)S(1)} collective-permute-done((bf16[2,64,2048]{2,1,0:T(8,128)(2,1)S(1)}, bf16[2,64,2048]{2,1,0:T(8,128)(2,1)S(1)}, u32[]{:S(2)}, u32[]{:S(2)}) %collective-permute-start.45) | collective-permute-done | bytes 524320 | tf_op jit(solution)/shard_map/ppermute | solution.py:46
  481.1 6.3 %collective-permute-done.50 = bf16[2,64,2048]{2,1,0:T(8,128)(2,1)S(1)} collective-permute-done((bf16[2,64,2048]{2,1,0:T(8,128)(2,1)S(1)}, bf16[2,64,2048]{2,1,0:T(8,128)(2,1)S(1)}, u32[]{:S(2)}, u32[]{:S(2)}) %collective-permute-start.50) | collective-permute-done | bytes 524320 | tf_op jit(solution)/shard_map/ppermute | solution.py:46
  506.7 15.2 %all-to-all-done.3.in_ref = bf16[8,64,1408]{2,1,0:T(8,128)(2,1)} async-done(((bf16[8,64,1408]{2,1,0:T(8,128)(2,1)}), bf16[8,64,1408]{2,1,0:T(8,128)(2,1)}, u32[]{:S(2)}, u32[]{:S(2)}) %all-to-all-start.3) | async-done | bytes 1441824 | tf_op jit(solution)/shard_map/all_to_all | solution.py:745
  531.8 9.4 %all-to-all-done.4 = f32[32,1,1408]{2,1,0:T(1,128)S(1)} async-done(((f32[32,1,1408]{2,1,0:T(1,128)}), f32[32,1,1408]{2,1,0:T(1,128)S(1)}, u32[]{:S(2)}, u32[]{:S(2)}) %all-to-all-start.4) | async-done | bytes 180256 | tf_op jit(solution)/shard_map/all_to_all | solution.py:740
  541.2 20.4 %reduce-scatter.4.cloned.1.call-done = bf16[512,1280]{0,1:T(8,128)(2,1)} async-done(((bf16[2048,1280]{0,1:T(8,128)(2,1)}), bf16[512,1280]{0,1:T(8,128)(2,1)}) %reduce-scatter.4.cloned.1.call-update) | async-done | bytes 1310736 | tf_op jit(solution)/shard_map/reduce_scatter | solution.py:853
  573.7 10.2 %all-to-all-done.5 = bf16[8,64,1024]{2,1,0:T(8,128)(2,1)S(1)} async-done(((bf16[8,64,1024]{2,1,0:T(8,128)(2,1)}), bf16[8,64,1024]{2,1,0:T(8,128)(2,1)S(1)}, u32[]{:S(2)}, u32[]{:S(2)}) %all-to-all-start.5) | async-done | bytes 1048608 | tf_op jit(solution)/shard_map/all_to_all | solution.py:745
  (550 shorter events, 274.4 us)
Async XLA Ops:
  7.2 111.2 %all-gather.7.cloned.1.call-start = ((), (), s32[]{:S(2)}) async-start(), calls=%async_computation.10 | async-start | bytes 1310720 | tf_op jit(solution)/shard_map/all_gather | solution.py:748
  7.9 118.3 %all-gather.5.cloned.1.call-start = ((), (), s32[]{:S(2)}) async-start(), calls=%async_computation.9 | async-start | bytes 5242880 | tf_op jit(solution)/shard_map/all_gather | solution.py:748
  33.8 199.2 %all-gather.11.cloned.1.call-start = ((), (), s32[]{:S(2)}) async-start(), calls=%async_computation.12 | async-start | bytes 7208960 | tf_op jit(solution)/shard_map/all_gather | solution.py:748
  61.1 230.8 %all-gather.9.cloned.1.call-start = ((), (), s32[]{:S(2)}) async-start(), calls=%async_computation.11 | async-start | bytes 3604480 | tf_op jit(solution)/shard_map/all_gather | solution.py:748
  62.3 32.5 %collective-permute-start.4 = (bf16[128,2048]{1,0:T(8,128)(2,1)S(1)}, bf16[128,2048]{1,0:T(8,128)(2,1)S(1)}, u32[]{:S(2)}, u32[]{:S(2)}) collective-permute-start(bf16[128,2048]{1,0:T(8,128)(2,1)S(1)} %bitcast.366), channel_id=1, source_target_pairs={{0,1},{1,0},{2,3},{3,2},{4,5},{5,4},{6,7},{7,6},{8,9},{9,8},{10,11... | collective-permute-start | bytes 1572872 | tf_op jit(solution)/shard_map/ppermute | solution.py:46
  62.3 25.0 %collective-permute-start.9 = (bf16[128,2048]{1,0:T(8,128)(2,1)}, bf16[128,2048]{1,0:T(8,128)(2,1)}, u32[]{:S(2)}, u32[]{:S(2)}) collective-permute-start(bf16[128,2048]{1,0:T(8,128)(2,1)} %bitcast.32), channel_id=1, source_target_pairs={{0,2},{1,3},{2,0},{3,1},{4,6},{5,7},{6,4},{7,5},{8,10},{9,11},{10,... | collective-permute-start | bytes 1572872 | tf_op jit(solution)/shard_map/ppermute | solution.py:46
  63.8 25.3 %collective-permute-start.10 = (bf16[128,2048]{1,0:T(8,128)(2,1)}, bf16[128,2048]{1,0:T(8,128)(2,1)S(1)}, u32[]{:S(2)}, u32[]{:S(2)}) collective-permute-start(bf16[128,2048]{1,0:T(8,128)(2,1)} %bitcast.32), channel_id=1, source_target_pairs={{0,4},{1,5},{2,6},{3,7},{4,0},{5,1},{6,2},{7,3},{8,12},{9,13},{10,... | collective-permute-start | bytes 1572872 | tf_op jit(solution)/shard_map/ppermute | solution.py:46
  87.4 82.8 %collective-permute-start.13 = (bf16[128,2048]{1,0:T(8,128)(2,1)}, bf16[128,2048]{1,0:T(8,128)(2,1)}, u32[]{:S(2)}, u32[]{:S(2)}) collective-permute-start(bf16[128,2048]{1,0:T(8,128)(2,1)} %bitcast.32), channel_id=1, source_target_pairs={{0,1},{1,0},{2,3},{3,2},{4,5},{5,4},{6,7},{7,6},{8,9},{9,8},{10,11... | collective-permute-start | bytes 1572872 | tf_op jit(solution)/shard_map/ppermute | solution.py:46
  89.1 76.3 %collective-permute-start.11 = (bf16[64,2048]{1,0:T(8,128)(2,1)}, bf16[64,2048]{1,0:T(8,128)(2,1)S(1)}, u32[]{:S(2)}, u32[]{:S(2)}) collective-permute-start(bf16[64,2048]{1,0:T(8,128)(2,1)} %slice.826), channel_id=1, source_target_pairs={{0,4},{1,5},{2,6},{3,7},{4,0},{5,1},{6,2},{7,3},{8,12},{9,13},{10,... | collective-permute-start | bytes 786440 | tf_op jit(solution)/shard_map/ppermute | solution.py:46
  91.9 74.7 %collective-permute-start.12 = (bf16[64,2048]{1,0:T(8,128)(2,1)}, bf16[64,2048]{1,0:T(8,128)(2,1)}, u32[]{:S(2)}, u32[]{:S(2)}) collective-permute-start(bf16[64,2048]{1,0:T(8,128)(2,1)} %slice.827), channel_id=1, source_target_pairs={{0,2},{1,3},{2,0},{3,1},{4,6},{5,7},{6,4},{7,5},{8,10},{9,11},{10,... | collective-permute-start | bytes 786440 | tf_op jit(solution)/shard_map/ppermute | solution.py:46
  99.5 17.6 %all-to-all-start.1 = ((bf16[32,2,1472]{2,1,0:T(2,128)(2,1)}), bf16[32,2,1472]{2,1,0:T(2,128)(2,1)S(1)}, u32[]{:S(2)}, u32[]{:S(2)}) async-start(bf16[32,2,1472]{2,1,0:T(2,128)(2,1)} %reshape.834), calls=%async_computation.1 | async-start | bytes 393216 | tf_op jit(solution)/shard_map/all_to_all | solution.py:740
  103.5 352.3 %reduce-scatter.8.cloned.1.call-start = ((), (), s32[]{:S(2)}) async-start(), calls=%async_computation.15 | async-start | bytes 3604480 | tf_op jit(solution)/shard_map/reduce_scatter | solution.py:853
  105.7 70.8 %collective-permute-start.14 = (bf16[128,2048]{1,0:T(8,128)(2,1)}, bf16[128,2048]{1,0:T(8,128)(2,1)}, u32[]{:S(2)}, u32[]{:S(2)}) collective-permute-start(bf16[128,2048]{1,0:T(8,128)(2,1)} %collective-permute-done.9), channel_id=1, source_target_pairs={{0,1},{1,0},{2,3},{3,2},{4,5},{5,4},{6,7},{7,6},{8,9},{9,8},{10,11... | collective-permute-start | bytes 1572872 | tf_op jit(solution)/shard_map/ppermute | solution.py:46
  168.3 40.3 %collective-permute-start.16 = (bf16[128,2048]{1,0:T(8,128)(2,1)}, bf16[128,2048]{1,0:T(8,128)(2,1)}, u32[]{:S(2)}, u32[]{:S(2)}) collective-permute-start(bf16[128,2048]{1,0:T(8,128)(2,1)} %constant_dynamic-update-slice_fusion.3), channel_id=1, source_target_pairs={{0,1},{1,0},{2,3},{3,2},{4,5},{5,4},{6,7},{7,6},{8,9},{9,8},{10,11... | collective-permute-start | bytes 1572872 | tf_op jit(solution)/shard_map/ppermute | solution.py:46
  210.5 17.7 %collective-permute-start.26 = (bf16[128,2048]{1,0:T(8,128)(2,1)S(1)}, bf16[128,2048]{1,0:T(8,128)(2,1)S(1)}, u32[]{:S(2)}, u32[]{:S(2)}) collective-permute-start(bf16[128,2048]{1,0:T(8,128)(2,1)S(1)} %multiply_convert_fusion.7), channel_id=1, source_target_pairs={{0,1},{1,0},{2,3},{3,2},{4,5},{5,4},{6,7},{7,6},{8,9},{9,8},{10,11... | collective-permute-start | bytes 1572872 | tf_op jit(solution)/shard_map/ppermute | solution.py:46
  302.8 195.2 %reduce-scatter.6.cloned.1.call-start = ((), (), s32[]{:S(2)}) async-start(), calls=%async_computation.14 | async-start | bytes 7208960 | tf_op jit(solution)/shard_map/reduce_scatter | solution.py:853
  334.0 227.7 %reduce-scatter.4.cloned.1.call-start = ((), (), s32[]{:S(2)}) async-start(), calls=%async_computation.13 | async-start | bytes 6553600 | tf_op jit(solution)/shard_map/reduce_scatter | solution.py:853
  386.5 34.1 %collective-permute-start.43 = (bf16[128,2048]{1,0:T(8,128)(2,1)S(1)}, bf16[128,2048]{1,0:T(8,128)(2,1)S(1)}, u32[]{:S(2)}, u32[]{:S(2)}) collective-permute-start(bf16[128,2048]{1,0:T(8,128)(2,1)S(1)} %dynamic-slice_bitcast_fusion), channel_id=1, source_target_pairs={{0,1},{1,0},{2,3},{3,2},{4,5},{5,4},{6,7},{7,6},{8,9},{9,8},{10,11... | collective-permute-start | bytes 1572872 | tf_op jit(solution)/shard_map/ppermute | solution.py:46
  437.8 20.4 %collective-permute-start.44 = (bf16[4,128,2048]{2,1,0:T(8,128)(2,1)}, bf16[4,128,2048]{2,1,0:T(8,128)(2,1)}, u32[]{:S(2)}, u32[]{:S(2)}) collective-permute-start(bf16[4,128,2048]{2,1,0:T(8,128)(2,1)} %bitcast.94), channel_id=1, source_target_pairs={{0,1},{1,0},{2,3},{3,2},{4,5},{5,4},{6,7},{7,6},{8,9},{9,8},{10,11... | collective-permute-start | bytes 6291464 | tf_op jit(solution)/shard_map/ppermute | solution.py:46
  465.6 21.8 %collective-permute-start.50 = (bf16[2,64,2048]{2,1,0:T(8,128)(2,1)S(1)}, bf16[2,64,2048]{2,1,0:T(8,128)(2,1)S(1)}, u32[]{:S(2)}, u32[]{:S(2)}) collective-permute-start(bf16[2,64,2048]{2,1,0:T(8,128)(2,1)S(1)} %slice.864), channel_id=1, source_target_pairs={{0,4},{1,5},{2,6},{3,7},{4,0},{5,1},{6,2},{7,3},{8,12},{9,13},{10,... | collective-permute-start | bytes 1572872 | tf_op jit(solution)/shard_map/ppermute | solution.py:46
  466.3 24.3 %collective-permute-start.52 = (bf16[2,64,2048]{2,1,0:T(8,128)(2,1)S(1)}, bf16[2,64,2048]{2,1,0:T(8,128)(2,1)S(1)}, u32[]{:S(2)}, u32[]{:S(2)}) collective-permute-start(bf16[2,64,2048]{2,1,0:T(8,128)(2,1)S(1)} %slice.712), channel_id=1, source_target_pairs={{0,2},{1,3},{2,0},{3,1},{4,6},{5,7},{6,4},{7,5},{8,10},{9,11},{10,... | collective-permute-start | bytes 1572872 | tf_op jit(solution)/shard_map/ppermute | solution.py:46
  476.3 19.9 %collective-permute-start.46 = (bf16[64,2048]{1,0:T(8,128)(2,1)S(1)}, bf16[64,2048]{1,0:T(8,128)(2,1)S(1)}, u32[]{:S(2)}, u32[]{:S(2)}) collective-permute-start(bf16[64,2048]{1,0:T(8,128)(2,1)S(1)} %slice_bitcast_fusion.6), channel_id=1, source_target_pairs={{0,2},{1,3},{2,0},{3,1},{4,6},{5,7},{6,4},{7,5},{8,10},{9,11},{10,... | collective-permute-start | bytes 786440 | tf_op jit(solution)/shard_map/ppermute | solution.py:46
  498.0 23.9 %all-to-all-start.3 = ((bf16[8,64,1408]{2,1,0:T(8,128)(2,1)}), bf16[8,64,1408]{2,1,0:T(8,128)(2,1)}, u32[]{:S(2)}, u32[]{:S(2)}) async-start(bf16[8,64,1408]{2,1,0:T(8,128)(2,1)} %bitcast.387), calls=%async_computation.5 | async-start | bytes 2883584 | tf_op jit(solution)/shard_map/all_to_all | solution.py:745
  564.8 19.1 %all-to-all-start.5 = ((bf16[8,64,1024]{2,1,0:T(8,128)(2,1)}), bf16[8,64,1024]{2,1,0:T(8,128)(2,1)S(1)}, u32[]{:S(2)}, u32[]{:S(2)}) async-start(bf16[8,64,1024]{2,1,0:T(8,128)(2,1)} %bitcast.115), calls=%async_computation.8 | async-start | bytes 2097152 | tf_op jit(solution)/shard_map/all_to_all | solution.py:745
  (106 other events, 1050.4 us)
Sparse Core Ops, SparseCore 0:
  9.6 30.6 all-gather.6
  41.8 84.3 all-gather.4
  127.8 105.1 all-gather.10
  234.4 57.4 all-gather.8
  302.9 54.8 reduce-scatter.7
  360.0 102.0 reduce-scatter.5
  464.4 97.1 reduce-scatter.3

commit v2 on v1

--- a/solution.py
+++ b/solution.py
@@ -111,6 +111,13 @@
         (dims, ((), ())),
         preferred_element_type=jnp.float32,
     )
+
+
+def split_dot(left_side, right_side, dims, exact_left):
+    whole = right_side if exact_left else left_side
+    high = rounded(whole)
+    parts = [(left_side, part) if exact_left else (part, right_side) for part in (high, whole - high)]
+    return low_dot(*parts[0], dims) + low_dot(*parts[1], dims)
 
 
 def rounded(value):
@@ -461,8 +468,8 @@
                 for which in range(PAIR)
             ]
         )
-        grad_cumulative = grad_cumulative + ends - low_dot(shifts, ones, TN)
-        grad_decay = rounded(low_dot(within, grad_cumulative, TN))
+        grad_cumulative = grad_cumulative + ends - split_dot(shifts, ones, TN, False)
+        grad_decay = rounded(split_dot(within, grad_cumulative, TN, True))
         both = stack([grad_scores, grad_key_key]).astype(bf16)
         down = low_dot(both, key, NN)
         grad_query = growth * made["grad_query_grown"] + down[: PAIR * BLOCK]
@@ -841,7 +848,7 @@
     silu_gate = gate_pre * sigmoid_gate
     activ = (silu_gate * up_proj).astype(bf16)
     down_grads = contract_rows(activ, seed_all).astype(bf16)
-    down_full, down_grads = lax.optimization_barrier((down_full, down_grads))
+    down_full = after(down_full, down_grads)
     from_down = times_transposed(seed_all, down_full)
     grad_gate = from_down * up_proj * sigmoid_gate * (1.0 + gate_pre * (1.0 - sigmoid_gate))
     grad_gate_up = jnp.concatenate([grad_gate, from_down * silu_gate], axis=1).astype(bf16)
@@ -874,12 +881,13 @@
     grad_rate, grad_bias = grad_small[1, :mine], grad_small[2, :mine]
     grad_output = from_heads(contract_rows(mixed, grad_mixer_out).astype(bf16))
     weight_grads = contract_rows(hidden_in, grad_projected).astype(bf16)
-    weight_grads = jnp.concatenate([weight_grads, grad_output.reshape(width, -1)], axis=1)
     weight_grads, grad_projected, grad_extra, activ = lax.optimization_barrier(
         (weight_grads, grad_projected, grad_extra, activ)
     )
     mixer_own = scatter_dp(weight_grads)
     back_in = times_transposed(grad_projected, mixer_full) + product(grad_extra, gates)
+    grad_output, back_in = lax.optimization_barrier((grad_output, back_in))
+    grad_output = scatter_dp(grad_output.reshape(n_dp * rows, width))
     back_in = scatter_seq(shares(back_in))
     grad_gate_up_own = exchange(grad_gate_up_own.reshape(n_seq, rows, -1))
     output_own = residual + scatter_seq(shares(product(activ, down_full)))
@@ -925,8 +933,9 @@
     )
     mixer_own, *done = lax.optimization_barrier((mixer_own, *done))
     swapped, grad_w_gate, grad_w_up, grad_down, output_own, input_grad = done
-    grad_output = mixer_own[:, 4 * cols :].reshape(rows, width).astype(f32)
-    mixer_own = exchange(mixer_own[:, : 4 * cols].reshape(n_seq, rows, -1))
+    mixer_own = exchange(mixer_own.reshape(n_seq, rows, -1))
+    grad_output, mixer_own = lax.optimization_barrier((grad_output, mixer_own))
+    grad_output = grad_output.astype(f32)
     sums = jnp.sum(swapped, axis=0)
     gate_sums = jnp.sum(swapped[:, : edges[1]].reshape(n_dp, n_seq, -1), axis=0)
     gate_sums = gate_sums.reshape(bands, group, 2, mine, rows)

time: 605 us -> 588 us (0.972)
  other arithmetic: 61.5 us -> 53.1 us
  waiting for transfers between devices: 207 us -> 199 us
    all_to_all x2, waiting for transfers between devices: 25.4 us -> 0.01 us  [exchange(): lax.all_to_all(blocks, 'seq', split_axis=0, concat_axis=0, tiled=True)]
    ppermute x54, waiting for transfers between devices: 101 us -> 116 us  [swap(): lax.ppermute(value, 'seq', [(place, place ^ bit) for place in range(count)])]
    unnamed x224 -> x220, local copies, waits for them, and re-layouts: 41.8 us -> 45.8 us
    reduce_scatter x3 -> x4, waiting for transfers between devices: 20.4 us -> 21.4 us  [scatter_dp(): lax.psum_scatter(value.astype(bf16), 'dp', scatter_dimension=0, tiled=True)]
  transfers between devices with their start and end apart: 65 -> 66, of which waited for: 33 -> 28; matrix products, arithmetic and copies ran while one was open for 34% -> 34% of each run, Pallas kernels for 7% -> 8%
where the time goes in v2:
time: 588 us; the launch traced here: 578 us
  waiting for transfers between devices  199 us (34%)
  matrix products  85.9 us (15%)
  local copies, waits for them, and re-layouts  79.3 us (13%)
  starting transfers between devices  55.5 us (9%)
  other arithmetic  53.1 us (9%)
  Pallas kernels  44.6 us (8%)
  blocking collectives  44.3 us (8%)
  between operations  16.5 us (3%)
    ppermute x54, waiting for transfers between devices, swap(): lax.ppermute(value, 'seq', [(place, place ^ bit) for place in range(count)])  116 us
    unnamed x220, local copies, waits for them, and re-layouts  45.8 us
    all_to_all x2, blocking collectives, exchange(): lax.all_to_all(blocks, 'seq', split_axis=0, concat_axis=0, tiled=True)  44.3 us
    all_gather x4, waiting for transfers between devices, gather_dp(): return lax.all_gather(block, 'dp', axis=0, tiled=True)  41.9 us
    ppermute x54, starting transfers between devices, swap(): lax.ppermute(value, 'seq', [(place, place ^ bit) for place in range(count)])  41 us
    dot_general x5, matrix products, contract_rows(): lax.dot_general(left_side, right_side, (((0,), (0,)), ((), ())), preferre...  29.4 us
    dot_general x5, matrix products, times_transposed(): lax.dot_general(left_side, right_side, (((1,), (1,)), ((), ())), preferre...  28.5 us
    dot_general x5, matrix products, product(): return jnp.dot(left_side, right_side, preferred_element_type=jnp.float32)  28 us
  transfers between devices with their start and end apart: 66, of which 28 were waited for; matrix products, arithmetic and copies ran while one was open for 34% of the time, Pallas kernels for 8%

profile of v2, /device:TPU:0, one launch (start us, length us, event | category | flops | bytes accessed | tf_op | source)
XLA Modules:
  0.0 578.3 jit_solution(9836599283803634677)
XLA Ops:
  13.3 20.4 %all_to_all.41 = bf16[8,64,1024]{2,1,0:T(8,128)(2,1)} all-to-all(bf16[8,64,1024]{2,1,0:T(8,128)(2,1)S(1)} %pad_maximum_fusion.3), channel_id=1, replica_groups=mesh['dp'=4,'seq'=8] {'seq'}, dimensions={0} | all-to-all | bytes 2097152 | tf_op jit(solution)/shard_map/all_to_all | solution.py:752
  37.2 23.8 %all_to_all.42 = bf16[8,64,1408]{2,1,0:T(8,128)(2,1)} all-to-all(bf16[8,64,1408]{2,1,0:T(8,128)(2,1)} %shard_map.314), channel_id=1, replica_groups=mesh['dp'=4,'seq'=8] {'seq'}, dimensions={0} | all-to-all | bytes 2883584 | tf_op jit(solution)/shard_map/all_to_all | solution.py:752
  68.6 7.4 %collective-permute-done = bf16[128,2048]{1,0:T(8,128)(2,1)S(1)} collective-permute-done((bf16[128,2048]{1,0:T(8,128)(2,1)S(1)}, bf16[128,2048]{1,0:T(8,128)(2,1)S(1)}, u32[]{:S(2)}, u32[]{:S(2)}) %collective-permute-start) | collective-permute-done | bytes 524320 | tf_op jit(solution)/shard_map/ppermute | solution.py:46
  79.8 7.5 %collective-permute-done.9 = bf16[128,2048]{1,0:T(8,128)(2,1)} collective-permute-done((bf16[128,2048]{1,0:T(8,128)(2,1)}, bf16[128,2048]{1,0:T(8,128)(2,1)}, u32[]{:S(2)}, u32[]{:S(2)}) %collective-permute-start.9) | collective-permute-done | bytes 524320 | tf_op jit(solution)/shard_map/ppermute | solution.py:46
  107.9 9.3 %all-to-all-done.1 = bf16[32,2,1472]{2,1,0:T(2,128)(2,1)S(1)} async-done(((bf16[32,2,1472]{2,1,0:T(2,128)(2,1)}), bf16[32,2,1472]{2,1,0:T(2,128)(2,1)S(1)}, u32[]{:S(2)}, u32[]{:S(2)}) %all-to-all-start.1) | async-done | bytes 188448 | tf_op jit(solution)/shard_map/all_to_all | solution.py:747
  131.6 9.0 %fusion.6.proj_ref = f32[2,4,2,64,1024]{4,3,2,1,0:T(8,128)} fusion(bf16[2048,1024]{1,0:T(8,128)(2,1)S(1)} %copy-done.60, f32[2048]{0:T(1024)S(1)} %reshape.801, f32[2,4,2,64]{3,2,1,0:T(2,128)S(1)} %rsqrt.40, bf16[2,4,2,64,2048]{4,3,2,1,0:T(8,128)(2,1)} %bitcast.321), kind=kOutput, calls=%fused_computation.16 | convolution fusion | flops 4303355904 | bytes 12595200 | tf_op jit(solution)/shard_map/dot_general | solution.py:26
  144.2 14.0 %shard_map.313 = (bf16[2,4,2,64,256]{4,3,2,1,0:T(8,128)(2,1)S(1)}, f32[4,2,2,64,768]{4,3,2,1,0:T(8,128)S(1)}, bf16[4,2,2,128,128]{4,3,2,1,0:T(8,128)(2,1)S(1)}, ...) custom-call(s32[1]{0:T(128)} %bitcast.24.me_ref, ...), custom_call_target="tpu_custom_call" | custom-call | flops 1207959552 | bytes 12582912 | tf_op jit(solution)/shard_map/pallas_call | solution.py:626
  181.8 7.5 %collective-permute-done.18 = bf16[2,64,2048]{2,1,0:T(8,128)(2,1)} collective-permute-done((bf16[2,64,2048]{2,1,0:T(8,128)(2,1)}, bf16[2,64,2048]{2,1,0:T(8,128)(2,1)}, u32[]{:S(2)}, u32[]{:S(2)}) %collective-permute-start.18) | collective-permute-done | bytes 524320 | tf_op jit(solution)/shard_map/ppermute | solution.py:46
  212.3 5.7 collective-permute-done.22
  233.0 10.6 %fusion.49 = f32[1024,1408]{1,0:T(8,128)S(1)} fusion(bf16[1024,2048]{1,0:T(8,128)(2,1)} %bitcast.60, bf16[2048,1408]{1,0:T(8,128)(2,1)} %all-gather.11.cloned.1.call-done), kind=kOutput, calls=%fused_computation.292 | convolution fusion | flops 5905580032 | bytes 15728640 | tf_op jit(solution)/shard_map/dot_general | solution.py:26
  253.5 38.5 %all-gather.9.cloned.1.call-done = bf16[704,2048]{1,0:T(8,128)(2,1)} async-done(((bf16[176,2048]{1,0:T(8,128)(2,1)}), bf16[704,2048]{1,0:T(8,128)(2,1)}) %all-gather.9.cloned.1.call-update) | async-done | bytes 2883600 | tf_op jit(solution)/shard_map/all_gather | solution.py:755
  291.9 9.2 %multiply_convert_fusion.3 = (bf16[1024,704]{1,0:T(8,128)(2,1)S(1)}, bf16[1024,704]{1,0:T(8,128)(2,1)S(1)}) fusion(f32[1024,1408]{1,0:T(8,128)} %copy-done.36, bf16[1024,2048]{1,0:T(8,128)(2,1)} %bitcast.409, bf16[704,2048]{1,0:T(8,128)(2,1)} %all-gather.9.cloned.1.call-done), kind=kOutput, calls=%fused_computation.24 | convolution fusion | flops 2962161664 | bytes 15728640 | tf_op jit(solution)/shard_map/dot_general | solution.py:36
  301.1 9.0 %convolution_convert_fusion.2 = bf16[1024,2048]{1,0:T(8,128)(2,1)S(1)} fusion(bf16[2048,1408]{1,0:T(8,128)(2,1)} %all-gather.11.cloned.1.call-done, bf16[1024,704]{1,0:T(8,128)(2,1)S(1)} %get-tuple-element.138, bf16[1024,704]{1,0:T(8,128)(2,1)S(1)} %get-tuple-element.137), kind=kOutput, calls=%fused_computation.19 | convolution fusion | flops 5913444352 | bytes 12845056 | tf_op jit(solution)/shard_map/dot_general | solution.py:36
  312.4 12.1 %convolution_convert_fusion = bf16[2048,1408]{1,0:T(8,128)(2,1)} fusion(bf16[1024,2048]{1,0:T(8,128)(2,1)} %bitcast.60, bf16[1024,704]{1,0:T(8,128)(2,1)S(1)} %get-tuple-element.138, bf16[1024,704]{1,0:T(8,128)(2,1)S(1)} %get-tuple-element.137), kind=kOutput, calls=%fused_computation.6 | convolution fusion | flops 5914230784 | bytes 12845056 | tf_op jit(solution)/shard_map/dot_general | solution.py:30
  331.3 11.2 %collective-permute-done.31 = bf16[2,64,2048]{2,1,0:T(8,128)(2,1)S(1)} collective-permute-done((bf16[2,64,2048]{2,1,0:T(8,128)(2,1)S(1)}, bf16[2,64,2048]{2,1,0:T(8,128)(2,1)S(1)}, u32[]{:S(2)}, u32[]{:S(2)}) %collective-permute-start.31) | collective-permute-done | bytes 524320 | tf_op jit(solution)/shard_map/ppermute | solution.py:46
  364.7 5.3 collective-permute-done.35
  385.1 24.3 %shard_map.315 = (bf16[2,4,2,64,1024]{4,3,2,1,0:T(8,128)(2,1)S(1)}, bf16[2,4,2,64,128]{4,3,2,1,0:T(8,128)(2,1)S(1)}, f32[4,768]{1,0:T(4,128)S(1)}, f32[8,128]{1,0:T(8,128)S(1)}) custom-call(s32[1]{0:T(128)} %bitcast.24.me_ref, f32[2,4,2,64,1024]{4,3,2,1,0:T(8,128)S(1)} %copy-done.1, f32[2,4,2,64,128]{4,3,2,1,0:T(8,128)S(1)} %copy-done.3, ...), custom_call_target="tpu_custom_call" | custom-call | flops 1207959552 | bytes 12582912 | tf_op jit(solution)/shard_map/pallas_call | solution.py:655
  410.9 6.2 %convolution_convert_fusion.4 = bf16[2048,1024]{1,0:T(8,128)(2,1)} fusion(bf16[1024,2048]{1,0:T(8,128)(2,1)S(1)} %bitcast.378, bf16[1024,1024]{1,0:T(8,128)(2,1)S(1)} %bitcast.362), kind=kOutput, calls=%fused_computation.21 | convolution fusion | flops 4297064448 | bytes 10485760 | tf_op jit(solution)/shard_map/dot_general | solution.py:30
  439.5 5.2 fusion.1
  461.5 7.8 %collective-permute-done.50 = bf16[2,64,2048]{2,1,0:T(8,128)(2,1)S(1)} collective-permute-done((bf16[2,64,2048]{2,1,0:T(8,128)(2,1)S(1)}, bf16[2,64,2048]{2,1,0:T(8,128)(2,1)S(1)}, u32[]{:S(2)}, u32[]{:S(2)}) %collective-permute-start.50) | collective-permute-done | bytes 524320 | tf_op jit(solution)/shard_map/ppermute | solution.py:46
  471.7 15.0 %collective-permute-done.51 = bf16[64,2048]{1,0:T(8,128)(2,1)S(1)} collective-permute-done((bf16[64,2048]{1,0:T(8,128)(2,1)S(1)}, bf16[64,2048]{1,0:T(8,128)(2,1)S(1)}, u32[]{:S(2)}, u32[]{:S(2)}) %collective-permute-start.51) | collective-permute-done | bytes 262176 | tf_op jit(solution)/shard_map/ppermute | solution.py:46
  496.8 19.8 %collective-permute-done.48 = bf16[64,2048]{1,0:T(8,128)(2,1)S(1)} collective-permute-done((bf16[64,2048]{1,0:T(8,128)(2,1)S(1)}, bf16[64,2048]{1,0:T(8,128)(2,1)S(1)}, u32[]{:S(2)}, u32[]{:S(2)}) %collective-permute-start.48) | collective-permute-done | bytes 262176 | tf_op jit(solution)/shard_map/ppermute | solution.py:46
  527.8 9.4 %all-to-all-done.4 = f32[32,1,1408]{2,1,0:T(1,128)S(1)} async-done(((f32[32,1,1408]{2,1,0:T(1,128)}), f32[32,1,1408]{2,1,0:T(1,128)S(1)}, u32[]{:S(2)}, u32[]{:S(2)}) %all-to-all-start.4) | async-done | bytes 180256 | tf_op jit(solution)/shard_map/all_to_all | solution.py:747
  544.5 21.4 %reduce-scatter.11.cloned.1.call-done = bf16[64,2048]{1,0:T(8,128)(2,1)} async-done(((bf16[256,2048]{1,0:T(8,128)(2,1)}), bf16[64,2048]{1,0:T(8,128)(2,1)}) %reduce-scatter.11.cloned.1.call-update) | async-done | bytes 262160 | tf_op jit(solution)/shard_map/reduce_scatter | solution.py:860
  (542 shorter events, 252.1 us)
Async XLA Ops:
  7.2 111.1 %all-gather.7.cloned.1.call-start = ((), (), s32[]{:S(2)}) async-start(), calls=%async_computation.11 | async-start | bytes 1310720 | tf_op jit(solution)/shard_map/all_gather | solution.py:755
  7.9 118.3 %all-gather.5.cloned.1.call-start = ((), (), s32[]{:S(2)}) async-start(), calls=%async_computation.10 | async-start | bytes 5242880 | tf_op jit(solution)/shard_map/all_gather | solution.py:755
  33.8 199.2 %all-gather.11.cloned.1.call-start = ((), (), s32[]{:S(2)}) async-start(), calls=%async_computation.13 | async-start | bytes 7208960 | tf_op jit(solution)/shard_map/all_gather | solution.py:755
  61.1 230.8 %all-gather.9.cloned.1.call-start = ((), (), s32[]{:S(2)}) async-start(), calls=%async_computation.12 | async-start | bytes 3604480 | tf_op jit(solution)/shard_map/all_gather | solution.py:755
  62.3 32.5 %collective-permute-start.4 = (bf16[128,2048]{1,0:T(8,128)(2,1)S(1)}, bf16[128,2048]{1,0:T(8,128)(2,1)S(1)}, u32[]{:S(2)}, u32[]{:S(2)}) collective-permute-start(bf16[128,2048]{1,0:T(8,128)(2,1)S(1)} %bitcast.367), channel_id=1, source_target_pairs={{0,1},{1,0},{2,3},{3,2},{4,5},{5,4},{6,7},{7,6},{8,9},{9,8},{10,11... | collective-permute-start | bytes 1572872 | tf_op jit(solution)/shard_map/ppermute | solution.py:46
  62.3 25.0 %collective-permute-start.9 = (bf16[128,2048]{1,0:T(8,128)(2,1)}, bf16[128,2048]{1,0:T(8,128)(2,1)}, u32[]{:S(2)}, u32[]{:S(2)}) collective-permute-start(bf16[128,2048]{1,0:T(8,128)(2,1)} %bitcast.32), channel_id=1, source_target_pairs={{0,2},{1,3},{2,0},{3,1},{4,6},{5,7},{6,4},{7,5},{8,10},{9,11},{10,... | collective-permute-start | bytes 1572872 | tf_op jit(solution)/shard_map/ppermute | solution.py:46
  63.8 25.3 %collective-permute-start.10 = (bf16[128,2048]{1,0:T(8,128)(2,1)}, bf16[128,2048]{1,0:T(8,128)(2,1)S(1)}, u32[]{:S(2)}, u32[]{:S(2)}) collective-permute-start(bf16[128,2048]{1,0:T(8,128)(2,1)} %bitcast.32), channel_id=1, source_target_pairs={{0,4},{1,5},{2,6},{3,7},{4,0},{5,1},{6,2},{7,3},{8,12},{9,13},{10,... | collective-permute-start | bytes 1572872 | tf_op jit(solution)/shard_map/ppermute | solution.py:46
  87.4 82.5 %collective-permute-start.13 = (bf16[128,2048]{1,0:T(8,128)(2,1)}, bf16[128,2048]{1,0:T(8,128)(2,1)}, u32[]{:S(2)}, u32[]{:S(2)}) collective-permute-start(bf16[128,2048]{1,0:T(8,128)(2,1)} %bitcast.32), channel_id=1, source_target_pairs={{0,1},{1,0},{2,3},{3,2},{4,5},{5,4},{6,7},{7,6},{8,9},{9,8},{10,11... | collective-permute-start | bytes 1572872 | tf_op jit(solution)/shard_map/ppermute | solution.py:46
  89.0 76.0 %collective-permute-start.11 = (bf16[64,2048]{1,0:T(8,128)(2,1)}, bf16[64,2048]{1,0:T(8,128)(2,1)S(1)}, u32[]{:S(2)}, u32[]{:S(2)}) collective-permute-start(bf16[64,2048]{1,0:T(8,128)(2,1)} %slice.818), channel_id=1, source_target_pairs={{0,4},{1,5},{2,6},{3,7},{4,0},{5,1},{6,2},{7,3},{8,12},{9,13},{10,... | collective-permute-start | bytes 786440 | tf_op jit(solution)/shard_map/ppermute | solution.py:46
  91.9 74.4 %collective-permute-start.12 = (bf16[64,2048]{1,0:T(8,128)(2,1)}, bf16[64,2048]{1,0:T(8,128)(2,1)}, u32[]{:S(2)}, u32[]{:S(2)}) collective-permute-start(bf16[64,2048]{1,0:T(8,128)(2,1)} %slice.819), channel_id=1, source_target_pairs={{0,2},{1,3},{2,0},{3,1},{4,6},{5,7},{6,4},{7,5},{8,10},{9,11},{10,... | collective-permute-start | bytes 786440 | tf_op jit(solution)/shard_map/ppermute | solution.py:46
  99.5 17.6 %all-to-all-start.1 = ((bf16[32,2,1472]{2,1,0:T(2,128)(2,1)}), bf16[32,2,1472]{2,1,0:T(2,128)(2,1)S(1)}, u32[]{:S(2)}, u32[]{:S(2)}) async-start(bf16[32,2,1472]{2,1,0:T(2,128)(2,1)} %reshape.830), calls=%async_computation.1 | async-start | bytes 393216 | tf_op jit(solution)/shard_map/all_to_all | solution.py:747
  103.5 345.9 %reduce-scatter.9.cloned.1.call-start = ((), (), s32[]{:S(2)}) async-start(), calls=%async_computation.16 | async-start | bytes 3604480 | tf_op jit(solution)/shard_map/reduce_scatter | solution.py:860
  105.7 70.4 %collective-permute-start.14 = (bf16[128,2048]{1,0:T(8,128)(2,1)}, bf16[128,2048]{1,0:T(8,128)(2,1)}, u32[]{:S(2)}, u32[]{:S(2)}) collective-permute-start(bf16[128,2048]{1,0:T(8,128)(2,1)} %collective-permute-done.9), channel_id=1, source_target_pairs={{0,1},{1,0},{2,3},{3,2},{4,5},{5,4},{6,7},{7,6},{8,9},{9,8},{10,11... | collective-permute-start | bytes 1572872 | tf_op jit(solution)/shard_map/ppermute | solution.py:46
  168.0 40.1 %collective-permute-start.16 = (bf16[128,2048]{1,0:T(8,128)(2,1)}, bf16[128,2048]{1,0:T(8,128)(2,1)}, u32[]{:S(2)}, u32[]{:S(2)}) collective-permute-start(bf16[128,2048]{1,0:T(8,128)(2,1)} %constant_dynamic-update-slice_fusion.3), channel_id=1, source_target_pairs={{0,1},{1,0},{2,3},{3,2},{4,5},{5,4},{6,7},{7,6},{8,9},{9,8},{10,11... | collective-permute-start | bytes 1572872 | tf_op jit(solution)/shard_map/ppermute | solution.py:46
  210.0 17.7 %collective-permute-start.26 = (bf16[128,2048]{1,0:T(8,128)(2,1)S(1)}, bf16[128,2048]{1,0:T(8,128)(2,1)S(1)}, u32[]{:S(2)}, u32[]{:S(2)}) collective-permute-start(bf16[128,2048]{1,0:T(8,128)(2,1)S(1)} %multiply_convert_fusion.7), channel_id=1, source_target_pairs={{0,1},{1,0},{2,3},{3,2},{4,5},{5,4},{6,7},{7,6},{8,9},{9,8},{10,11... | collective-permute-start | bytes 1572872 | tf_op jit(solution)/shard_map/ppermute | solution.py:46
  253.4 235.3 %reduce-scatter.7.cloned.1.call-start = ((), (), s32[]{:S(2)}) async-start(), calls=%async_computation.15 | async-start | bytes 7208960 | tf_op jit(solution)/shard_map/reduce_scatter | solution.py:860
  324.5 212.7 %reduce-scatter.5.cloned.1.call-start = ((), (), s32[]{:S(2)}) async-start(), calls=%async_computation.14 | async-start | bytes 5242880 | tf_op jit(solution)/shard_map/reduce_scatter | solution.py:860
  417.1 148.7 %reduce-scatter.11.cloned.1.call-start = ((), (), s32[]{:S(2)}) async-start(), calls=%async_computation.17 | async-start | bytes 1310720 | tf_op jit(solution)/shard_map/reduce_scatter | solution.py:860
  427.7 24.1 %collective-permute-start.49 = (bf16[4,128,2048]{2,1,0:T(8,128)(2,1)}, bf16[4,128,2048]{2,1,0:T(8,128)(2,1)}, u32[]{:S(2)}, u32[]{:S(2)}) collective-permute-start(bf16[4,128,2048]{2,1,0:T(8,128)(2,1)} %bitcast.108), channel_id=1, source_target_pairs={{0,1},{1,0},{2,3},{3,2},{4,5},{5,4},{6,7},{7,6},{8,9},{9,8},{10,11... | collective-permute-start | bytes 6291464 | tf_op jit(solution)/shard_map/ppermute | solution.py:46
  459.1 28.8 %collective-permute-start.45 = (bf16[2,64,2048]{2,1,0:T(8,128)(2,1)S(1)}, bf16[2,64,2048]{2,1,0:T(8,128)(2,1)S(1)}, u32[]{:S(2)}, u32[]{:S(2)}) collective-permute-start(bf16[2,64,2048]{2,1,0:T(8,128)(2,1)S(1)} %slice.847), channel_id=1, source_target_pairs={{0,4},{1,5},{2,6},{3,7},{4,0},{5,1},{6,2},{7,3},{8,12},{9,13},{10,... | collective-permute-start | bytes 1572872 | tf_op jit(solution)/shard_map/ppermute | solution.py:46
  460.8 27.8 %collective-permute-start.47 = (bf16[2,64,2048]{2,1,0:T(8,128)(2,1)S(1)}, bf16[2,64,2048]{2,1,0:T(8,128)(2,1)S(1)}, u32[]{:S(2)}, u32[]{:S(2)}) collective-permute-start(bf16[2,64,2048]{2,1,0:T(8,128)(2,1)S(1)} %slice.691), channel_id=1, source_target_pairs={{0,2},{1,3},{2,0},{3,1},{4,6},{5,7},{6,4},{7,5},{8,10},{9,11},{10,... | collective-permute-start | bytes 1572872 | tf_op jit(solution)/shard_map/ppermute | solution.py:46
  488.8 28.0 %all-to-all-start.3 = ((bf16[8,64,1408]{2,1,0:T(8,128)(2,1)}), bf16[8,64,1408]{2,1,0:T(8,128)(2,1)S(1)}, u32[]{:S(2)}, u32[]{:S(2)}) async-start(bf16[8,64,1408]{2,1,0:T(8,128)(2,1)} %bitcast.388), calls=%async_computation.5 | async-start | bytes 2883584 | tf_op jit(solution)/shard_map/all_to_all | solution.py:752
  492.4 24.2 %collective-permute-start.48 = (bf16[64,2048]{1,0:T(8,128)(2,1)S(1)}, bf16[64,2048]{1,0:T(8,128)(2,1)S(1)}, u32[]{:S(2)}, u32[]{:S(2)}) collective-permute-start(bf16[64,2048]{1,0:T(8,128)(2,1)S(1)} %slice_bitcast_fusion.4), channel_id=1, source_target_pairs={{0,4},{1,5},{2,6},{3,7},{4,0},{5,1},{6,2},{7,3},{8,12},{9,13},{10,... | collective-permute-start | bytes 786440 | tf_op jit(solution)/shard_map/ppermute | solution.py:46
  537.2 28.6 %all-to-all-start.5 = ((bf16[8,64,1024]{2,1,0:T(8,128)(2,1)}), bf16[8,64,1024]{2,1,0:T(8,128)(2,1)S(1)}, u32[]{:S(2)}, u32[]{:S(2)}) async-start(bf16[8,64,1024]{2,1,0:T(8,128)(2,1)} %bitcast.389), calls=%async_computation.9 | async-start | bytes 2097152 | tf_op jit(solution)/shard_map/all_to_all | solution.py:752
  (105 other events, 1011.6 us)
Sparse Core Ops, SparseCore 0:
  9.6 30.6 all-gather.6
  41.8 84.3 all-gather.4
  127.8 105.1 all-gather.10
  234.4 57.4 all-gather.8
  294.1 54.8 reduce-scatter.8
  351.1 102.1 reduce-scatter.6
  455.6 78.5 reduce-scatter.4
  536.6 29.2 reduce-scatter.10

commit v3 on v2

--- a/solution.py
+++ b/solution.py
@@ -113,11 +113,22 @@
     )
 
 
-def split_dot(left_side, right_side, dims, exact_left):
-    whole = right_side if exact_left else left_side
-    high = rounded(whole)
-    parts = [(left_side, part) if exact_left else (part, right_side) for part in (high, whole - high)]
-    return low_dot(*parts[0], dims) + low_dot(*parts[1], dims)
+def two_terms(value):
+    bf16 = jnp.bfloat16
+    if value.dtype == bf16:
+        return [value]
+    high = value.astype(bf16)
+    return [high, (value - high.astype(jnp.float32)).astype(bf16)]
+
+
+def wide_dot(left_side, right_side, dims):
+    left_terms, right_terms = two_terms(left_side), two_terms(right_side)
+    result = low_dot(left_terms[0], right_terms[0], dims)
+    for term in right_terms[1:]:
+        result = result + low_dot(left_terms[0], term, dims)
+    for term in left_terms[1:]:
+        result = result + low_dot(term, right_terms[0], dims)
+    return result
 
 
 def rounded(value):
@@ -149,7 +160,7 @@
     mask_ref[1] = jnp.where(apart == 0, 1.0, 0.0)
     for level in range(level_ref.shape[0]):
         inside = (apart >= 1 << level) & (apart < 2 << level) & (down > across)
-        level_ref[level] = jnp.where(inside, 1.0, 0.0).astype(jnp.bfloat16)
+        level_ref[level] = jnp.where(inside, 1.0, 0.0)
 
 
 def head_pieces(convolved, extras, gate_ref, mine, width):
@@ -264,44 +275,42 @@
         chains = head_pieces(convolved, extras, gate_ref, mine, width)
         for pair in range(pairs):
             made = block_values(chains[PAIR * pair : PAIR * (pair + 1)], mask_ref, width)
-            lower = (made["beta"] * made["key_key"] * made["fall"]).astype(bf16)
-            made["lower"] = lower
-            made["inverse"] = mask_ref[1] - (level_ref[0] * lower).astype(jnp.float32)
+            made["lower"] = made["beta"] * made["key_key"] * made["fall"]
+            made["inverse"] = mask_ref[1] - level_ref[0] * made["lower"]
             blocks.append((block, pair, made))
     for level in range(1, level_ref.shape[0]):
         inner = [
-            low_dot(level_ref[level] * made["lower"], made["inverse"], NN) for _, _, made in blocks
+            wide_dot(level_ref[level] * made["lower"], made["inverse"], NN) for _, _, made in blocks
         ]
         for (_, _, made), right_side in zip(blocks, inner):
-            made["inverse"] = made["inverse"] - low_dot(made["inverse"], right_side, NN)
+            made["inverse"] = made["inverse"] - wide_dot(made["inverse"], right_side, NN)
     for block, pair, made in blocks:
-        inverse = made["inverse"].astype(bf16)
+        inverse = made["inverse"]
         inverse_ref[0, block, pair] = inverse
         weighted = jnp.concatenate(
             [made["beta"] * made["value"], made["beta"] * made["key_grown"]], axis=1
         )
-        made["fresh_carried"] = low_dot(inverse, weighted, NN)
-        made_ref[0, block, pair] = made["fresh_carried"].astype(bf16)
+        made["fresh_carried"] = wide_dot(inverse, weighted, NN)
+        made_ref[0, block, pair] = made["fresh_carried"]
     for block, pair, made in blocks:
         fresh, carried = made["fresh_carried"][:, :width], made["fresh_carried"][:, width:]
         written, results = [], []
         for which in range(PAIR):
             chain = PAIR * pair + which
             state = state_ref[chain]
-            low_state = state.astype(bf16)
-            memory_ref[0, block, chain] = low_state
-            seen = low_dot(
-                stack([half(carried, which), half(made["query_grown"], which)]), low_state, NN
+            memory_ref[0, block, chain] = state
+            seen = wide_dot(
+                stack([half(carried, which), half(made["query_grown"], which)]), state, NN
             )
             new = half(fresh, which) - seen[:BLOCK]
             written.append(new)
             results.append(seen[BLOCK:])
-            state_ref[chain] = half(made["totals"], which)[0:1] * state + low_dot(
+            state_ref[chain] = half(made["totals"], which)[0:1] * state + wide_dot(
                 half(made["key_fallen"], which), new, TN
             )
-        written = stack(written).astype(bf16)
+        written = stack(written)
         written_ref[0, block, pair] = written
-        core = (stack(results) + low_dot(made["scores"], written, NN)).astype(bf16)
+        core = (stack(results) + wide_dot(made["scores"], written, NN)).astype(bf16)
         core_ref[0, block, pair] = core
         core = core.astype(jnp.float32)
         normed = core * lax.rsqrt(rows_sum(core * core) / width + eps_norm) * gain_ref[0:1]
@@ -389,9 +398,9 @@
             grad_unit = stack(grad_unit)
             inner = rows_sum(grad_unit * normed) / width
             made["grad_core"] = (core_scale * (grad_unit - normed * inner)).astype(bf16)
-            made["from_scores"] = low_dot(made["scores"], made["grad_core"], TN)
+            made["from_scores"] = wide_dot(made["scores"], made["grad_core"], TN)
             made["grad_scores"] = (
-                low_dot(made["grad_core"], written_ref[0, block, pair], NT) * made["fall"]
+                wide_dot(made["grad_core"], written_ref[0, block, pair], NT) * made["fall"]
             )
             blocks.append((block, pair, made))
     grad_small_ref[0:1] += grad_gain
@@ -402,28 +411,23 @@
         for which in range(PAIR):
             chain = PAIR * pair + which
             state, grad_state = memory_ref[0, block, chain], state_ref[chain]
-            low_grad_state = grad_state.astype(bf16)
             grad_out = half(made["grad_core"], which)
-            grad_new = half(made["from_scores"], which) + low_dot(
-                half(made["key_fallen"], which), low_grad_state, NN
+            grad_new = half(made["from_scores"], which) + wide_dot(
+                half(made["key_fallen"], which), grad_state, NN
             )
-            low_new = grad_new.astype(bf16)
             totals = half(made["totals"], which)[0:1]
             state_ref[chain] = (
                 totals * grad_state
-                + low_dot(half(made["query_grown"], which), grad_out, TN)
-                - low_dot(half(carried, which), low_new, TN)
+                + wide_dot(half(made["query_grown"], which), grad_out, TN)
+                - wide_dot(half(carried, which), grad_new, TN)
             )
-            back = low_dot(stack([grad_out, low_new]), state, NT)
             parts.append(
                 (
-                    low_new,
-                    back[:BLOCK],
-                    -back[BLOCK:],
-                    low_dot(half(written_ref[0, block, pair], which), low_grad_state, NT),
-                    rows_sum(
-                        jnp.sum(state.astype(f32) * grad_state, axis=0, keepdims=True) * totals
-                    ),
+                    grad_new,
+                    wide_dot(grad_out, state, NT),
+                    -wide_dot(grad_new, state, NT),
+                    wide_dot(half(written_ref[0, block, pair], which), grad_state, NT),
+                    rows_sum(jnp.sum(state * grad_state, axis=0, keepdims=True) * totals),
                 )
             )
         made["grad_new"], made["grad_query_grown"], made["grad_carried"] = [
@@ -440,12 +444,12 @@
         beta, growth, fall = made["beta"], made["growth"], made["fall"]
         query, key, value = made["query"], made["key"], made["value"]
         fall_strict = fall - mask_ref[1]
-        grad_weighted = low_dot(
+        grad_weighted = wide_dot(
             inverse_ref[0, block, pair],
-            jnp.concatenate([made["grad_new"].astype(f32), made["grad_carried"]], axis=1),
+            jnp.concatenate([made["grad_new"], made["grad_carried"]], axis=1),
             TN,
         )
-        grad_lower = -low_dot(grad_weighted, made_ref[0, block, pair], NT) * fall_strict
+        grad_lower = -wide_dot(grad_weighted, made_ref[0, block, pair], NT) * fall_strict
         grad_key_key = grad_lower * beta
         from_lower = grad_lower * made["key_key"]
         grad_value_part, grad_key_part = grad_weighted[:, :width], grad_weighted[:, width:]
@@ -468,16 +472,16 @@
                 for which in range(PAIR)
             ]
         )
-        grad_cumulative = grad_cumulative + ends - split_dot(shifts, ones, TN, False)
-        grad_decay = rounded(split_dot(within, grad_cumulative, TN, True))
-        both = stack([grad_scores, grad_key_key]).astype(bf16)
-        down = low_dot(both, key, NN)
+        grad_cumulative = grad_cumulative + ends - wide_dot(shifts, ones, TN)
+        grad_decay = rounded(wide_dot(within.astype(bf16), grad_cumulative, TN))
+        both = stack([grad_scores, grad_key_key])
+        down = wide_dot(both, key.astype(bf16), NN)
         grad_query = growth * made["grad_query_grown"] + down[: PAIR * BLOCK]
         grad_key = (
             made["key_fall"] * made["grad_key_fallen"]
             + beta * growth * grad_key_part
             + down[PAIR * BLOCK :]
-            + low_dot(both, stack([query, key]), TN)
+            + wide_dot(both, stack([query, key]).astype(bf16), TN)
         )
         grad_query = rounded(grad_query) * width ** (-0.5)
         grad_key = rounded(grad_key)
@@ -564,6 +568,21 @@
     return pl.pallas_call(functools.partial(ff_unpack_body, width), out_shape=[shape, shape])(packed)
 
 
+def mixer_unpack_body(order, in_ref, *out_refs):
+    width = out_refs[0].shape[1] // len(order)
+    columns = in_ref.shape[2] // len(out_refs)
+    for which, ref in enumerate(out_refs):
+        for head, (spot, place) in enumerate(order):
+            first = which * columns + place * width
+            piece = in_ref[spot, :, first : first + width].astype(jnp.float32)
+            ref[:, head * width : (head + 1) * width] = piece
+
+
+def mixer_unpack(packed, order, head_width):
+    shape = jax.ShapeDtypeStruct((packed.shape[1], len(order) * head_width), jnp.float32)
+    return pl.pallas_call(functools.partial(mixer_unpack_body, order), out_shape=[shape] * 4)(packed)
+
+
 def whole_spec(shape):
     return pl.BlockSpec(shape, lambda step, me: (0,) * len(shape))
 
@@ -598,17 +617,17 @@
         for shape, kind in [
             ((2, sequences, span, 3 * cols), jnp.float32),
             ((2, pairs, size, head_width), jnp.bfloat16),
-            ((2, pairs, size, size), jnp.bfloat16),
-            ((2, pairs, size, 2 * head_width), jnp.bfloat16),
-            ((2, pairs, size, head_width), jnp.bfloat16),
-            ((2, chains, head_width, head_width), jnp.bfloat16),
+            ((2, pairs, size, size), jnp.float32),
+            ((2, pairs, size, 2 * head_width), jnp.float32),
+            ((2, pairs, size, head_width), jnp.float32),
+            ((2, chains, head_width, head_width), jnp.float32),
         ]
     ]
     scratch = [
         pltpu.VMEM((sequences, span + 8, 3 * cols), jnp.float32),
         pltpu.VMEM((chains, head_width, head_width), jnp.float32),
         pltpu.VMEM((2, size, size), jnp.float32),
-        pltpu.VMEM((int(BLOCK).bit_length() - 1, size, size), jnp.bfloat16),
+        pltpu.VMEM((int(BLOCK).bit_length() - 1, size, size), jnp.float32),
     ]
     cost = pl.CostEstimate(
         flops=4 * steps * pairs * size**3 * 18,
@@ -934,7 +953,13 @@
     mixer_own, *done = lax.optimization_barrier((mixer_own, *done))
     swapped, grad_w_gate, grad_w_up, grad_down, output_own, input_grad = done
     mixer_own = exchange(mixer_own.reshape(n_seq, rows, -1))
-    grad_output, mixer_own = lax.optimization_barrier((grad_output, mixer_own))
+    order = []
+    for head in range(heads):
+        spot, from_band = divmod(head, bands)
+        from_place, which = divmod(spot, mine)
+        order.append((from_band * group + from_place, which))
+    mixer_grads = mixer_unpack(mixer_own, tuple(order), head_width)
+    grad_output, *mixer_grads = lax.optimization_barrier((grad_output, *mixer_grads))
     grad_output = grad_output.astype(f32)
     sums = jnp.sum(swapped, axis=0)
     gate_sums = jnp.sum(swapped[:, : edges[1]].reshape(n_dp, n_seq, -1), axis=0)
@@ -946,15 +971,13 @@
         output_own.astype(bf16).reshape(tokens_shape),
         input_grad.reshape(tokens_shape),
         gain_sums[0],
-        by_columns(mixer_own[:, :, :cols]),
-        by_columns(mixer_own[:, :, cols : 2 * cols]),
-        by_columns(mixer_own[:, :, 2 * cols : 3 * cols]),
+        *mixer_grads[:3],
         sums[edges[2] : edges[3]].reshape(conv_weight.shape),
         gate_sums[0],
         gate_sums[1],
         common[head_width : head_width + heads],
         common[head_width + heads :],
-        by_columns(mixer_own[:, :, 3 * cols :]),
+        mixer_grads[3],
         common[:head_width],
         grad_output,
         gain_sums[1],

time: 588 us -> 583 us (level)
  Pallas kernels: 44.6 us -> 60.1 us
  waiting for transfers between devices: 199 us -> 184 us
    reduce_scatter x4, waiting for transfers between devices: 21.4 us -> 0.06 us  [scatter_dp(): lax.psum_scatter(value.astype(bf16), 'dp', scatter_dimension=0, tiled=True)]
    all_to_all x2, waiting for transfers between devices: 0.01 us -> 11.6 us  [exchange(): lax.all_to_all(blocks, 'seq', split_axis=0, concat_axis=0, tiled=True)]
    pallas_call x1, Pallas kernels: 24.3 us -> 32.6 us  [mixer_backward(): pl.pallas_call(mixer_backward_body, grid_spec=pltpu.PrefetchScalarGridSpe...]
    unnamed x220 -> x156, local copies, waits for them, and re-layouts: 45.8 us -> 43.5 us
  transfers between devices with their start and end apart: 66 -> 66, of which waited for: 28 -> 27; matrix products, arithmetic and copies ran while one was open for 34% -> 34% of each run, Pallas kernels for 8% -> 10%
where the time goes in v3:
time: 583 us; the launch traced here: 573 us
  waiting for transfers between devices  184 us (32%)
  matrix products  85.7 us (15%)
  local copies, waits for them, and re-layouts  76.8 us (13%)
  Pallas kernels  60.1 us (10%)
  starting transfers between devices  56 us (10%)
  other arithmetic  50.7 us (9%)
  blocking collectives  44.3 us (8%)
  between operations  16.3 us (3%)
    ppermute x54, waiting for transfers between devices, swap(): lax.ppermute(value, 'seq', [(place, place ^ bit) for place in range(count)])  116 us
    all_to_all x2, blocking collectives, exchange(): lax.all_to_all(blocks, 'seq', split_axis=0, concat_axis=0, tiled=True)  44.3 us
    unnamed x156, local copies, waits for them, and re-layouts  43.5 us
    ppermute x54, starting transfers between devices, swap(): lax.ppermute(value, 'seq', [(place, place ^ bit) for place in range(count)])  41.5 us
    all_gather x4, waiting for transfers between devices, gather_dp(): return lax.all_gather(block, 'dp', axis=0, tiled=True)  39.4 us
    pallas_call x1, Pallas kernels, mixer_backward(): pl.pallas_call(mixer_backward_body, grid_spec=pltpu.PrefetchScalarGridSpe...  32.6 us
    dot_general x5, matrix products, contract_rows(): lax.dot_general(left_side, right_side, (((0,), (0,)), ((), ())), preferre...  29.3 us
    dot_general x5, matrix products, times_transposed(): lax.dot_general(left_side, right_side, (((1,), (1,)), ((), ())), preferre...  28.4 us
  transfers between devices with their start and end apart: 66, of which 27 were waited for; matrix products, arithmetic and copies ran while one was open for 34% of the time, Pallas kernels for 10%

profile of v3, /device:TPU:0, one launch (start us, length us, event | category | flops | bytes accessed | tf_op | source)
XLA Modules:
  0.0 573.3 jit_solution(7855459956701058846)
XLA Ops:
  13.3 20.4 %all_to_all.41 = bf16[8,64,1024]{2,1,0:T(8,128)(2,1)} all-to-all(bf16[8,64,1024]{2,1,0:T(8,128)(2,1)S(1)} %pad_maximum_fusion.3), channel_id=1, replica_groups=mesh['dp'=4,'seq'=8] {'seq'}, dimensions={0} | all-to-all | bytes 2097152 | tf_op jit(solution)/shard_map/all_to_all | solution.py:771
  37.2 23.8 %all_to_all.42 = bf16[8,64,1408]{2,1,0:T(8,128)(2,1)} all-to-all(bf16[8,64,1408]{2,1,0:T(8,128)(2,1)} %shard_map.314), channel_id=1, replica_groups=mesh['dp'=4,'seq'=8] {'seq'}, dimensions={0} | all-to-all | bytes 2883584 | tf_op jit(solution)/shard_map/all_to_all | solution.py:771
  68.6 7.4 %collective-permute-done = bf16[128,2048]{1,0:T(8,128)(2,1)S(1)} collective-permute-done((bf16[128,2048]{1,0:T(8,128)(2,1)S(1)}, bf16[128,2048]{1,0:T(8,128)(2,1)S(1)}, u32[]{:S(2)}, u32[]{:S(2)}) %collective-permute-start) | collective-permute-done | bytes 524320 | tf_op jit(solution)/shard_map/ppermute | solution.py:46
  79.8 7.5 %collective-permute-done.9 = bf16[128,2048]{1,0:T(8,128)(2,1)} collective-permute-done((bf16[128,2048]{1,0:T(8,128)(2,1)}, bf16[128,2048]{1,0:T(8,128)(2,1)}, u32[]{:S(2)}, u32[]{:S(2)}) %collective-permute-start.9) | collective-permute-done | bytes 524320 | tf_op jit(solution)/shard_map/ppermute | solution.py:46
  107.9 9.3 %all-to-all-done.1 = bf16[32,2,1472]{2,1,0:T(2,128)(2,1)S(1)} async-done(((bf16[32,2,1472]{2,1,0:T(2,128)(2,1)}), bf16[32,2,1472]{2,1,0:T(2,128)(2,1)S(1)}, u32[]{:S(2)}, u32[]{:S(2)}) %all-to-all-start.1) | async-done | bytes 188448 | tf_op jit(solution)/shard_map/all_to_all | solution.py:766
  131.6 9.0 %fusion.6.proj_ref = f32[2,4,2,64,1024]{4,3,2,1,0:T(8,128)} fusion(bf16[2048,1024]{1,0:T(8,128)(2,1)S(1)} %copy-done.58, f32[2048]{0:T(1024)S(1)} %reshape.801, f32[2,4,2,64]{3,2,1,0:T(2,128)S(1)} %rsqrt.40, bf16[2,4,2,64,2048]{4,3,2,1,0:T(8,128)(2,1)} %bitcast.257), kind=kOutput, calls=%fused_computation.16 | convolution fusion | flops 4303355904 | bytes 12595200 | tf_op jit(solution)/shard_map/dot_general | solution.py:26
  141.9 18.7 %shard_map.313 = (bf16[2,4,2,64,256]{4,3,2,1,0:T(8,128)(2,1)S(1)}, f32[4,2,2,64,768]{4,3,2,1,0:T(8,128)S(1)}, bf16[4,2,2,128,128]{4,3,2,1,0:T(8,128)(2,1)S(1)}, ...) custom-call(s32[1]{0:T(128)} %bitcast.24.me_ref, ...), custom_call_target="tpu_custom_call" | custom-call | flops 1207959552 | bytes 12582912 | tf_op jit(solution)/shard_map/pallas_call | solution.py:645
  184.2 7.5 %collective-permute-done.18 = bf16[2,64,2048]{2,1,0:T(8,128)(2,1)} collective-permute-done((bf16[2,64,2048]{2,1,0:T(8,128)(2,1)}, bf16[2,64,2048]{2,1,0:T(8,128)(2,1)}, u32[]{:S(2)}, u32[]{:S(2)}) %collective-permute-start.18) | collective-permute-done | bytes 524320 | tf_op jit(solution)/shard_map/ppermute | solution.py:46
  214.7 5.7 collective-permute-done.22
  233.5 10.6 %fusion.49 = f32[1024,1408]{1,0:T(8,128)S(1)} fusion(bf16[1024,2048]{1,0:T(8,128)(2,1)} %bitcast.60, bf16[2048,1408]{1,0:T(8,128)(2,1)} %all-gather.11.cloned.1.call-done), kind=kOutput, calls=%fused_computation.196 | convolution fusion | flops 5905580032 | bytes 15728640 | tf_op jit(solution)/shard_map/dot_general | solution.py:26
  254.1 37.8 %all-gather.9.cloned.1.call-done = bf16[704,2048]{1,0:T(8,128)(2,1)} async-done(((bf16[176,2048]{1,0:T(8,128)(2,1)}), bf16[704,2048]{1,0:T(8,128)(2,1)}) %all-gather.9.cloned.1.call-update) | async-done | bytes 2883600 | tf_op jit(solution)/shard_map/all_gather | solution.py:774
  291.9 9.2 %multiply_convert_fusion.3 = (bf16[1024,704]{1,0:T(8,128)(2,1)S(1)}, bf16[1024,704]{1,0:T(8,128)(2,1)S(1)}) fusion(f32[1024,1408]{1,0:T(8,128)} %copy-done.34, bf16[1024,2048]{1,0:T(8,128)(2,1)} %bitcast.345, bf16[704,2048]{1,0:T(8,128)(2,1)} %all-gather.9.cloned.1.call-done), kind=kOutput, calls=%fused_computation.24 | convolution fusion | flops 2962161664 | bytes 15728640 | tf_op jit(solution)/shard_map/dot_general | solution.py:36
  301.1 9.0 %convolution_convert_fusion.2 = bf16[1024,2048]{1,0:T(8,128)(2,1)S(1)} fusion(bf16[2048,1408]{1,0:T(8,128)(2,1)} %all-gather.11.cloned.1.call-done, bf16[1024,704]{1,0:T(8,128)(2,1)S(1)} %get-tuple-element.152, bf16[1024,704]{1,0:T(8,128)(2,1)S(1)} %get-tuple-element.151), kind=kOutput, calls=%fused_computation.19 | convolution fusion | flops 5913444352 | bytes 12845056 | tf_op jit(solution)/shard_map/dot_general | solution.py:36
  312.4 12.1 %convolution_convert_fusion = bf16[2048,1408]{1,0:T(8,128)(2,1)} fusion(bf16[1024,2048]{1,0:T(8,128)(2,1)} %bitcast.60, bf16[1024,704]{1,0:T(8,128)(2,1)S(1)} %get-tuple-element.152, bf16[1024,704]{1,0:T(8,128)(2,1)S(1)} %get-tuple-element.151), kind=kOutput, calls=%fused_computation.6 | convolution fusion | flops 5914230784 | bytes 12845056 | tf_op jit(solution)/shard_map/dot_general | solution.py:30
  331.4 11.2 %collective-permute-done.31 = bf16[2,64,2048]{2,1,0:T(8,128)(2,1)S(1)} collective-permute-done((bf16[2,64,2048]{2,1,0:T(8,128)(2,1)S(1)}, bf16[2,64,2048]{2,1,0:T(8,128)(2,1)S(1)}, u32[]{:S(2)}, u32[]{:S(2)}) %collective-permute-start.31) | collective-permute-done | bytes 524320 | tf_op jit(solution)/shard_map/ppermute | solution.py:46
  364.8 5.3 collective-permute-done.35
  384.8 32.6 %shard_map.315 = (bf16[2,4,2,64,1024]{4,3,2,1,0:T(8,128)(2,1)S(1)}, bf16[2,4,2,64,128]{4,3,2,1,0:T(8,128)(2,1)S(1)}, f32[4,768]{1,0:T(4,128)S(1)}, f32[8,128]{1,0:T(8,128)S(1)}) custom-call(s32[1]{0:T(128)} %bitcast.24.me_ref, f32[2,4,2,64,1024]{4,3,2,1,0:T(8,128)} %fusion.6.proj_ref, f32[2,4,2,64,128]{4,3,2,1,0:T(8,128)S(1)} %copy-done.1, ...), custom_call_target="tpu_custom_call" | custom-call | flops 1207959552 | bytes 12582912 | tf_op jit(solution)/shard_map/pallas_call | solution.py:674
  418.7 6.2 %convolution_convert_fusion.4 = bf16[2048,1024]{1,0:T(8,128)(2,1)} fusion(bf16[1024,2048]{1,0:T(8,128)(2,1)S(1)} %bitcast.314, bf16[1024,1024]{1,0:T(8,128)(2,1)S(1)} %bitcast.298), kind=kOutput, calls=%fused_computation.21 | convolution fusion | flops 4297064448 | bytes 10485760 | tf_op jit(solution)/shard_map/dot_general | solution.py:30
  447.2 5.2 fusion.1
  469.1 7.8 %collective-permute-done.50 = bf16[2,64,2048]{2,1,0:T(8,128)(2,1)S(1)} collective-permute-done((bf16[2,64,2048]{2,1,0:T(8,128)(2,1)S(1)}, bf16[2,64,2048]{2,1,0:T(8,128)(2,1)S(1)}, u32[]{:S(2)}, u32[]{:S(2)}) %collective-permute-start.50) | collective-permute-done | bytes 524320 | tf_op jit(solution)/shard_map/ppermute | solution.py:46
  479.5 14.9 %collective-permute-done.51 = bf16[64,2048]{1,0:T(8,128)(2,1)S(1)} collective-permute-done((bf16[64,2048]{1,0:T(8,128)(2,1)S(1)}, bf16[64,2048]{1,0:T(8,128)(2,1)S(1)}, u32[]{:S(2)}, u32[]{:S(2)}) %collective-permute-start.51) | collective-permute-done | bytes 262176 | tf_op jit(solution)/shard_map/ppermute | solution.py:46
  504.3 20.0 %collective-permute-done.48 = bf16[64,2048]{1,0:T(8,128)(2,1)S(1)} collective-permute-done((bf16[64,2048]{1,0:T(8,128)(2,1)S(1)}, bf16[64,2048]{1,0:T(8,128)(2,1)S(1)}, u32[]{:S(2)}, u32[]{:S(2)}) %collective-permute-start.48) | collective-permute-done | bytes 262176 | tf_op jit(solution)/shard_map/ppermute | solution.py:46
  535.5 6.2 %all-to-all-done.4 = f32[32,1,1408]{2,1,0:T(1,128)S(1)} async-done(((f32[32,1,1408]{2,1,0:T(1,128)}), f32[32,1,1408]{2,1,0:T(1,128)S(1)}, u32[]{:S(2)}, u32[]{:S(2)}) %all-to-all-start.4) | async-done | bytes 180256 | tf_op jit(solution)/shard_map/all_to_all | solution.py:766
  549.1 11.6 %all-to-all-done.5.in_ref = bf16[8,64,1024]{2,1,0:T(8,128)(2,1)S(1)} async-done(((bf16[8,64,1024]{2,1,0:T(8,128)(2,1)}), bf16[8,64,1024]{2,1,0:T(8,128)(2,1)S(1)}, u32[]{:S(2)}, u32[]{:S(2)}) %all-to-all-start.5) | async-done | bytes 1048608 | tf_op jit(solution)/shard_map/all_to_all | solution.py:771
  (469 shorter events, 248.0 us)
Async XLA Ops:
  7.2 111.1 %all-gather.7.cloned.1.call-start = ((), (), s32[]{:S(2)}) async-start(), calls=%async_computation.11 | async-start | bytes 1310720 | tf_op jit(solution)/shard_map/all_gather | solution.py:774
  7.9 118.3 %all-gather.5.cloned.1.call-start = ((), (), s32[]{:S(2)}) async-start(), calls=%async_computation.10 | async-start | bytes 5242880 | tf_op jit(solution)/shard_map/all_gather | solution.py:774
  33.8 199.7 %all-gather.11.cloned.1.call-start = ((), (), s32[]{:S(2)}) async-start(), calls=%async_computation.13 | async-start | bytes 7208960 | tf_op jit(solution)/shard_map/all_gather | solution.py:774
  61.1 230.8 %all-gather.9.cloned.1.call-start = ((), (), s32[]{:S(2)}) async-start(), calls=%async_computation.12 | async-start | bytes 3604480 | tf_op jit(solution)/shard_map/all_gather | solution.py:774
  62.3 32.4 %collective-permute-start.4 = (bf16[128,2048]{1,0:T(8,128)(2,1)S(1)}, bf16[128,2048]{1,0:T(8,128)(2,1)S(1)}, u32[]{:S(2)}, u32[]{:S(2)}) collective-permute-start(bf16[128,2048]{1,0:T(8,128)(2,1)S(1)} %bitcast.303), channel_id=1, source_target_pairs={{0,1},{1,0},{2,3},{3,2},{4,5},{5,4},{6,7},{7,6},{8,9},{9,8},{10,11... | collective-permute-start | bytes 1572872 | tf_op jit(solution)/shard_map/ppermute | solution.py:46
  62.3 25.0 %collective-permute-start.9 = (bf16[128,2048]{1,0:T(8,128)(2,1)}, bf16[128,2048]{1,0:T(8,128)(2,1)}, u32[]{:S(2)}, u32[]{:S(2)}) collective-permute-start(bf16[128,2048]{1,0:T(8,128)(2,1)} %bitcast.32), channel_id=1, source_target_pairs={{0,2},{1,3},{2,0},{3,1},{4,6},{5,7},{6,4},{7,5},{8,10},{9,11},{10,... | collective-permute-start | bytes 1572872 | tf_op jit(solution)/shard_map/ppermute | solution.py:46
  63.8 25.3 %collective-permute-start.10 = (bf16[128,2048]{1,0:T(8,128)(2,1)}, bf16[128,2048]{1,0:T(8,128)(2,1)S(1)}, u32[]{:S(2)}, u32[]{:S(2)}) collective-permute-start(bf16[128,2048]{1,0:T(8,128)(2,1)} %bitcast.32), channel_id=1, source_target_pairs={{0,4},{1,5},{2,6},{3,7},{4,0},{5,1},{6,2},{7,3},{8,12},{9,13},{10,... | collective-permute-start | bytes 1572872 | tf_op jit(solution)/shard_map/ppermute | solution.py:46
  87.4 84.8 %collective-permute-start.13 = (bf16[128,2048]{1,0:T(8,128)(2,1)}, bf16[128,2048]{1,0:T(8,128)(2,1)}, u32[]{:S(2)}, u32[]{:S(2)}) collective-permute-start(bf16[128,2048]{1,0:T(8,128)(2,1)} %bitcast.32), channel_id=1, source_target_pairs={{0,1},{1,0},{2,3},{3,2},{4,5},{5,4},{6,7},{7,6},{8,9},{9,8},{10,11... | collective-permute-start | bytes 1572872 | tf_op jit(solution)/shard_map/ppermute | solution.py:46
  89.1 78.4 %collective-permute-start.11 = (bf16[64,2048]{1,0:T(8,128)(2,1)}, bf16[64,2048]{1,0:T(8,128)(2,1)S(1)}, u32[]{:S(2)}, u32[]{:S(2)}) collective-permute-start(bf16[64,2048]{1,0:T(8,128)(2,1)} %slice.366), channel_id=1, source_target_pairs={{0,4},{1,5},{2,6},{3,7},{4,0},{5,1},{6,2},{7,3},{8,12},{9,13},{10,... | collective-permute-start | bytes 786440 | tf_op jit(solution)/shard_map/ppermute | solution.py:46
  91.9 76.7 %collective-permute-start.12 = (bf16[64,2048]{1,0:T(8,128)(2,1)}, bf16[64,2048]{1,0:T(8,128)(2,1)}, u32[]{:S(2)}, u32[]{:S(2)}) collective-permute-start(bf16[64,2048]{1,0:T(8,128)(2,1)} %slice.367), channel_id=1, source_target_pairs={{0,2},{1,3},{2,0},{3,1},{4,6},{5,7},{6,4},{7,5},{8,10},{9,11},{10,... | collective-permute-start | bytes 786440 | tf_op jit(solution)/shard_map/ppermute | solution.py:46
  99.5 17.6 %all-to-all-start.1 = ((bf16[32,2,1472]{2,1,0:T(2,128)(2,1)}), bf16[32,2,1472]{2,1,0:T(2,128)(2,1)S(1)}, u32[]{:S(2)}, u32[]{:S(2)}) async-start(bf16[32,2,1472]{2,1,0:T(2,128)(2,1)} %reshape.830), calls=%async_computation.1 | async-start | bytes 393216 | tf_op jit(solution)/shard_map/all_to_all | solution.py:766
  103.5 353.6 %reduce-scatter.9.cloned.1.call-start = ((), (), s32[]{:S(2)}) async-start(), calls=%async_computation.16 | async-start | bytes 3604480 | tf_op jit(solution)/shard_map/reduce_scatter | solution.py:879
  105.7 72.8 %collective-permute-start.14 = (bf16[128,2048]{1,0:T(8,128)(2,1)}, bf16[128,2048]{1,0:T(8,128)(2,1)}, u32[]{:S(2)}, u32[]{:S(2)}) collective-permute-start(bf16[128,2048]{1,0:T(8,128)(2,1)} %collective-permute-done.9), channel_id=1, source_target_pairs={{0,1},{1,0},{2,3},{3,2},{4,5},{5,4},{6,7},{7,6},{8,9},{9,8},{10,11... | collective-permute-start | bytes 1572872 | tf_op jit(solution)/shard_map/ppermute | solution.py:46
  170.3 40.2 %collective-permute-start.16 = (bf16[128,2048]{1,0:T(8,128)(2,1)}, bf16[128,2048]{1,0:T(8,128)(2,1)}, u32[]{:S(2)}, u32[]{:S(2)}) collective-permute-start(bf16[128,2048]{1,0:T(8,128)(2,1)} %constant_dynamic-update-slice_fusion.3), channel_id=1, source_target_pairs={{0,1},{1,0},{2,3},{3,2},{4,5},{5,4},{6,7},{7,6},{8,9},{9,8},{10,11... | collective-permute-start | bytes 1572872 | tf_op jit(solution)/shard_map/ppermute | solution.py:46
  212.4 17.8 %collective-permute-start.26 = (bf16[128,2048]{1,0:T(8,128)(2,1)S(1)}, bf16[128,2048]{1,0:T(8,128)(2,1)S(1)}, u32[]{:S(2)}, u32[]{:S(2)}) collective-permute-start(bf16[128,2048]{1,0:T(8,128)(2,1)S(1)} %multiply_convert_fusion.7), channel_id=1, source_target_pairs={{0,1},{1,0},{2,3},{3,2},{4,5},{5,4},{6,7},{7,6},{8,9},{9,8},{10,11... | collective-permute-start | bytes 1572872 | tf_op jit(solution)/shard_map/ppermute | solution.py:46
  254.0 242.5 %reduce-scatter.7.cloned.1.call-start = ((), (), s32[]{:S(2)}) async-start(), calls=%async_computation.15 | async-start | bytes 7208960 | tf_op jit(solution)/shard_map/reduce_scatter | solution.py:879
  324.5 217.2 %reduce-scatter.5.cloned.1.call-start = ((), (), s32[]{:S(2)}) async-start(), calls=%async_computation.14 | async-start | bytes 5242880 | tf_op jit(solution)/shard_map/reduce_scatter | solution.py:879
  425.0 139.3 %reduce-scatter.11.cloned.1.call-start = ((), (), s32[]{:S(2)}) async-start(), calls=%async_computation.17 | async-start | bytes 1310720 | tf_op jit(solution)/shard_map/reduce_scatter | solution.py:879
  435.4 24.0 %collective-permute-start.49 = (bf16[4,128,2048]{2,1,0:T(8,128)(2,1)}, bf16[4,128,2048]{2,1,0:T(8,128)(2,1)}, u32[]{:S(2)}, u32[]{:S(2)}) collective-permute-start(bf16[4,128,2048]{2,1,0:T(8,128)(2,1)} %bitcast.108), channel_id=1, source_target_pairs={{0,1},{1,0},{2,3},{3,2},{4,5},{5,4},{6,7},{7,6},{8,9},{9,8},{10,11... | collective-permute-start | bytes 6291464 | tf_op jit(solution)/shard_map/ppermute | solution.py:46
  467.0 28.6 %collective-permute-start.45 = (bf16[2,64,2048]{2,1,0:T(8,128)(2,1)S(1)}, bf16[2,64,2048]{2,1,0:T(8,128)(2,1)S(1)}, u32[]{:S(2)}, u32[]{:S(2)}) collective-permute-start(bf16[2,64,2048]{2,1,0:T(8,128)(2,1)S(1)} %slice.395), channel_id=1, source_target_pairs={{0,4},{1,5},{2,6},{3,7},{4,0},{5,1},{6,2},{7,3},{8,12},{9,13},{10,... | collective-permute-start | bytes 1572872 | tf_op jit(solution)/shard_map/ppermute | solution.py:46
  468.5 27.9 %collective-permute-start.47 = (bf16[2,64,2048]{2,1,0:T(8,128)(2,1)S(1)}, bf16[2,64,2048]{2,1,0:T(8,128)(2,1)S(1)}, u32[]{:S(2)}, u32[]{:S(2)}) collective-permute-start(bf16[2,64,2048]{2,1,0:T(8,128)(2,1)S(1)} %slice.335), channel_id=1, source_target_pairs={{0,2},{1,3},{2,0},{3,1},{4,6},{5,7},{6,4},{7,5},{8,10},{9,11},{10,... | collective-permute-start | bytes 1572872 | tf_op jit(solution)/shard_map/ppermute | solution.py:46
  496.6 28.0 %all-to-all-start.3 = ((bf16[8,64,1408]{2,1,0:T(8,128)(2,1)}), bf16[8,64,1408]{2,1,0:T(8,128)(2,1)S(1)}, u32[]{:S(2)}, u32[]{:S(2)}) async-start(bf16[8,64,1408]{2,1,0:T(8,128)(2,1)} %bitcast.324), calls=%async_computation.5 | async-start | bytes 2883584 | tf_op jit(solution)/shard_map/all_to_all | solution.py:771
  500.2 24.2 %collective-permute-start.48 = (bf16[64,2048]{1,0:T(8,128)(2,1)S(1)}, bf16[64,2048]{1,0:T(8,128)(2,1)S(1)}, u32[]{:S(2)}, u32[]{:S(2)}) collective-permute-start(bf16[64,2048]{1,0:T(8,128)(2,1)S(1)} %slice_bitcast_fusion.4), channel_id=1, source_target_pairs={{0,4},{1,5},{2,6},{3,7},{4,0},{5,1},{6,2},{7,3},{8,12},{9,13},{10,... | collective-permute-start | bytes 786440 | tf_op jit(solution)/shard_map/ppermute | solution.py:46
  541.8 18.9 %all-to-all-start.5 = ((bf16[8,64,1024]{2,1,0:T(8,128)(2,1)}), bf16[8,64,1024]{2,1,0:T(8,128)(2,1)S(1)}, u32[]{:S(2)}, u32[]{:S(2)}) async-start(bf16[8,64,1024]{2,1,0:T(8,128)(2,1)} %bitcast.325), calls=%async_computation.9 | async-start | bytes 2097152 | tf_op jit(solution)/shard_map/all_to_all | solution.py:771
  (103 other events, 994.1 us)
Sparse Core Ops, SparseCore 0:
  9.6 30.6 all-gather.6
  41.8 84.3 all-gather.4
  127.8 105.1 all-gather.10
  234.4 57.4 all-gather.8
  294.1 54.8 reduce-scatter.8
  351.1 102.1 reduce-scatter.6
  455.6 77.2 reduce-scatter.4
  535.3 27.6 reduce-scatter.10

commit v4 on v3

--- a/solution.py
+++ b/solution.py
@@ -706,6 +706,26 @@
     return lax.optimization_barrier((value,) + others)[0]
 
 
+def shift_dp(value, step, sources):
+    return lax.ppermute(value, "dp", [(place, place + step) for place in sources])
+
+
+def line_gather(block, ties):
+    count = lax.axis_size("dp")
+    me = lax.axis_index("dp")
+    ups, downs = [block], [block]
+    for step in range(1, count):
+        if step <= len(ties):
+            ups[-1], downs[-1] = lax.optimization_barrier((ups[-1], downs[-1], ties[step - 1]))[:2]
+        ups.append(shift_dp(ups[-1], 1, range(step - 1, count - 1)))
+        downs.append(shift_dp(downs[-1], -1, range(1, count - step + 1)))
+    result = jnp.zeros((count,) + block.shape, block.dtype)
+    for step in range(count):
+        piece = block if step == 0 else ups[step] + downs[count - step]
+        result = lax.dynamic_update_index_in_dim(result, piece, (me - step) % count, 0)
+    return result
+
+
 def on_device(
     inputs,
     norm_attn,
@@ -812,7 +832,8 @@
 
     gate_up_sent = exchange(ff_pack(w_gate, w_up, n_seq, ff_rows)).reshape(n_seq * rows, -1)
     gate_up_full = gather_dp(gate_up_sent)
-    down_full = gather_dp(w_down).reshape(ff, width)
+    most = ff_rows - min(64, ff_rows // 2)
+    down_rest = gather_dp(w_down[most:]).reshape(n_dp, ff_rows - most, width)
     mixer_full, shared, output_full = lax.optimization_barrier((mixer_full, shared, output_full))
 
     x_own = inputs.reshape(count * span, width)
@@ -861,13 +882,15 @@
     residual = x_own.astype(f32) + scatter_seq(shares(product(mixed, output_full)))
     normed_mid, pull_mid = jax.vjp(rms_scale, residual, gain_mlp)
     hidden_mid = gather_seq(normed_mid.astype(bf16)).reshape(total, width)
+    down_most = line_gather(w_down[:most], (mixer_full, residual, hidden_mid))
     gate_up = product(hidden_mid, gate_up_full)
     gate_pre, up_proj = gate_up[:, :ff], gate_up[:, ff:]
     sigmoid_gate = jax.nn.sigmoid(gate_pre)
     silu_gate = gate_pre * sigmoid_gate
     activ = (silu_gate * up_proj).astype(bf16)
     down_grads = contract_rows(activ, seed_all).astype(bf16)
-    down_full = after(down_full, down_grads)
+    down_rest = after(down_rest, down_grads)
+    down_full = jnp.concatenate([down_most, down_rest], axis=1).reshape(ff, width)
     from_down = times_transposed(seed_all, down_full)
     grad_gate = from_down * up_proj * sigmoid_gate * (1.0 + gate_pre * (1.0 - sigmoid_gate))
     grad_gate_up = jnp.concatenate([grad_gate, from_down * silu_gate], axis=1).astype(bf16)

time: 583 us -> 575 us (0.986)
  waiting for transfers between devices: 184 us -> 171 us
  matrix products: 85.7 us -> 76.7 us
  starting transfers between devices: 56 us -> 64.2 us
    all_gather x4, waiting for transfers between devices: 39.4 us -> 11.5 us  [gather_dp(): return lax.all_gather(block, 'dp', axis=0, tiled=True)]
    ppermute x0 -> x6, waiting for transfers between devices: none -> 13 us  [shift_dp(): lax.ppermute(value, 'dp', [(place, place + step) for place in sources])]
    ppermute x0 -> x6, starting transfers between devices: none -> 9.19 us  [shift_dp(): lax.ppermute(value, 'dp', [(place, place + step) for place in sources])]
    dynamic_update_slice x0 -> x3, other arithmetic: none -> 6.39 us  [line_gather(): lax.dynamic_update_index_in_dim(result, piece, (me - step) % count, 0)]
    unnamed x156 -> x184, local copies, waits for them, and re-layouts: 43.5 us -> 44.3 us
  transfers between devices with their start and end apart: 66 -> 72, of which waited for: 27 -> 33; matrix products, arithmetic and copies ran while one was open for 34% -> 33% of each run, Pallas kernels for 10% -> 11%
where the time goes in v4:
time: 575 us; the launch traced here: 565 us
  waiting for transfers between devices  171 us (30%)
  local copies, waits for them, and re-layouts  78.8 us (14%)
  matrix products  76.7 us (13%)
  starting transfers between devices  64.2 us (11%)
  Pallas kernels  60.3 us (10%)
  other arithmetic  53.5 us (9%)
  blocking collectives  44.4 us (8%)
  between operations  16.2 us (3%)
    ppermute x54, waiting for transfers between devices, swap(): lax.ppermute(value, 'seq', [(place, place ^ bit) for place in range(count)])  118 us
    all_to_all x2, blocking collectives, exchange(): lax.all_to_all(blocks, 'seq', split_axis=0, concat_axis=0, tiled=True)  44.4 us
    unnamed x184, local copies, waits for them, and re-layouts  44.3 us
    ppermute x54, starting transfers between devices, swap(): lax.ppermute(value, 'seq', [(place, place ^ bit) for place in range(count)])  39.2 us
    pallas_call x1, Pallas kernels, mixer_backward(): pl.pallas_call(mixer_backward_body, grid_spec=pltpu.PrefetchScalarGridSpe...  32.8 us
    dot_general x5, matrix products, contract_rows(): lax.dot_general(left_side, right_side, (((0,), (0,)), ((), ())), preferre...  26.2 us
    dot_general x5, matrix products, times_transposed(): lax.dot_general(left_side, right_side, (((1,), (1,)), ((), ())), preferre...  25.2 us
    dot_general x5, matrix products, product(): return jnp.dot(left_side, right_side, preferred_element_type=jnp.float32)  25.2 us
  transfers between devices with their start and end apart: 72, of which 33 were waited for; matrix products, arithmetic and copies ran while one was open for 33% of the time, Pallas kernels for 11%

profile of v4, /device:TPU:0, one launch (start us, length us, event | category | flops | bytes accessed | tf_op | source)
XLA Modules:
  0.0 564.7 jit_solution(3000036099024810538)
XLA Ops:
  13.3 20.4 %all_to_all.41 = bf16[8,64,1024]{2,1,0:T(8,128)(2,1)} all-to-all(bf16[8,64,1024]{2,1,0:T(8,128)(2,1)S(1)} %pad_maximum_fusion.4), channel_id=1, replica_groups=mesh['dp'=4,'seq'=8] {'seq'}, dimensions={0} | all-to-all | bytes 2097152 | tf_op jit(solution)/shard_map/all_to_all | solution.py:791
  37.2 24.0 %all_to_all.42 = bf16[8,64,1408]{2,1,0:T(8,128)(2,1)} all-to-all(bf16[8,64,1408]{2,1,0:T(8,128)(2,1)} %shard_map.314), channel_id=1, replica_groups=mesh['dp'=4,'seq'=8] {'seq'}, dimensions={0} | all-to-all | bytes 2883584 | tf_op jit(solution)/shard_map/all_to_all | solution.py:791
  70.6 5.6 collective-permute-done
  80.0 7.5 %collective-permute-done.9 = bf16[128,2048]{1,0:T(8,128)(2,1)} collective-permute-done((bf16[128,2048]{1,0:T(8,128)(2,1)}, bf16[128,2048]{1,0:T(8,128)(2,1)}, u32[]{:S(2)}, u32[]{:S(2)}) %collective-permute-start.9) | collective-permute-done | bytes 524320 | tf_op jit(solution)/shard_map/ppermute | solution.py:46
  108.1 9.1 %all-to-all-done.1 = bf16[32,2,1472]{2,1,0:T(2,128)(2,1)S(1)} async-done(((bf16[32,2,1472]{2,1,0:T(2,128)(2,1)}), bf16[32,2,1472]{2,1,0:T(2,128)(2,1)S(1)}, u32[]{:S(2)}, u32[]{:S(2)}) %all-to-all-start.1) | async-done | bytes 188448 | tf_op jit(solution)/shard_map/all_to_all | solution.py:786
  132.0 6.5 %fusion.6.proj_ref = f32[2,4,2,64,1024]{4,3,2,1,0:T(8,128)} fusion(bf16[2048,1024]{1,0:T(8,128)(2,1)S(1)} %copy-done.71, f32[2048]{0:T(1024)S(1)} %reshape.809, f32[2,4,2,64]{3,2,1,0:T(2,128)S(1)} %rsqrt.40, bf16[2,4,2,64,2048]{4,3,2,1,0:T(8,128)(2,1)S(1)} %bitcast.309), kind=kOutput, calls=%fused_computation.16 | convolution fusion | flops 4303355904 | bytes 12595200 | tf_op jit(solution)/shard_map/dot_general | solution.py:26
  139.9 18.7 %shard_map.313 = (bf16[2,4,2,64,256]{4,3,2,1,0:T(8,128)(2,1)S(1)}, f32[4,2,2,64,768]{4,3,2,1,0:T(8,128)S(1)}, bf16[4,2,2,128,128]{4,3,2,1,0:T(8,128)(2,1)S(1)}, ...) custom-call(s32[1]{0:T(128)} %bitcast.24.me_ref, ...), custom_call_target="tpu_custom_call" | custom-call | flops 1207959552 | bytes 12582912 | tf_op jit(solution)/shard_map/pallas_call | solution.py:645
  193.6 6.8 %collective-permute-done.22 = bf16[2,64,2048]{2,1,0:T(8,128)(2,1)S(1)} collective-permute-done((bf16[2,64,2048]{2,1,0:T(8,128)(2,1)S(1)}, bf16[2,64,2048]{2,1,0:T(8,128)(2,1)S(1)}, u32[]{:S(2)}, u32[]{:S(2)}) %collective-permute-start.22) | collective-permute-done | bytes 524320 | tf_op jit(solution)/shard_map/ppermute | solution.py:46
  237.8 11.1 %collective-permute-done.25 = bf16[112,2048]{1,0:T(8,128)(2,1)} collective-permute-done((bf16[112,2048]{1,0:T(8,128)(2,1)}, bf16[112,2048]{1,0:T(8,128)(2,1)}, u32[]{:S(2)}, u32[]{:S(2)}) %collective-permute-start.25) | collective-permute-done | bytes 458784 | tf_op jit(solution)/shard_map/ppermute | solution.py:710
  251.6 10.4 %fusion.49 = f32[1024,1408]{1,0:T(8,128)S(1)} fusion(bf16[1024,2048]{1,0:T(8,128)(2,1)} %bitcast.358, bf16[2048,1408]{1,0:T(8,128)(2,1)} %all-gather.11.cloned.1.call-done), kind=kOutput, calls=%fused_computation.201 | convolution fusion | flops 5905580032 | bytes 15728640 | tf_op jit(solution)/shard_map/dot_general | solution.py:26
  272.2 10.0 %all-gather.9.cloned.1.call-done = bf16[256,2048]{1,0:T(8,128)(2,1)} async-done(((bf16[64,2048]{1,0:T(8,128)(2,1)}), bf16[256,2048]{1,0:T(8,128)(2,1)}) %all-gather.9.cloned.1.call-update) | async-done | bytes 1048592 | tf_op jit(solution)/shard_map/all_gather | solution.py:794
  290.6 8.0 %multiply_convert_fusion.3 = (bf16[1024,704]{1,0:T(8,128)(2,1)S(1)}, bf16[1024,704]{1,0:T(8,128)(2,1)S(1)}) fusion(f32[1024,1408]{1,0:T(8,128)S(1)} %copy-done.39, bf16[1024,2048]{1,0:T(8,128)(2,1)} %bitcast.360, bf16[704,2048]{1,0:T(8,128)(2,1)S(1)} %bitcast.331), kind=kOutput, calls=%fused_computation.24 | convolution fusion | flops 2962161664 | bytes 15728640 | tf_op jit(solution)/shard_map/dot_general | solution.py:36
  298.6 6.9 %convolution_convert_fusion.2 = bf16[1024,2048]{1,0:T(8,128)(2,1)S(1)} fusion(bf16[2048,1408]{1,0:T(8,128)(2,1)S(1)} %bitcast.373, bf16[1024,704]{1,0:T(8,128)(2,1)S(1)} %get-tuple-element.166, bf16[1024,704]{1,0:T(8,128)(2,1)S(1)} %get-tuple-element.165), kind=kOutput, calls=%fused_computation.19 | convolution fusion | flops 5913444352 | bytes 12845056 | tf_op jit(solution)/shard_map/dot_general | solution.py:36
  309.3 8.8 %convolution_convert_fusion = bf16[2048,1408]{1,0:T(8,128)(2,1)} fusion(bf16[1024,2048]{1,0:T(8,128)(2,1)S(1)} %bitcast.359, bf16[1024,704]{1,0:T(8,128)(2,1)S(1)} %get-tuple-element.166, bf16[1024,704]{1,0:T(8,128)(2,1)S(1)} %get-tuple-element.165), kind=kOutput, calls=%fused_computation.6 | convolution fusion | flops 5914230784 | bytes 12845056 | tf_op jit(solution)/shard_map/dot_general | solution.py:30
  324.1 10.7 %collective-permute-done.37 = bf16[2,64,2048]{2,1,0:T(8,128)(2,1)S(1)} collective-permute-done((bf16[2,64,2048]{2,1,0:T(8,128)(2,1)S(1)}, bf16[2,64,2048]{2,1,0:T(8,128)(2,1)S(1)}, u32[]{:S(2)}, u32[]{:S(2)}) %collective-permute-start.37) | collective-permute-done | bytes 524320 | tf_op jit(solution)/shard_map/ppermute | solution.py:46
  354.2 6.8 %collective-permute-done.41 = bf16[128,2048]{1,0:T(8,128)(2,1)S(1)} collective-permute-done((bf16[128,2048]{1,0:T(8,128)(2,1)S(1)}, bf16[128,2048]{1,0:T(8,128)(2,1)S(1)}, u32[]{:S(2)}, u32[]{:S(2)}) %collective-permute-start.41) | collective-permute-done | bytes 524320 | tf_op jit(solution)/shard_map/ppermute | solution.py:46
  376.2 32.8 %shard_map.315 = (bf16[2,4,2,64,1024]{4,3,2,1,0:T(8,128)(2,1)S(1)}, bf16[2,4,2,64,128]{4,3,2,1,0:T(8,128)(2,1)S(1)}, f32[4,768]{1,0:T(4,128)S(1)}, f32[8,128]{1,0:T(8,128)S(1)}) custom-call(s32[1]{0:T(128)} %bitcast.24.me_ref, f32[2,4,2,64,1024]{4,3,2,1,0:T(8,128)} %fusion.6.proj_ref, f32[2,4,2,64,128]{4,3,2,1,0:T(8,128)S(1)} %copy-done.1, ...), custom_call_target="tpu_custom_call" | custom-call | flops 1207959552 | bytes 12582912 | tf_op jit(solution)/shard_map/pallas_call | solution.py:674
  410.4 6.2 %convolution_convert_fusion.4 = bf16[2048,1024]{1,0:T(8,128)(2,1)} fusion(bf16[1024,2048]{1,0:T(8,128)(2,1)S(1)} %bitcast.324, bf16[1024,1024]{1,0:T(8,128)(2,1)S(1)} %bitcast.306), kind=kOutput, calls=%fused_computation.21 | convolution fusion | flops 4297064448 | bytes 10485760 | tf_op jit(solution)/shard_map/dot_general | solution.py:30
  429.0 4.5 fusion.50
  459.8 7.4 %collective-permute-done.56 = bf16[2,64,2048]{2,1,0:T(8,128)(2,1)S(1)} collective-permute-done((bf16[2,64,2048]{2,1,0:T(8,128)(2,1)S(1)}, bf16[2,64,2048]{2,1,0:T(8,128)(2,1)S(1)}, u32[]{:S(2)}, u32[]{:S(2)}) %collective-permute-start.56) | collective-permute-done | bytes 524320 | tf_op jit(solution)/shard_map/ppermute | solution.py:46
  469.7 15.4 %collective-permute-done.57 = bf16[64,2048]{1,0:T(8,128)(2,1)S(1)} collective-permute-done((bf16[64,2048]{1,0:T(8,128)(2,1)S(1)}, bf16[64,2048]{1,0:T(8,128)(2,1)S(1)}, u32[]{:S(2)}, u32[]{:S(2)}) %collective-permute-start.57) | collective-permute-done | bytes 262176 | tf_op jit(solution)/shard_map/ppermute | solution.py:46
  495.2 19.6 %collective-permute-done.54 = bf16[64,2048]{1,0:T(8,128)(2,1)S(1)} collective-permute-done((bf16[64,2048]{1,0:T(8,128)(2,1)S(1)}, bf16[64,2048]{1,0:T(8,128)(2,1)S(1)}, u32[]{:S(2)}, u32[]{:S(2)}) %collective-permute-start.54) | collective-permute-done | bytes 262176 | tf_op jit(solution)/shard_map/ppermute | solution.py:46
  527.1 6.2 %all-to-all-done.4 = f32[32,1,1408]{2,1,0:T(1,128)S(1)} async-done(((f32[32,1,1408]{2,1,0:T(1,128)}), f32[32,1,1408]{2,1,0:T(1,128)S(1)}, u32[]{:S(2)}, u32[]{:S(2)}) %all-to-all-start.4) | async-done | bytes 180256 | tf_op jit(solution)/shard_map/all_to_all | solution.py:786
  540.7 11.6 %all-to-all-done.5.in_ref = bf16[8,64,1024]{2,1,0:T(8,128)(2,1)S(1)} async-done(((bf16[8,64,1024]{2,1,0:T(8,128)(2,1)}), bf16[8,64,1024]{2,1,0:T(8,128)(2,1)S(1)}, u32[]{:S(2)}, u32[]{:S(2)}) %all-to-all-start.5) | async-done | bytes 1048608 | tf_op jit(solution)/shard_map/all_to_all | solution.py:791
  (518 shorter events, 273.5 us)
Async XLA Ops:
  7.2 111.1 %all-gather.7.cloned.1.call-start = ((), (), s32[]{:S(2)}) async-start(), calls=%async_computation.11 | async-start | bytes 1310720 | tf_op jit(solution)/shard_map/all_gather | solution.py:794
  7.9 118.3 %all-gather.5.cloned.1.call-start = ((), (), s32[]{:S(2)}) async-start(), calls=%async_computation.10 | async-start | bytes 5242880 | tf_op jit(solution)/shard_map/all_gather | solution.py:794
  33.7 217.9 %all-gather.11.cloned.1.call-start = ((), (), s32[]{:S(2)}) async-start(), calls=%async_computation.13 | async-start | bytes 7208960 | tf_op jit(solution)/shard_map/all_gather | solution.py:794
  61.2 221.0 %all-gather.9.cloned.1.call-start = ((), (), s32[]{:S(2)}) async-start(), calls=%async_computation.12 | async-start | bytes 1310720 | tf_op jit(solution)/shard_map/all_gather | solution.py:794
  62.5 32.5 %collective-permute-start.4 = (bf16[128,2048]{1,0:T(8,128)(2,1)S(1)}, bf16[128,2048]{1,0:T(8,128)(2,1)S(1)}, u32[]{:S(2)}, u32[]{:S(2)}) collective-permute-start(bf16[128,2048]{1,0:T(8,128)(2,1)S(1)} %bitcast.312), channel_id=1, source_target_pairs={{0,1},{1,0},{2,3},{3,2},{4,5},{5,4},{6,7},{7,6},{8,9},{9,8},{10,11... | collective-permute-start | bytes 1572872 | tf_op jit(solution)/shard_map/ppermute | solution.py:46
  62.5 25.0 %collective-permute-start.9 = (bf16[128,2048]{1,0:T(8,128)(2,1)}, bf16[128,2048]{1,0:T(8,128)(2,1)}, u32[]{:S(2)}, u32[]{:S(2)}) collective-permute-start(bf16[128,2048]{1,0:T(8,128)(2,1)} %bitcast.32), channel_id=1, source_target_pairs={{0,2},{1,3},{2,0},{3,1},{4,6},{5,7},{6,4},{7,5},{8,10},{9,11},{10,... | collective-permute-start | bytes 1572872 | tf_op jit(solution)/shard_map/ppermute | solution.py:46
  63.9 25.3 %collective-permute-start.10 = (bf16[128,2048]{1,0:T(8,128)(2,1)}, bf16[128,2048]{1,0:T(8,128)(2,1)S(1)}, u32[]{:S(2)}, u32[]{:S(2)}) collective-permute-start(bf16[128,2048]{1,0:T(8,128)(2,1)} %bitcast.32), channel_id=1, source_target_pairs={{0,4},{1,5},{2,6},{3,7},{4,0},{5,1},{6,2},{7,3},{8,12},{9,13},{10,... | collective-permute-start | bytes 1572872 | tf_op jit(solution)/shard_map/ppermute | solution.py:46
  87.5 83.6 %collective-permute-start.13 = (bf16[128,2048]{1,0:T(8,128)(2,1)}, bf16[128,2048]{1,0:T(8,128)(2,1)}, u32[]{:S(2)}, u32[]{:S(2)}) collective-permute-start(bf16[128,2048]{1,0:T(8,128)(2,1)} %bitcast.32), channel_id=1, source_target_pairs={{0,1},{1,0},{2,3},{3,2},{4,5},{5,4},{6,7},{7,6},{8,9},{9,8},{10,11... | collective-permute-start | bytes 1572872 | tf_op jit(solution)/shard_map/ppermute | solution.py:46
  89.2 76.2 %collective-permute-start.11 = (bf16[64,2048]{1,0:T(8,128)(2,1)}, bf16[64,2048]{1,0:T(8,128)(2,1)}, u32[]{:S(2)}, u32[]{:S(2)}) collective-permute-start(bf16[64,2048]{1,0:T(8,128)(2,1)} %slice.374), channel_id=1, source_target_pairs={{0,4},{1,5},{2,6},{3,7},{4,0},{5,1},{6,2},{7,3},{8,12},{9,13},{10,... | collective-permute-start | bytes 786440 | tf_op jit(solution)/shard_map/ppermute | solution.py:46
  92.1 75.5 %collective-permute-start.12 = (bf16[64,2048]{1,0:T(8,128)(2,1)}, bf16[64,2048]{1,0:T(8,128)(2,1)}, u32[]{:S(2)}, u32[]{:S(2)}) collective-permute-start(bf16[64,2048]{1,0:T(8,128)(2,1)} %slice.375), channel_id=1, source_target_pairs={{0,2},{1,3},{2,0},{3,1},{4,6},{5,7},{6,4},{7,5},{8,10},{9,11},{10,... | collective-permute-start | bytes 786440 | tf_op jit(solution)/shard_map/ppermute | solution.py:46
  103.6 343.7 %reduce-scatter.9.cloned.1.call-start = ((), (), s32[]{:S(2)}) async-start(), calls=%async_computation.16 | async-start | bytes 3604480 | tf_op jit(solution)/shard_map/reduce_scatter | solution.py:902
  105.9 71.6 %collective-permute-start.14 = (bf16[128,2048]{1,0:T(8,128)(2,1)}, bf16[128,2048]{1,0:T(8,128)(2,1)}, u32[]{:S(2)}, u32[]{:S(2)}) collective-permute-start(bf16[128,2048]{1,0:T(8,128)(2,1)} %collective-permute-done.9), channel_id=1, source_target_pairs={{0,1},{1,0},{2,3},{3,2},{4,5},{5,4},{6,7},{7,6},{8,9},{9,8},{10,11... | collective-permute-start | bytes 1572872 | tf_op jit(solution)/shard_map/ppermute | solution.py:46
  169.2 44.5 %collective-permute-start.16 = (bf16[128,2048]{1,0:T(8,128)(2,1)}, bf16[128,2048]{1,0:T(8,128)(2,1)}, u32[]{:S(2)}, u32[]{:S(2)}) collective-permute-start(bf16[128,2048]{1,0:T(8,128)(2,1)} %constant_dynamic-update-slice_fusion.3), channel_id=1, source_target_pairs={{0,1},{1,0},{2,3},{3,2},{4,5},{5,4},{6,7},{7,6},{8,9},{9,8},{10,11... | collective-permute-start | bytes 1572872 | tf_op jit(solution)/shard_map/ppermute | solution.py:46
  180.3 35.3 %collective-permute-start.17 = (bf16[112,2048]{1,0:T(8,128)(2,1)}, bf16[112,2048]{1,0:T(8,128)(2,1)}, u32[]{:S(2)}, u32[]{:S(2)}) collective-permute-start(bf16[112,2048]{1,0:T(8,128)(2,1)} %slice.299), channel_id=1, source_target_pairs={{0,8},{8,16},{16,24},{1,9},{9,17},{17,25},{2,10},{10,18},{18,26},{... | collective-permute-start | bytes 1376264 | tf_op jit(solution)/shard_map/ppermute | solution.py:710
  182.8 34.7 %collective-permute-start.18 = (bf16[112,2048]{1,0:T(8,128)(2,1)}, bf16[112,2048]{1,0:T(8,128)(2,1)}, u32[]{:S(2)}, u32[]{:S(2)}) collective-permute-start(bf16[112,2048]{1,0:T(8,128)(2,1)} %slice.299), channel_id=1, source_target_pairs={{8,0},{16,8},{24,16},{9,1},{17,9},{25,17},{10,2},{18,10},{26,18},{... | collective-permute-start | bytes 1376264 | tf_op jit(solution)/shard_map/ppermute | solution.py:710
  219.0 29.9 %collective-permute-start.25 = (bf16[112,2048]{1,0:T(8,128)(2,1)}, bf16[112,2048]{1,0:T(8,128)(2,1)}, u32[]{:S(2)}, u32[]{:S(2)}) collective-permute-start(bf16[112,2048]{1,0:T(8,128)(2,1)} %collective-permute-done.18), channel_id=1, source_target_pairs={{8,0},{16,8},{9,1},{17,9},{10,2},{18,10},{11,3},{19,11},{12,4},{20... | collective-permute-start | bytes 1376264 | tf_op jit(solution)/shard_map/ppermute | solution.py:710
  248.9 33.2 %collective-permute-start.34 = (bf16[112,2048]{1,0:T(8,128)(2,1)}, bf16[112,2048]{1,0:T(8,128)(2,1)}, u32[]{:S(2)}, u32[]{:S(2)}) collective-permute-start(bf16[112,2048]{1,0:T(8,128)(2,1)} %collective-permute-done.25), channel_id=1, source_target_pairs={{8,0},{9,1},{10,2},{11,3},{12,4},{13,5},{14,6},{15,7}} | collective-permute-start | bytes 1376264 | tf_op jit(solution)/shard_map/ppermute | solution.py:710
  250.2 36.3 %collective-permute-start.35 = (bf16[112,2048]{1,0:T(8,128)(2,1)}, bf16[112,2048]{1,0:T(8,128)(2,1)}, u32[]{:S(2)}, u32[]{:S(2)}) collective-permute-start(bf16[112,2048]{1,0:T(8,128)(2,1)} %collective-permute-done.24), channel_id=1, source_target_pairs={{16,24},{17,25},{18,26},{19,27},{20,28},{21,29},{22,30},{23,31}} | collective-permute-start | bytes 1376264 | tf_op jit(solution)/shard_map/ppermute | solution.py:710
  272.0 214.8 %reduce-scatter.7.cloned.1.call-start = ((), (), s32[]{:S(2)}) async-start(), calls=%async_computation.15 | async-start | bytes 7208960 | tf_op jit(solution)/shard_map/reduce_scatter | solution.py:902
  318.1 215.3 %reduce-scatter.5.cloned.1.call-start = ((), (), s32[]{:S(2)}) async-start(), calls=%async_computation.14 | async-start | bytes 5242880 | tf_op jit(solution)/shard_map/reduce_scatter | solution.py:902
  416.6 139.3 %reduce-scatter.11.cloned.1.call-start = ((), (), s32[]{:S(2)}) async-start(), calls=%async_computation.17 | async-start | bytes 1310720 | tf_op jit(solution)/shard_map/reduce_scatter | solution.py:902
  456.9 29.2 %collective-permute-start.51 = (bf16[2,64,2048]{2,1,0:T(8,128)(2,1)S(1)}, bf16[2,64,2048]{2,1,0:T(8,128)(2,1)S(1)}, u32[]{:S(2)}, u32[]{:S(2)}) collective-permute-start(bf16[2,64,2048]{2,1,0:T(8,128)(2,1)S(1)} %slice.403), channel_id=1, source_target_pairs={{0,4},{1,5},{2,6},{3,7},{4,0},{5,1},{6,2},{7,3},{8,12},{9,13},{10,... | collective-permute-start | bytes 1572872 | tf_op jit(solution)/shard_map/ppermute | solution.py:46
  458.5 28.1 %collective-permute-start.53 = (bf16[2,64,2048]{2,1,0:T(8,128)(2,1)S(1)}, bf16[2,64,2048]{2,1,0:T(8,128)(2,1)S(1)}, u32[]{:S(2)}, u32[]{:S(2)}) collective-permute-start(bf16[2,64,2048]{2,1,0:T(8,128)(2,1)S(1)} %slice.343), channel_id=1, source_target_pairs={{0,2},{1,3},{2,0},{3,1},{4,6},{5,7},{6,4},{7,5},{8,10},{9,11},{10,... | collective-permute-start | bytes 1572872 | tf_op jit(solution)/shard_map/ppermute | solution.py:46
  486.8 28.1 %all-to-all-start.3 = ((bf16[8,64,1408]{2,1,0:T(8,128)(2,1)}), bf16[8,64,1408]{2,1,0:T(8,128)(2,1)S(1)}, u32[]{:S(2)}, u32[]{:S(2)}) async-start(bf16[8,64,1408]{2,1,0:T(8,128)(2,1)} %bitcast.336), calls=%async_computation.5 | async-start | bytes 2883584 | tf_op jit(solution)/shard_map/all_to_all | solution.py:791
  (123 other events, 1221.4 us)
Sparse Core Ops, SparseCore 0:
  9.6 30.6 all-gather.6
  41.8 84.3 all-gather.4
  127.8 123.7 all-gather.10
  253.0 29.0 all-gather.8
  284.3 56.3 reduce-scatter.8
  342.8 102.0 reduce-scatter.6
  447.2 77.2 reduce-scatter.4
  527.0 27.6 reduce-scatter.10

commit v5 on v4

--- a/solution.py
+++ b/solution.py
@@ -882,7 +882,7 @@
     residual = x_own.astype(f32) + scatter_seq(shares(product(mixed, output_full)))
     normed_mid, pull_mid = jax.vjp(rms_scale, residual, gain_mlp)
     hidden_mid = gather_seq(normed_mid.astype(bf16)).reshape(total, width)
-    down_most = line_gather(w_down[:most], (mixer_full, residual, hidden_mid))
+    down_most = line_gather(w_down[:most], (mixer_full, mixed, hidden_mid))
     gate_up = product(hidden_mid, gate_up_full)
     gate_pre, up_proj = gate_up[:, :ff], gate_up[:, ff:]
     sigmoid_gate = jax.nn.sigmoid(gate_pre)
@@ -971,10 +971,10 @@
     parts.append(jnp.zeros((devices, -edges[-1] % 128), f32))
     swapped = swap_all(jnp.concatenate(parts, axis=1))
     done = lax.optimization_barrier(
-        (swapped, grad_w_gate, grad_w_up, grad_down.astype(f32), output_own, input_grad)
+        (grad_w_gate, grad_w_up, grad_down.astype(f32), output_own, input_grad)
     )
     mixer_own, *done = lax.optimization_barrier((mixer_own, *done))
-    swapped, grad_w_gate, grad_w_up, grad_down, output_own, input_grad = done
+    grad_w_gate, grad_w_up, grad_down, output_own, input_grad = done
     mixer_own = exchange(mixer_own.reshape(n_seq, rows, -1))
     order = []
     for head in range(heads):

time: 575 us -> 576 us (level)
  starting transfers between devices: 64.2 us -> 77 us
  waiting for transfers between devices: 171 us -> 162 us
    ppermute x6, starting transfers between devices: 9.19 us -> 20.6 us  [shift_dp(): lax.ppermute(value, 'dp', [(place, place + step) for place in sources])]
    all_gather x4, waiting for transfers between devices: 11.5 us -> 1.59 us  [gather_dp(): return lax.all_gather(block, 'dp', axis=0, tiled=True)]
    unnamed x184 -> x180, local copies, waits for them, and re-layouts: 44.3 us -> 44.1 us
where the time goes in v5:
time: 576 us; the launch traced here: 569 us
  waiting for transfers between devices  162 us (28%)
  local copies, waits for them, and re-layouts  78.7 us (14%)
  starting transfers between devices  77 us (13%)
  matrix products  76.2 us (13%)
  Pallas kernels  60.4 us (10%)
  other arithmetic  54.2 us (9%)
  blocking collectives  44.4 us (8%)
  between operations  16.2 us (3%)
    ppermute x54, waiting for transfers between devices, swap(): lax.ppermute(value, 'seq', [(place, place ^ bit) for place in range(count)])  117 us
    all_to_all x2, blocking collectives, exchange(): lax.all_to_all(blocks, 'seq', split_axis=0, concat_axis=0, tiled=True)  44.4 us
    unnamed x180, local copies, waits for them, and re-layouts  44.1 us
    ppermute x54, starting transfers between devices, swap(): lax.ppermute(value, 'seq', [(place, place ^ bit) for place in range(count)])  37.3 us
    pallas_call x1, Pallas kernels, mixer_backward(): pl.pallas_call(mixer_backward_body, grid_spec=pltpu.PrefetchScalarGridSpe...  32.8 us
    dot_general x5, matrix products, contract_rows(): lax.dot_general(left_side, right_side, (((0,), (0,)), ((), ())), preferre...  26.1 us
    dot_general x5, matrix products, product(): return jnp.dot(left_side, right_side, preferred_element_type=jnp.float32)  25.1 us
    dot_general x5, matrix products, times_transposed(): lax.dot_general(left_side, right_side, (((1,), (1,)), ((), ())), preferre...  25 us
  transfers between devices with their start and end apart: 72, of which 33 were waited for; matrix products, arithmetic and copies ran while one was open for 33% of the time, Pallas kernels for 11%

profile of v5, /device:TPU:0, one launch (start us, length us, event | category | flops | bytes accessed | tf_op | source)
XLA Modules:
  0.0 568.7 jit_solution(17557050122599921859)
XLA Ops:
  13.3 20.4 %all_to_all.41 = bf16[8,64,1024]{2,1,0:T(8,128)(2,1)} all-to-all(bf16[8,64,1024]{2,1,0:T(8,128)(2,1)S(1)} %pad_maximum_fusion.4), channel_id=1, replica_groups=mesh['dp'=4,'seq'=8] {'seq'}, dimensions={0} | all-to-all | bytes 2097152 | tf_op jit(solution)/shard_map/all_to_all | solution.py:791
  37.2 24.0 %all_to_all.42 = bf16[8,64,1408]{2,1,0:T(8,128)(2,1)} all-to-all(bf16[8,64,1408]{2,1,0:T(8,128)(2,1)} %shard_map.314), channel_id=1, replica_groups=mesh['dp'=4,'seq'=8] {'seq'}, dimensions={0} | all-to-all | bytes 2883584 | tf_op jit(solution)/shard_map/all_to_all | solution.py:791
  80.0 7.5 %collective-permute-done.9 = bf16[128,2048]{1,0:T(8,128)(2,1)} collective-permute-done((bf16[128,2048]{1,0:T(8,128)(2,1)}, bf16[128,2048]{1,0:T(8,128)(2,1)}, u32[]{:S(2)}, u32[]{:S(2)}) %collective-permute-start.9) | collective-permute-done | bytes 524320 | tf_op jit(solution)/shard_map/ppermute | solution.py:46
  108.1 9.1 %all-to-all-done.1 = bf16[32,2,1472]{2,1,0:T(2,128)(2,1)S(1)} async-done(((bf16[32,2,1472]{2,1,0:T(2,128)(2,1)}), bf16[32,2,1472]{2,1,0:T(2,128)(2,1)S(1)}, u32[]{:S(2)}, u32[]{:S(2)}) %all-to-all-start.1) | async-done | bytes 188448 | tf_op jit(solution)/shard_map/all_to_all | solution.py:786
  132.0 6.4 %fusion.6.proj_ref = f32[2,4,2,64,1024]{4,3,2,1,0:T(8,128)} fusion(bf16[2048,1024]{1,0:T(8,128)(2,1)S(1)} %copy-done.69, f32[2048]{0:T(1024)S(1)} %reshape.809, f32[2,4,2,64]{3,2,1,0:T(2,128)S(1)} %rsqrt.40, bf16[2,4,2,64,2048]{4,3,2,1,0:T(8,128)(2,1)S(1)} %bitcast.319), kind=kOutput, calls=%fused_computation.16 | convolution fusion | flops 4303355904 | bytes 12595200 | tf_op jit(solution)/shard_map/dot_general | solution.py:26
  139.7 18.7 %shard_map.313 = (bf16[2,4,2,64,256]{4,3,2,1,0:T(8,128)(2,1)S(1)}, f32[4,2,2,64,768]{4,3,2,1,0:T(8,128)S(1)}, bf16[4,2,2,128,128]{4,3,2,1,0:T(8,128)(2,1)S(1)}, ...) custom-call(s32[1]{0:T(128)} %bitcast.24.me_ref, ...), custom_call_target="tpu_custom_call" | custom-call | flops 1207959552 | bytes 12582912 | tf_op jit(solution)/shard_map/pallas_call | solution.py:645
  193.4 6.8 %collective-permute-done.24 = bf16[2,64,2048]{2,1,0:T(8,128)(2,1)S(1)} collective-permute-done((bf16[2,64,2048]{2,1,0:T(8,128)(2,1)S(1)}, bf16[2,64,2048]{2,1,0:T(8,128)(2,1)S(1)}, u32[]{:S(2)}, u32[]{:S(2)}) %collective-permute-start.24) | collective-permute-done | bytes 524320 | tf_op jit(solution)/shard_map/ppermute | solution.py:46
  224.5 6.0 %collective-permute-done.28 = bf16[64,2048]{1,0:T(8,128)(2,1)S(1)} collective-permute-done((bf16[64,2048]{1,0:T(8,128)(2,1)S(1)}, bf16[64,2048]{1,0:T(8,128)(2,1)S(1)}, u32[]{:S(2)}, u32[]{:S(2)}) %collective-permute-start.28) | collective-permute-done | bytes 262176 | tf_op jit(solution)/shard_map/ppermute | solution.py:46
  236.0 12.1 %collective-permute-done.20 = bf16[112,2048]{1,0:T(8,128)(2,1)} collective-permute-done((bf16[112,2048]{1,0:T(8,128)(2,1)}, bf16[112,2048]{1,0:T(8,128)(2,1)}, u32[]{:S(2)}, u32[]{:S(2)}) %collective-permute-start.20) | collective-permute-done | bytes 458784 | tf_op jit(solution)/shard_map/ppermute | solution.py:710
  248.1 12.7 %collective-permute-start.34 = (bf16[112,2048]{1,0:T(8,128)(2,1)}, bf16[112,2048]{1,0:T(8,128)(2,1)}, u32[]{:S(2)}, u32[]{:S(2)}) collective-permute-start(bf16[112,2048]{1,0:T(8,128)(2,1)} %collective-permute-done.20), channel_id=1, source_target_pairs={{8,0},{9,1},{10,2},{11,3},{12,4},{13,5},{14,6},{15,7}} | collective-permute-start | bytes 1376264 | tf_op jit(solution)/shard_map/ppermute | solution.py:710
  262.3 10.4 %fusion.50 = f32[1024,1408]{1,0:T(8,128)S(1)} fusion(bf16[1024,2048]{1,0:T(8,128)(2,1)} %bitcast.361, bf16[2048,1408]{1,0:T(8,128)(2,1)} %all-gather.11.cloned.1.call-done), kind=kOutput, calls=%fused_computation.202 | convolution fusion | flops 5905580032 | bytes 15728640 | tf_op jit(solution)/shard_map/dot_general | solution.py:26
  291.1 7.7 %multiply_convert_fusion.3 = (bf16[1024,704]{1,0:T(8,128)(2,1)S(1)}, bf16[1024,704]{1,0:T(8,128)(2,1)S(1)}) fusion(f32[1024,1408]{1,0:T(8,128)S(1)} %copy-done.39, bf16[1024,2048]{1,0:T(8,128)(2,1)} %bitcast.363, bf16[704,2048]{1,0:T(8,128)(2,1)S(1)} %bitcast.335), kind=kOutput, calls=%fused_computation.24 | convolution fusion | flops 2962161664 | bytes 15728640 | tf_op jit(solution)/shard_map/dot_general | solution.py:36
  298.8 6.9 %convolution_convert_fusion.2 = bf16[1024,2048]{1,0:T(8,128)(2,1)S(1)} fusion(bf16[2048,1408]{1,0:T(8,128)(2,1)S(1)} %bitcast.376, bf16[1024,704]{1,0:T(8,128)(2,1)S(1)} %get-tuple-element.160, bf16[1024,704]{1,0:T(8,128)(2,1)S(1)} %get-tuple-element.159), kind=kOutput, calls=%fused_computation.19 | convolution fusion | flops 5913444352 | bytes 12845056 | tf_op jit(solution)/shard_map/dot_general | solution.py:36
  309.5 8.8 %convolution_convert_fusion = bf16[2048,1408]{1,0:T(8,128)(2,1)} fusion(bf16[1024,2048]{1,0:T(8,128)(2,1)S(1)} %bitcast.362, bf16[1024,704]{1,0:T(8,128)(2,1)S(1)} %get-tuple-element.160, bf16[1024,704]{1,0:T(8,128)(2,1)S(1)} %get-tuple-element.159), kind=kOutput, calls=%fused_computation.6 | convolution fusion | flops 5914230784 | bytes 12845056 | tf_op jit(solution)/shard_map/dot_general | solution.py:30
  324.7 10.9 %collective-permute-done.37 = bf16[2,64,2048]{2,1,0:T(8,128)(2,1)S(1)} collective-permute-done((bf16[2,64,2048]{2,1,0:T(8,128)(2,1)S(1)}, bf16[2,64,2048]{2,1,0:T(8,128)(2,1)S(1)}, u32[]{:S(2)}, u32[]{:S(2)}) %collective-permute-start.37) | collective-permute-done | bytes 524320 | tf_op jit(solution)/shard_map/ppermute | solution.py:46
  354.6 7.3 %collective-permute-done.41 = bf16[128,2048]{1,0:T(8,128)(2,1)S(1)} collective-permute-done((bf16[128,2048]{1,0:T(8,128)(2,1)S(1)}, bf16[128,2048]{1,0:T(8,128)(2,1)S(1)}, u32[]{:S(2)}, u32[]{:S(2)}) %collective-permute-start.41) | collective-permute-done | bytes 524320 | tf_op jit(solution)/shard_map/ppermute | solution.py:46
  377.0 32.8 %shard_map.315 = (bf16[2,4,2,64,1024]{4,3,2,1,0:T(8,128)(2,1)S(1)}, bf16[2,4,2,64,128]{4,3,2,1,0:T(8,128)(2,1)S(1)}, f32[4,768]{1,0:T(4,128)S(1)}, f32[8,128]{1,0:T(8,128)S(1)}) custom-call(s32[1]{0:T(128)} %bitcast.24.me_ref, f32[2,4,2,64,1024]{4,3,2,1,0:T(8,128)} %fusion.6.proj_ref, f32[2,4,2,64,128]{4,3,2,1,0:T(8,128)S(1)} %copy-done.1, ...), custom_call_target="tpu_custom_call" | custom-call | flops 1207959552 | bytes 12582912 | tf_op jit(solution)/shard_map/pallas_call | solution.py:674
  411.1 6.2 %convolution_convert_fusion.4 = bf16[2048,1024]{1,0:T(8,128)(2,1)} fusion(bf16[1024,2048]{1,0:T(8,128)(2,1)S(1)} %bitcast.328, bf16[1024,1024]{1,0:T(8,128)(2,1)S(1)} %bitcast.310), kind=kOutput, calls=%fused_computation.21 | convolution fusion | flops 4297064448 | bytes 10485760 | tf_op jit(solution)/shard_map/dot_general | solution.py:30
  460.0 7.8 %collective-permute-done.56 = bf16[2,64,2048]{2,1,0:T(8,128)(2,1)S(1)} collective-permute-done((bf16[2,64,2048]{2,1,0:T(8,128)(2,1)S(1)}, bf16[2,64,2048]{2,1,0:T(8,128)(2,1)S(1)}, u32[]{:S(2)}, u32[]{:S(2)}) %collective-permute-start.56) | collective-permute-done | bytes 524320 | tf_op jit(solution)/shard_map/ppermute | solution.py:46
  470.2 14.9 %collective-permute-done.57 = bf16[64,2048]{1,0:T(8,128)(2,1)S(1)} collective-permute-done((bf16[64,2048]{1,0:T(8,128)(2,1)S(1)}, bf16[64,2048]{1,0:T(8,128)(2,1)S(1)}, u32[]{:S(2)}, u32[]{:S(2)}) %collective-permute-start.57) | collective-permute-done | bytes 262176 | tf_op jit(solution)/shard_map/ppermute | solution.py:46
  495.4 19.7 %collective-permute-done.54 = bf16[64,2048]{1,0:T(8,128)(2,1)S(1)} collective-permute-done((bf16[64,2048]{1,0:T(8,128)(2,1)S(1)}, bf16[64,2048]{1,0:T(8,128)(2,1)S(1)}, u32[]{:S(2)}, u32[]{:S(2)}) %collective-permute-start.54) | collective-permute-done | bytes 262176 | tf_op jit(solution)/shard_map/ppermute | solution.py:46
  521.2 7.4 %all-to-all-start.4 = ((f32[32,1,1408]{2,1,0:T(1,128)}), f32[32,1,1408]{2,1,0:T(1,128)S(1)}, u32[]{:S(2)}, u32[]{:S(2)}) async-start(f32[32,1,1408]{2,1,0:T(1,128)} %copy.84), calls=%async_computation.7 | async-start | bytes 360448 | tf_op jit(solution)/shard_map/all_to_all | solution.py:786
  531.1 6.2 %all-to-all-done.4 = f32[32,1,1408]{2,1,0:T(1,128)S(1)} async-done(((f32[32,1,1408]{2,1,0:T(1,128)}), f32[32,1,1408]{2,1,0:T(1,128)S(1)}, u32[]{:S(2)}, u32[]{:S(2)}) %all-to-all-start.4) | async-done | bytes 180256 | tf_op jit(solution)/shard_map/all_to_all | solution.py:786
  544.7 11.5 %all-to-all-done.5.in_ref = bf16[8,64,1024]{2,1,0:T(8,128)(2,1)S(1)} async-done(((bf16[8,64,1024]{2,1,0:T(8,128)(2,1)}), bf16[8,64,1024]{2,1,0:T(8,128)(2,1)S(1)}, u32[]{:S(2)}, u32[]{:S(2)}) %all-to-all-start.5) | async-done | bytes 1048608 | tf_op jit(solution)/shard_map/all_to_all | solution.py:791
  (514 shorter events, 270.1 us)
Async XLA Ops:
  7.2 111.1 %all-gather.7.cloned.1.call-start = ((), (), s32[]{:S(2)}) async-start(), calls=%async_computation.11 | async-start | bytes 1310720 | tf_op jit(solution)/shard_map/all_gather | solution.py:794
  7.9 118.3 %all-gather.5.cloned.1.call-start = ((), (), s32[]{:S(2)}) async-start(), calls=%async_computation.10 | async-start | bytes 5242880 | tf_op jit(solution)/shard_map/all_gather | solution.py:794
  33.7 228.5 %all-gather.11.cloned.1.call-start = ((), (), s32[]{:S(2)}) async-start(), calls=%async_computation.13 | async-start | bytes 7208960 | tf_op jit(solution)/shard_map/all_gather | solution.py:794
  61.2 221.5 %all-gather.9.cloned.1.call-start = ((), (), s32[]{:S(2)}) async-start(), calls=%async_computation.12 | async-start | bytes 1310720 | tf_op jit(solution)/shard_map/all_gather | solution.py:794
  62.4 32.5 %collective-permute-start.4 = (bf16[128,2048]{1,0:T(8,128)(2,1)S(1)}, bf16[128,2048]{1,0:T(8,128)(2,1)S(1)}, u32[]{:S(2)}, u32[]{:S(2)}) collective-permute-start(bf16[128,2048]{1,0:T(8,128)(2,1)S(1)} %bitcast.315), channel_id=1, source_target_pairs={{0,1},{1,0},{2,3},{3,2},{4,5},{5,4},{6,7},{7,6},{8,9},{9,8},{10,11... | collective-permute-start | bytes 1572872 | tf_op jit(solution)/shard_map/ppermute | solution.py:46
  62.5 25.0 %collective-permute-start.9 = (bf16[128,2048]{1,0:T(8,128)(2,1)}, bf16[128,2048]{1,0:T(8,128)(2,1)}, u32[]{:S(2)}, u32[]{:S(2)}) collective-permute-start(bf16[128,2048]{1,0:T(8,128)(2,1)} %bitcast.32), channel_id=1, source_target_pairs={{0,2},{1,3},{2,0},{3,1},{4,6},{5,7},{6,4},{7,5},{8,10},{9,11},{10,... | collective-permute-start | bytes 1572872 | tf_op jit(solution)/shard_map/ppermute | solution.py:46
  63.9 25.3 %collective-permute-start.10 = (bf16[128,2048]{1,0:T(8,128)(2,1)}, bf16[128,2048]{1,0:T(8,128)(2,1)S(1)}, u32[]{:S(2)}, u32[]{:S(2)}) collective-permute-start(bf16[128,2048]{1,0:T(8,128)(2,1)} %bitcast.32), channel_id=1, source_target_pairs={{0,4},{1,5},{2,6},{3,7},{4,0},{5,1},{6,2},{7,3},{8,12},{9,13},{10,... | collective-permute-start | bytes 1572872 | tf_op jit(solution)/shard_map/ppermute | solution.py:46
  87.5 83.5 %collective-permute-start.13 = (bf16[128,2048]{1,0:T(8,128)(2,1)}, bf16[128,2048]{1,0:T(8,128)(2,1)}, u32[]{:S(2)}, u32[]{:S(2)}) collective-permute-start(bf16[128,2048]{1,0:T(8,128)(2,1)} %bitcast.32), channel_id=1, source_target_pairs={{0,1},{1,0},{2,3},{3,2},{4,5},{5,4},{6,7},{7,6},{8,9},{9,8},{10,11... | collective-permute-start | bytes 1572872 | tf_op jit(solution)/shard_map/ppermute | solution.py:46
  89.2 76.1 %collective-permute-start.11 = (bf16[64,2048]{1,0:T(8,128)(2,1)}, bf16[64,2048]{1,0:T(8,128)(2,1)}, u32[]{:S(2)}, u32[]{:S(2)}) collective-permute-start(bf16[64,2048]{1,0:T(8,128)(2,1)} %slice.374), channel_id=1, source_target_pairs={{0,4},{1,5},{2,6},{3,7},{4,0},{5,1},{6,2},{7,3},{8,12},{9,13},{10,... | collective-permute-start | bytes 786440 | tf_op jit(solution)/shard_map/ppermute | solution.py:46
  92.0 75.4 %collective-permute-start.12 = (bf16[64,2048]{1,0:T(8,128)(2,1)}, bf16[64,2048]{1,0:T(8,128)(2,1)}, u32[]{:S(2)}, u32[]{:S(2)}) collective-permute-start(bf16[64,2048]{1,0:T(8,128)(2,1)} %slice.375), channel_id=1, source_target_pairs={{0,2},{1,3},{2,0},{3,1},{4,6},{5,7},{6,4},{7,5},{8,10},{9,11},{10,... | collective-permute-start | bytes 786440 | tf_op jit(solution)/shard_map/ppermute | solution.py:46
  103.6 344.3 %reduce-scatter.9.cloned.1.call-start = ((), (), s32[]{:S(2)}) async-start(), calls=%async_computation.16 | async-start | bytes 3604480 | tf_op jit(solution)/shard_map/reduce_scatter | solution.py:902
  105.9 71.4 %collective-permute-start.14 = (bf16[128,2048]{1,0:T(8,128)(2,1)}, bf16[128,2048]{1,0:T(8,128)(2,1)}, u32[]{:S(2)}, u32[]{:S(2)}) collective-permute-start(bf16[128,2048]{1,0:T(8,128)(2,1)} %collective-permute-done.9), channel_id=1, source_target_pairs={{0,1},{1,0},{2,3},{3,2},{4,5},{5,4},{6,7},{7,6},{8,9},{9,8},{10,11... | collective-permute-start | bytes 1572872 | tf_op jit(solution)/shard_map/ppermute | solution.py:46
  169.1 43.5 %collective-permute-start.16 = (bf16[128,2048]{1,0:T(8,128)(2,1)}, bf16[128,2048]{1,0:T(8,128)(2,1)}, u32[]{:S(2)}, u32[]{:S(2)}) collective-permute-start(bf16[128,2048]{1,0:T(8,128)(2,1)} %constant_dynamic-update-slice_fusion.3), channel_id=1, source_target_pairs={{0,1},{1,0},{2,3},{3,2},{4,5},{5,4},{6,7},{7,6},{8,9},{9,8},{10,11... | collective-permute-start | bytes 1572872 | tf_op jit(solution)/shard_map/ppermute | solution.py:46
  180.2 34.3 %collective-permute-start.17 = (bf16[112,2048]{1,0:T(8,128)(2,1)}, bf16[112,2048]{1,0:T(8,128)(2,1)}, u32[]{:S(2)}, u32[]{:S(2)}) collective-permute-start(bf16[112,2048]{1,0:T(8,128)(2,1)} %slice.299), channel_id=1, source_target_pairs={{0,8},{8,16},{16,24},{1,9},{9,17},{17,25},{2,10},{10,18},{18,26},{... | collective-permute-start | bytes 1376264 | tf_op jit(solution)/shard_map/ppermute | solution.py:710
  182.7 34.6 %collective-permute-start.18 = (bf16[112,2048]{1,0:T(8,128)(2,1)}, bf16[112,2048]{1,0:T(8,128)(2,1)}, u32[]{:S(2)}, u32[]{:S(2)}) collective-permute-start(bf16[112,2048]{1,0:T(8,128)(2,1)} %slice.299), channel_id=1, source_target_pairs={{8,0},{16,8},{24,16},{9,1},{17,9},{25,17},{10,2},{18,10},{26,18},{... | collective-permute-start | bytes 1376264 | tf_op jit(solution)/shard_map/ppermute | solution.py:710
  218.7 29.3 %collective-permute-start.20 = (bf16[112,2048]{1,0:T(8,128)(2,1)}, bf16[112,2048]{1,0:T(8,128)(2,1)}, u32[]{:S(2)}, u32[]{:S(2)}) collective-permute-start(bf16[112,2048]{1,0:T(8,128)(2,1)} %collective-permute-done.18), channel_id=1, source_target_pairs={{8,0},{16,8},{9,1},{17,9},{10,2},{18,10},{11,3},{19,11},{12,4},{20... | collective-permute-start | bytes 1376264 | tf_op jit(solution)/shard_map/ppermute | solution.py:710
  248.1 34.6 %collective-permute-start.34 = (bf16[112,2048]{1,0:T(8,128)(2,1)}, bf16[112,2048]{1,0:T(8,128)(2,1)}, u32[]{:S(2)}, u32[]{:S(2)}) collective-permute-start(bf16[112,2048]{1,0:T(8,128)(2,1)} %collective-permute-done.20), channel_id=1, source_target_pairs={{8,0},{9,1},{10,2},{11,3},{12,4},{13,5},{14,6},{15,7}} | collective-permute-start | bytes 1376264 | tf_op jit(solution)/shard_map/ppermute | solution.py:710
  260.8 26.3 %collective-permute-start.35 = (bf16[112,2048]{1,0:T(8,128)(2,1)}, bf16[112,2048]{1,0:T(8,128)(2,1)}, u32[]{:S(2)}, u32[]{:S(2)}) collective-permute-start(bf16[112,2048]{1,0:T(8,128)(2,1)} %collective-permute-done.19), channel_id=1, source_target_pairs={{16,24},{17,25},{18,26},{19,27},{20,28},{21,29},{22,30},{23,31}} | collective-permute-start | bytes 1376264 | tf_op jit(solution)/shard_map/ppermute | solution.py:710
  282.6 204.7 %reduce-scatter.7.cloned.1.call-start = ((), (), s32[]{:S(2)}) async-start(), calls=%async_computation.15 | async-start | bytes 7208960 | tf_op jit(solution)/shard_map/reduce_scatter | solution.py:902
  318.4 212.8 %reduce-scatter.5.cloned.1.call-start = ((), (), s32[]{:S(2)}) async-start(), calls=%async_computation.14 | async-start | bytes 5242880 | tf_op jit(solution)/shard_map/reduce_scatter | solution.py:902
  417.3 142.5 %reduce-scatter.11.cloned.1.call-start = ((), (), s32[]{:S(2)}) async-start(), calls=%async_computation.17 | async-start | bytes 1310720 | tf_op jit(solution)/shard_map/reduce_scatter | solution.py:902
  457.4 29.0 %collective-permute-start.51 = (bf16[2,64,2048]{2,1,0:T(8,128)(2,1)S(1)}, bf16[2,64,2048]{2,1,0:T(8,128)(2,1)S(1)}, u32[]{:S(2)}, u32[]{:S(2)}) collective-permute-start(bf16[2,64,2048]{2,1,0:T(8,128)(2,1)S(1)} %slice.403), channel_id=1, source_target_pairs={{0,4},{1,5},{2,6},{3,7},{4,0},{5,1},{6,2},{7,3},{8,12},{9,13},{10,... | collective-permute-start | bytes 1572872 | tf_op jit(solution)/shard_map/ppermute | solution.py:46
  458.3 28.8 %collective-permute-start.53 = (bf16[2,64,2048]{2,1,0:T(8,128)(2,1)S(1)}, bf16[2,64,2048]{2,1,0:T(8,128)(2,1)S(1)}, u32[]{:S(2)}, u32[]{:S(2)}) collective-permute-start(bf16[2,64,2048]{2,1,0:T(8,128)(2,1)S(1)} %slice.342), channel_id=1, source_target_pairs={{0,2},{1,3},{2,0},{3,1},{4,6},{5,7},{6,4},{7,5},{8,10},{9,11},{10,... | collective-permute-start | bytes 1572872 | tf_op jit(solution)/shard_map/ppermute | solution.py:46
  487.3 28.0 %all-to-all-start.3 = ((bf16[8,64,1408]{2,1,0:T(8,128)(2,1)}), bf16[8,64,1408]{2,1,0:T(8,128)(2,1)S(1)}, u32[]{:S(2)}, u32[]{:S(2)}) async-start(bf16[8,64,1408]{2,1,0:T(8,128)(2,1)} %bitcast.340), calls=%async_computation.5 | async-start | bytes 2883584 | tf_op jit(solution)/shard_map/all_to_all | solution.py:791
  (121 other events, 1201.4 us)
Sparse Core Ops, SparseCore 0:
  9.6 30.6 all-gather.6
  41.8 84.3 all-gather.4
  127.8 124.4 all-gather.10
  253.7 27.8 all-gather.8
  283.8 61.0 reduce-scatter.8
  347.0 102.0 reduce-scatter.6
  451.4 77.2 reduce-scatter.4
  531.1 27.6 reduce-scatter.10
